TPU v7x, 32 devices: a whole 2x2x4 slice. The times are simulated.
32 devices in a mesh: sens: 2 (over x), src: 16 (over z, y, core).
Axes of the slice: x: 2, y: 2, z: 4, core: 2. Of those that a mesh axis runs over, the one named last changes fastest.
Arguments:
- slip_param: float32 [1024, 384], P(('src', 'sens')), may hold values from -4 to 4
- rigidity: float32 [1024], P(('src', 'sens')), may hold values from 1 to 36
- kernel: bfloat16 [2, 512, 1024, 384], P(None, 'sens', 'src'), may hold values from -0.08984375 to 0.08984375
- observed: float32 [512, 384], P('sens'), may hold values from -6 to 6
Outputs:
- final_param: float32 [1024, 384], P(('src', 'sens'))
- misfit: float32 [512, 384], P(('sens', 'src'))
All inputs are finite; a program needn't handle non-finite values.
Results may differ from a plain program's by a relative error of at most 0.0003.
Values sent between devices are 32-bit elements; how exact they have to be, the bound alone decides.
No kernel may reach another device: no remote copies, remote signals or barrier semaphores. Data moves between devices by JAX's collectives and lax.ppermute only.
A program may use at most 64 MiB of HBM per device.

v0:
```python
import math

import jax
import jax.numpy as jnp
from jax import lax
from jax.sharding import PartitionSpec as P

SOURCES = 1024
ITERS = 3


highest = lax.Precision.HIGHEST
step_rate = 0.3
epsilon = 1e-06


def forward_table(length):
    padded = 2 * length
    sample_index = jnp.arange(length, dtype=jnp.int32)[:, None]
    freq_index = jnp.arange(length, dtype=jnp.int32)[None, :]
    phases = (sample_index * freq_index % padded).astype(jnp.float32) * (2.0 * math.pi / padded)
    return jnp.concatenate([jnp.cos(phases), -jnp.sin(phases)], axis=1)


def spectral_weights(length):
    padded = 2 * length
    column = jnp.arange(2 * length, dtype=jnp.int32) % length
    return jnp.where(column == 0, 1.0 / padded, 2.0 / padded).astype(jnp.float32)


def forward_terms(kernel, spectra):
    freqs = kernel.shape[-1]
    real_part = spectra[:, :freqs][None]
    imag_part = spectra[:, freqs:][None]
    kernel_real = kernel[0].astype(jnp.float32)
    kernel_imag = kernel[1].astype(jnp.float32)
    out_real = jnp.sum(kernel_real * real_part - kernel_imag * imag_part, axis=1)
    out_imag = jnp.sum(kernel_real * imag_part + kernel_imag * real_part, axis=1)
    return jnp.concatenate([out_real, out_imag], axis=1)


def adjoint_terms(kernel, spectra):
    freqs = kernel.shape[-1]
    real_part = spectra[:, :freqs][:, None]
    imag_part = spectra[:, freqs:][:, None]
    kernel_real = kernel[0].astype(jnp.float32)
    kernel_imag = kernel[1].astype(jnp.float32)
    back_real = jnp.sum(kernel_real * real_part + kernel_imag * imag_part, axis=0)
    back_imag = jnp.sum(kernel_real * imag_part - kernel_imag * real_part, axis=0)
    return jnp.concatenate([back_real, back_imag], axis=1)


def local(slip_param, rigidity, kernel, observed):
    length = slip_param.shape[1]
    table = forward_table(length)
    weighted = table * spectral_weights(length)[None, :]
    block_rows = kernel.shape[1]
    own_count = block_rows // lax.axis_size("src")
    offset = lax.axis_index("src") * own_count
    own_observed = lax.dynamic_slice_in_dim(observed, offset, own_count, 0)
    entry_count = SOURCES * length
    scale_rows = rigidity[:, None]
    misfit = own_observed
    for iteration in range(ITERS):
        slip = scale_rows * jax.nn.softplus(slip_param)
        slips = lax.all_gather(slip, "sens", axis=0, tiled=True)
        spectra = jnp.dot(slips, table, precision=highest)
        terms = forward_terms(kernel, spectra)
        terms = jnp.dot(terms, weighted.T, precision=highest)
        summed = lax.psum_scatter(terms, "src", scatter_dimension=0, tiled=True)
        misfit = summed - own_observed
        residual = lax.all_gather(misfit, "src", axis=0, tiled=True)
        adjoint_spec = jnp.dot(residual, weighted, precision=highest)
        back_terms = adjoint_terms(kernel, adjoint_spec)
        back_terms = jnp.dot(back_terms, table.T, precision=highest)
        own_back = lax.psum_scatter(back_terms, "sens", scatter_dimension=0, tiled=True)
        gradient = own_back * scale_rows * jax.nn.sigmoid(slip_param)
        square_sum = lax.psum(jnp.sum(gradient * gradient), ("sens", "src"))
        root_mean = jnp.sqrt(square_sum / entry_count + epsilon)
        slip_param = slip_param - step_rate * gradient / root_mean
    return (slip_param, misfit)


def solution(mesh):
    in_specs = (
        P(("src", "sens"), None),
        P(("src", "sens")),
        P(None, "sens", "src", None),
        P("sens", None),
    )
    out_specs = (P(("src", "sens"), None), P(("sens", "src"), None))
    return jax.shard_map(local, mesh=mesh, in_specs=in_specs, out_specs=out_specs, check_vma=False)
```

profile of v0, /device:TPU:0, one launch (start us, length us, event | category | flops | bytes accessed | tf_op | source)
XLA Modules:
  0.0 532.8 jit_solution(11554790442669328523)
XLA Ops:
  7.2 2.4 sine_negate_fusion
  10.5 5.7 %all_gather.18 = f32[64,384]{1,0:T(8,128)S(1)} all-gather(f32[32,384]{1,0:T(8,128)S(1)} %fusion.69), channel_id=1, replica_groups=mesh['sens'=2,'src'=16] {'sens'}, dimensions={0}, use_global_device_ids=true | all-gather | bytes 147456 | tf_op jit(solution)/shard_map/all_gather | solution.py:66
  17.0 18.3 %fusion.1 = (f32[256,384]{1,0:T(8,128)S(1)}, f32[256,384]{1,0:T(8,128)S(1)}) fusion(f32[64,384]{1,0:T(8,128)S(1)} %get-tuple-element.29, f32[64,384]{1,0:T(8,128)S(1)} %get-tuple-element.28, bf16[2,256,64,384]{3,2,1,0:T(8,128)(2,1)} %param.6), kind=kLoop, calls=%fused_computation.25 | loop fusion | flops 62717952 | bytes 26148864 | tf_op jit(solution)/shard_map/reduce_sum | solution.py:37
  35.3 2.2 fusion.34
  37.6 57.8 %reduce-scatter.7.cloned.1.call-done = f32[16,384]{1,0:T(8,128)} async-done(((f32[256,384]{1,0:T(8,128)}), f32[16,384]{1,0:T(8,128)}) %reduce-scatter.7.cloned.1.call-update) | async-done | bytes 24592 | tf_op jit(solution)/shard_map/reduce_scatter | solution.py:70
  96.2 20.7 %all_gather.19 = f32[256,384]{1,0:T(8,128)S(1)} all-gather(f32[16,384]{1,0:T(8,128)S(1)} %dynamic-slice_subtract_fusion.2), channel_id=1, replica_groups=mesh['sens'=2,'src'=16] {'src'}, dimensions={0}, use_global_device_ids=true | all-gather | bytes 417792 | tf_op jit(solution)/shard_map/all_gather | solution.py:72
  118.4 12.8 %fusion.5 = (f32[64,384]{1,0:T(8,128)S(1)}, f32[64,384]{1,0:T(8,128)S(1)}) fusion(f32[256,384]{1,0:T(8,128)S(1)} %get-tuple-element.23, f32[256,384]{1,0:T(8,128)S(1)} %get-tuple-element.22, bf16[2,256,64,384]{3,2,1,0:T(8,128)(2,1)} %param.6), kind=kLoop, calls=%fused_computation.29 | loop fusion | flops 62865408 | bytes 26148864 | tf_op jit(solution)/shard_map/reduce_sum | solution.py:48
  131.2 1.9 fusion.57
  133.2 7.5 %reduce-scatter.9.cloned.1.call-done = f32[32,384]{1,0:T(8,128)} async-done(((f32[64,384]{1,0:T(8,128)}), f32[32,384]{1,0:T(8,128)}) %reduce-scatter.9.cloned.1.call-update) | async-done | bytes 49168 | tf_op jit(solution)/shard_map/reduce_scatter | solution.py:76
  140.7 1.5 multiply_reduce_fusion.2
  142.1 39.5 %psum.21 = f32[]{:T(128)} all-reduce(f32[]{:T(128)} %multiply_reduce_fusion.2), channel_id=1, replica_groups=mesh['sens'=2,'src'=16] {'sens','src'}, use_global_device_ids=true, to_apply=%region_7.8 | all-reduce | flops 1 | bytes 8 | tf_op jit(solution)/shard_map/psum | solution.py:78
  183.2 5.0 all_gather.20
  189.1 18.3 %fusion.9 = (f32[256,384]{1,0:T(8,128)S(1)}, f32[256,384]{1,0:T(8,128)S(1)}) fusion(f32[64,384]{1,0:T(8,128)S(1)} %get-tuple-element.27, f32[64,384]{1,0:T(8,128)S(1)} %get-tuple-element.26, bf16[2,256,64,384]{3,2,1,0:T(8,128)(2,1)} %param.6), kind=kLoop, calls=%fused_computation.33 | loop fusion | flops 62717952 | bytes 26148864 | tf_op jit(solution)/shard_map/reduce_sum | solution.py:37
  207.4 2.2 fusion.30
  209.7 56.8 %reduce-scatter.11.cloned.1.call-done = f32[16,384]{1,0:T(8,128)} async-done(((f32[256,384]{1,0:T(8,128)}), f32[16,384]{1,0:T(8,128)}) %reduce-scatter.11.cloned.1.call-update) | async-done | bytes 24592 | tf_op jit(solution)/shard_map/reduce_scatter | solution.py:70
  267.3 20.7 %all_gather.21 = f32[256,384]{1,0:T(8,128)S(1)} all-gather(f32[16,384]{1,0:T(8,128)S(1)} %dynamic-slice_subtract_fusion.1), channel_id=1, replica_groups=mesh['sens'=2,'src'=16] {'src'}, dimensions={0}, use_global_device_ids=true | all-gather | bytes 417792 | tf_op jit(solution)/shard_map/all_gather | solution.py:72
  289.5 12.8 %fusion.13 = (f32[64,384]{1,0:T(8,128)S(1)}, f32[64,384]{1,0:T(8,128)S(1)}) fusion(f32[256,384]{1,0:T(8,128)S(1)} %get-tuple-element.21, f32[256,384]{1,0:T(8,128)S(1)} %get-tuple-element.20, bf16[2,256,64,384]{3,2,1,0:T(8,128)(2,1)} %param.6), kind=kLoop, calls=%fused_computation.37 | loop fusion | flops 62865408 | bytes 26148864 | tf_op jit(solution)/shard_map/reduce_sum | solution.py:48
  302.3 1.9 fusion.61
  304.2 7.4 %reduce-scatter.13.cloned.1.call-done = f32[32,384]{1,0:T(8,128)} async-done(((f32[64,384]{1,0:T(8,128)}), f32[32,384]{1,0:T(8,128)}) %reduce-scatter.13.cloned.1.call-update) | async-done | bytes 49168 | tf_op jit(solution)/shard_map/reduce_scatter | solution.py:76
  311.6 1.5 multiply_reduce_fusion.1
  313.1 39.5 %psum.22 = f32[]{:T(128)} all-reduce(f32[]{:T(128)} %multiply_reduce_fusion.1), channel_id=1, replica_groups=mesh['sens'=2,'src'=16] {'sens','src'}, use_global_device_ids=true, to_apply=%region_15.16 | all-reduce | flops 1 | bytes 8 | tf_op jit(solution)/shard_map/psum | solution.py:78
  354.2 5.0 all_gather.22
  360.0 18.3 %fusion.17 = (f32[256,384]{1,0:T(8,128)S(1)}, f32[256,384]{1,0:T(8,128)S(1)}) fusion(f32[64,384]{1,0:T(8,128)S(1)} %get-tuple-element.25, f32[64,384]{1,0:T(8,128)S(1)} %get-tuple-element.24, bf16[2,256,64,384]{3,2,1,0:T(8,128)(2,1)} %param.6), kind=kLoop, calls=%fused_computation.41 | loop fusion | flops 62717952 | bytes 26148864 | tf_op jit(solution)/shard_map/reduce_sum | solution.py:37
  378.3 2.2 fusion.26
  380.6 56.8 %reduce-scatter.15.cloned.1.call-done = f32[16,384]{1,0:T(8,128)} async-done(((f32[256,384]{1,0:T(8,128)}), f32[16,384]{1,0:T(8,128)}) %reduce-scatter.15.cloned.1.call-update) | async-done | bytes 24592 | tf_op jit(solution)/shard_map/reduce_scatter | solution.py:70
  438.2 20.8 %all_gather.23 = f32[256,384]{1,0:T(8,128)S(1)} all-gather(f32[16,384]{1,0:T(8,128)S(1)} %dynamic-slice_subtract_fusion), channel_id=1, replica_groups=mesh['sens'=2,'src'=16] {'src'}, dimensions={0}, use_global_device_ids=true | all-gather | bytes 417792 | tf_op jit(solution)/shard_map/all_gather | solution.py:72
  460.5 12.9 %fusion.21 = (f32[64,384]{1,0:T(8,128)S(1)}, f32[64,384]{1,0:T(8,128)S(1)}) fusion(f32[256,384]{1,0:T(8,128)S(1)} %get-tuple-element.19, f32[256,384]{1,0:T(8,128)S(1)} %get-tuple-element.18, bf16[2,256,64,384]{3,2,1,0:T(8,128)(2,1)} %param.6), kind=kLoop, calls=%fused_computation.45 | loop fusion | flops 62865408 | bytes 26148864 | tf_op jit(solution)/shard_map/reduce_sum | solution.py:48
  473.4 1.9 fusion.65
  475.3 7.5 %reduce-scatter.17.cloned.1.call-done = f32[32,384]{1,0:T(8,128)} async-done(((f32[64,384]{1,0:T(8,128)}), f32[32,384]{1,0:T(8,128)}) %reduce-scatter.17.cloned.1.call-update) | async-done | bytes 49168 | tf_op jit(solution)/shard_map/reduce_scatter | solution.py:76
  482.8 1.5 multiply_reduce_fusion
  484.2 39.5 %psum.23 = f32[]{:T(128)} all-reduce(f32[]{:T(128)} %multiply_reduce_fusion), channel_id=1, replica_groups=mesh['sens'=2,'src'=16] {'sens','src'}, use_global_device_ids=true, to_apply=%region_23.24 | all-reduce | flops 1 | bytes 8 | tf_op jit(solution)/shard_map/psum | solution.py:78
  524.4 1.5 divide_subtract_fusion
  (37 shorter events, 12.4 us)
Async XLA Ops:
  7.2 88.3 %reduce-scatter.7.cloned.1.call-start = ((), (), s32[]{:S(2)}) async-start(), calls=%async_computation.6 | async-start | bytes 417792 | tf_op jit(solution)/shard_map/reduce_scatter | solution.py:70
  37.6 103.1 %reduce-scatter.9.cloned.1.call-start = ((), (), s32[]{:S(2)}) async-start(), calls=%async_computation.7 | async-start | bytes 147456 | tf_op jit(solution)/shard_map/reduce_scatter | solution.py:76
  118.4 22.2 %copy-start = (f32[32,384]{1,0:T(8,128)S(1)}, f32[32,384]{1,0:T(8,128)}, u32[]{:S(2)}) copy-start(f32[32,384]{1,0:T(8,128)} %param.4) | copy-start | bytes 147460
  118.4 22.2 %copy-start.2 = (f32[32]{0:T(128)S(1)}, f32[32]{0:T(128)}, u32[]{:S(2)}) copy-start(f32[32]{0:T(128)} %param.5) | copy-start | bytes 388
  133.1 133.4 %reduce-scatter.11.cloned.1.call-start = ((), (), s32[]{:S(2)}) async-start(), calls=%async_computation.8 | async-start | bytes 417792 | tf_op jit(solution)/shard_map/reduce_scatter | solution.py:70
  209.6 102.0 %reduce-scatter.13.cloned.1.call-start = ((), (), s32[]{:S(2)}) async-start(), calls=%async_computation.9 | async-start | bytes 147456 | tf_op jit(solution)/shard_map/reduce_scatter | solution.py:76
  304.2 133.2 %reduce-scatter.15.cloned.1.call-start = ((), (), s32[]{:S(2)}) async-start(), calls=%async_computation.10 | async-start | bytes 417792 | tf_op jit(solution)/shard_map/reduce_scatter | solution.py:70
  380.6 102.2 %reduce-scatter.17.cloned.1.call-start = ((), (), s32[]{:S(2)}) async-start(), calls=%async_computation.11 | async-start | bytes 147456 | tf_op jit(solution)/shard_map/reduce_scatter | solution.py:76
  438.2 35.2 %copy-start.1 = (f32[16,384]{1,0:T(8,128)}, f32[16,384]{1,0:T(8,128)S(1)}, u32[]{:S(2)}) copy-start(f32[16,384]{1,0:T(8,128)S(1)} %dynamic-slice_subtract_fusion) | copy-start | bytes 73732
Sparse Core Ops, SparseCore 0:
  37.7 57.7 reduce-scatter.6
  133.3 7.3 reduce-scatter.8
  209.7 56.7 reduce-scatter.10
  304.3 7.3 reduce-scatter.12
  380.7 56.6 reduce-scatter.14
  475.4 7.3 reduce-scatter.16
where the time goes:
time: 534 us; the launch traced here: 533 us
  blocking collectives  196 us (37%)
  waiting for transfers between devices  194 us (36%)
  other arithmetic  107 us (20%)
  matrix products  19.1 us (4%)
  between operations  16.4 us (3%)
    reduce_scatter x3, waiting for transfers between devices, local(): summed = lax.psum_scatter(terms, 'src', scatter_dimension=0, tiled=True)  171 us
    psum x3, blocking collectives, local(): square_sum = lax.psum(jnp.sum(gradient * gradient), ('sens', 'src'))  118 us
    all_gather x3, blocking collectives, local(): residual = lax.all_gather(misfit, 'src', axis=0, tiled=True)  62.1 us
    reduce_sum x3, other arithmetic, forward_terms(): jnp.sum(kernel_real * real_part - kernel_imag * imag_part, axis=1)  54.8 us
    reduce_sum x3, other arithmetic, adjoint_terms(): jnp.sum(kernel_real * real_part + kernel_imag * imag_part, axis=0)  38.5 us
    reduce_scatter x3, waiting for transfers between devices, local(): lax.psum_scatter(back_terms, 'sens', scatter_dimension=0, tiled=True)  22.4 us
    all_gather x3, blocking collectives, local(): slips = lax.all_gather(slip, 'sens', axis=0, tiled=True)  15.7 us
  transfers between devices with their start and end apart: 6, of which 6 were waited for; matrix products, arithmetic and copies ran while one was open for 0% of the time, Pallas kernels for 0%

commit v1 on v0

v1 whole, which is shorter than its diff:
```python
import math

import jax
import jax.numpy as jnp
from jax import lax
from jax.sharding import Mesh, PartitionSpec as P

ITERS = 3

highest = lax.Precision.HIGHEST
step_rate = 0.3
epsilon = 1e-06


def forward_table(length):
    padded = 2 * length
    sample_index = jnp.arange(length, dtype=jnp.int32)[:, None]
    freq_index = jnp.arange(length, dtype=jnp.int32)[None, :]
    phases = (sample_index * freq_index % padded).astype(jnp.float32) * (2.0 * math.pi / padded)
    return jnp.concatenate([jnp.cos(phases), -jnp.sin(phases)], axis=1)


def spectral_weights(length):
    padded = 2 * length
    column = jnp.arange(2 * length, dtype=jnp.int32) % length
    return jnp.where(column == 0, 1.0 / padded, 2.0 / padded).astype(jnp.float32)


def forward_terms(kernel, spectra):
    freqs = kernel.shape[-1]
    real_part = spectra[:, :freqs][None]
    imag_part = spectra[:, freqs:][None]
    kernel_real = kernel[0].astype(jnp.float32)
    kernel_imag = kernel[1].astype(jnp.float32)
    out_real = jnp.sum(kernel_real * real_part - kernel_imag * imag_part, axis=1)
    out_imag = jnp.sum(kernel_real * imag_part + kernel_imag * real_part, axis=1)
    return jnp.concatenate([out_real, out_imag], axis=1)


def adjoint_terms(kernel, spectra):
    freqs = kernel.shape[-1]
    real_part = spectra[:, :freqs][:, None]
    imag_part = spectra[:, freqs:][:, None]
    kernel_real = kernel[0].astype(jnp.float32)
    kernel_imag = kernel[1].astype(jnp.float32)
    back_real = jnp.sum(kernel_real * real_part + kernel_imag * imag_part, axis=0)
    back_imag = jnp.sum(kernel_real * imag_part - kernel_imag * real_part, axis=0)
    return jnp.concatenate([back_real, back_imag], axis=1)


def swap_cores(x):
    return lax.ppermute(x, "core", [(0, 1), (1, 0)])


def gather_sens(x):
    if lax.axis_size("sens") == 2:
        first = lax.axis_index("sens") == 0
        other = lax.ppermute(x, "sens", [(0, 1), (1, 0)])
        return jnp.concatenate([jnp.where(first, x, other), jnp.where(first, other, x)], axis=0)
    return lax.all_gather(x, "sens", axis=0, tiled=True)


def sum_sens(x):
    if lax.axis_size("sens") == 2:
        return x + lax.ppermute(x, "sens", [(0, 1), (1, 0)])
    return lax.psum(x, "sens")


def scatter_sum_src(x):
    chips, cores = lax.axis_size("chip"), lax.axis_size("core")
    x = x.reshape(chips, cores, -1, x.shape[-1])
    if cores == 2:
        first = lax.axis_index("core") == 0
        keep = jnp.where(first, x[:, 0], x[:, 1])
        send = jnp.where(first, x[:, 1], x[:, 0])
        x = keep + swap_cores(send)
    else:
        x = x[:, 0]
    return jnp.sum(lax.all_to_all(x, "chip", 0, 0), axis=0)


def gather_src(x):
    chips, cores = lax.axis_size("chip"), lax.axis_size("core")
    rows, width = x.shape
    mine = lax.all_to_all(jnp.broadcast_to(x[None], (chips, rows, width)), "chip", 0, 0)
    if cores == 2:
        first = lax.axis_index("core") == 0
        other = swap_cores(mine)
        mine = jnp.stack([jnp.where(first, mine, other), jnp.where(first, other, mine)], axis=1)
    return mine.reshape(chips * cores * rows, width)


def sum_src_scalar(value):
    count = lax.axis_size("chip") * lax.axis_size("core")
    sent = jnp.broadcast_to(value.reshape(1, 1), (count, 128))
    return jnp.sum(lax.all_to_all(sent, ("chip", "core"), 0, 0)[:, 0])


def local(slip_param, rigidity, kernel, observed):
    length = slip_param.shape[1]
    own_sources = slip_param.shape[0]
    table = forward_table(length)
    weighted = table * spectral_weights(length)[None, :]
    src = lax.axis_size("chip") * lax.axis_size("core")
    src_index = lax.axis_index("chip") * lax.axis_size("core") + lax.axis_index("core")
    own_count = kernel.shape[1] // src
    own_observed = lax.dynamic_slice_in_dim(observed, src_index * own_count, own_count, 0)
    entry_count = own_sources * lax.axis_size("sens") * src * length
    packed = gather_sens(jnp.concatenate([slip_param, jnp.broadcast_to(rigidity[:, None], (own_sources, 128))], axis=1))
    param, scale_rows = packed[:, :length], packed[:, length:length + 1]
    misfit = own_observed
    for iteration in range(ITERS):
        slip = scale_rows * jax.nn.softplus(param)
        spectra = jnp.dot(slip, table, precision=highest)
        terms = forward_terms(kernel, spectra)
        terms = jnp.dot(terms, weighted.T, precision=highest)
        misfit = scatter_sum_src(terms) - own_observed
        residual = gather_src(misfit)
        adjoint_spec = jnp.dot(residual, weighted, precision=highest)
        back_terms = adjoint_terms(kernel, adjoint_spec)
        back_terms = jnp.dot(back_terms, table.T, precision=highest)
        gradient = sum_sens(back_terms) * scale_rows * jax.nn.sigmoid(param)
        square_sum = sum_src_scalar(jnp.sum(gradient * gradient))
        root_mean = jnp.sqrt(square_sum / entry_count + epsilon)
        param = param - step_rate * gradient / root_mean
    own_param = lax.dynamic_slice_in_dim(param, lax.axis_index("sens") * own_sources, own_sources, 0)
    return (own_param, misfit)


def solution(mesh):
    sens, src = mesh.shape["sens"], mesh.shape["src"]
    cores = 2 if src % 2 == 0 else 1
    split = Mesh(mesh.devices.reshape(sens, src // cores, cores), ("sens", "chip", "core"))
    in_specs = (
        P(("chip", "core", "sens"), None),
        P(("chip", "core", "sens")),
        P(None, "sens", ("chip", "core"), None),
        P("sens", None),
    )
    out_specs = (P(("chip", "core", "sens"), None), P(("sens", "chip", "core"), None))
    return jax.shard_map(local, mesh=split, in_specs=in_specs, out_specs=out_specs, check_vma=False)
```

time: 534 us -> 252 us (0.47)
  waiting for transfers between devices: 194 us -> 33.1 us
  blocking collectives: 196 us -> 72.9 us
  starting transfers between devices: 0.25 us -> 17.6 us
  between operations: 16.4 us -> 3.11 us
    reduce_scatter x6 -> x0, waiting for transfers between devices: 194 us -> none  [the longest x3 171 us: local(): summed = lax.psum_scatter(terms, 'src', scatter_dimension=0, tiled=True)]
    psum x3 -> x0, blocking collectives: 118 us -> none  [local(): square_sum = lax.psum(jnp.sum(gradient * gradient), ('sens', 'src'))]
    all_gather x6 -> x0, blocking collectives: 77.8 us -> none  [the longest x3 62.1 us: local(): residual = lax.all_gather(misfit, 'src', axis=0, tiled=True)]
    all_to_all x0 -> x7, blocking collectives: none -> 72.9 us  [the longest x3 32.2 us: gather_src(): lax.all_to_all(jnp.broadcast_to(x[None], (chips, rows, width)), 'chip', 0...]
    ppermute x0 -> x10, waiting for transfers between devices: none -> 18.5 us  [the longest x3 9.93 us: sum_sens(): return x + lax.ppermute(x, 'sens', [(0, 1), (1, 0)])]
    all_to_all x0 -> x2, waiting for transfers between devices: none -> 14.6 us  [the longest x1 8.26 us: scatter_sum_src(): return jnp.sum(lax.all_to_all(x, 'chip', 0, 0), axis=0)]
    all_to_all x0 -> x2, starting transfers between devices: none -> 9.62 us  [the longest x1 6.14 us: scatter_sum_src(): return jnp.sum(lax.all_to_all(x, 'chip', 0, 0), axis=0)]
    ppermute x0 -> x10, starting transfers between devices: none -> 7.97 us  [the longest x3 4.78 us: sum_sens(): return x + lax.ppermute(x, 'sens', [(0, 1), (1, 0)])]
  transfers between devices with their start and end apart: 6 -> 12, of which waited for: 6 -> 11; matrix products, arithmetic and copies ran while one was open for 0% -> 1% of each run, Pallas kernels for 0% -> 0%
where the time goes in v1:
time: 252 us; the launch traced here: 251 us
  other arithmetic  106 us (42%)
  blocking collectives  72.9 us (29%)
  waiting for transfers between devices  33.1 us (13%)
  starting transfers between devices  17.6 us (7%)
  matrix products  15.1 us (6%)
  local copies, waits for them, and re-layouts  3.62 us (1%)
  between operations  3.11 us (1%)
    reduce_sum x3, other arithmetic, forward_terms(): jnp.sum(kernel_real * real_part - kernel_imag * imag_part, axis=1)  54.9 us
    reduce_sum x3, other arithmetic, adjoint_terms(): jnp.sum(kernel_real * real_part + kernel_imag * imag_part, axis=0)  38.6 us
    all_to_all x3, blocking collectives, gather_src(): lax.all_to_all(jnp.broadcast_to(x[None], (chips, rows, width)), 'chip', 0...  32.2 us
    all_to_all x2, blocking collectives, scatter_sum_src(): return jnp.sum(lax.all_to_all(x, 'chip', 0, 0), axis=0)  21.9 us
    all_to_all x2, blocking collectives, sum_src_scalar(): return jnp.sum(lax.all_to_all(sent, ('chip', 'core'), 0, 0)[:, 0])  18.8 us
    ppermute x3, waiting for transfers between devices, sum_sens(): return x + lax.ppermute(x, 'sens', [(0, 1), (1, 0)])  9.93 us
    ppermute x6, waiting for transfers between devices, swap_cores(): return lax.ppermute(x, 'core', [(0, 1), (1, 0)])  8.6 us
    all_to_all x1, waiting for transfers between devices, scatter_sum_src(): return jnp.sum(lax.all_to_all(x, 'chip', 0, 0), axis=0)  8.26 us
  transfers between devices with their start and end apart: 12, of which 11 were waited for; matrix products, arithmetic and copies ran while one was open for 1% of the time, Pallas kernels for 0%

profile of v1, /device:TPU:0, one launch (start us, length us, event | category | flops | bytes accessed | tf_op | source)
XLA Modules:
  0.0 251.0 jit_solution(16310873602990406628)
XLA Ops:
  2.2 3.0 %collective-permute-start = (f32[32,512]{1,0:T(8,128)S(1)}, f32[32,512]{1,0:T(8,128)S(1)}, u32[]{:S(2)}, u32[]{:S(2)}) collective-permute-start(f32[32,512]{1,0:T(8,128)S(1)} %pad_maximum_fusion.4), channel_id=1, source_target_pairs={{0,16},{16,0},{1,17},{17,1},{2,18},{18,2},{3,19},{19,3},{4,20},{20... | collective-permute-start | bytes 196616 | tf_op jit(solution)/shard_map/ppermute | solution.py:58
  5.1 2.4 sine_negate_fusion
  9.4 18.3 %fusion.1 = (f32[256,384]{1,0:T(8,128)S(1)}, f32[256,384]{1,0:T(8,128)S(1)}) fusion(f32[64,384]{1,0:T(8,128)S(1)} %get-tuple-element.37, f32[64,384]{1,0:T(8,128)S(1)} %get-tuple-element.36, bf16[2,256,64,384]{3,2,1,0:T(8,128)(2,1)} %param.6), kind=kLoop, calls=%fused_computation.25 | loop fusion | flops 62717952 | bytes 26148864 | tf_op jit(solution)/shard_map/reduce_sum | solution.py:35
  27.7 1.5 fusion.34
  31.4 6.1 %all-to-all-start = ((f32[8,16,384]{2,1,0:T(8,128)}), f32[8,16,384]{2,1,0:T(8,128)S(1)}, u32[]{:S(2)}, u32[]{:S(2)}) async-start(f32[8,16,384]{2,1,0:T(8,128)} %fusion.70), calls=%async_computation | async-start | bytes 393216 | tf_op jit(solution)/shard_map/all_to_all | solution.py:79
  37.6 8.3 %all-to-all-done = f32[8,16,384]{2,1,0:T(8,128)S(1)} async-done(((f32[8,16,384]{2,1,0:T(8,128)}), f32[8,16,384]{2,1,0:T(8,128)S(1)}, u32[]{:S(2)}, u32[]{:S(2)}) %all-to-all-start) | async-done | bytes 196640 | tf_op jit(solution)/shard_map/all_to_all | solution.py:79
  46.6 10.7 %all_to_all.57 = f32[8,16,384]{2,1,0:T(8,128)S(1)} all-to-all(f32[8,16,384]{2,1,0:T(8,128)S(1)} %broadcast_in_dim.25), channel_id=1, replica_groups=mesh['sens'=2,'chip'=8,'core'=2] {'chip'}, dimensions={0} | all-to-all | bytes 393216 | tf_op jit(solution)/shard_map/all_to_all | solution.py:85
  57.4 1.4 collective-permute-done.2
  58.9 1.5 fusion.32
  60.4 12.9 %fusion.5 = (f32[64,384]{1,0:T(8,128)S(1)}, f32[64,384]{1,0:T(8,128)S(1)}) fusion(f32[256,384]{1,0:T(8,128)S(1)} %get-tuple-element.25, f32[256,384]{1,0:T(8,128)S(1)} %get-tuple-element.24, bf16[2,256,64,384]{3,2,1,0:T(8,128)(2,1)} %param.6), kind=kLoop, calls=%fused_computation.29 | loop fusion | flops 62865408 | bytes 26148864 | tf_op jit(solution)/shard_map/reduce_sum | solution.py:46
  74.5 1.6 collective-permute-start.3
  76.1 3.3 %collective-permute-done.3 = f32[64,384]{1,0:T(8,128)S(1)} collective-permute-done((f32[64,384]{1,0:T(8,128)S(1)}, f32[64,384]{1,0:T(8,128)S(1)}, u32[]{:S(2)}, u32[]{:S(2)}) %collective-permute-start.3) | collective-permute-done | bytes 98336 | tf_op jit(solution)/shard_map/ppermute | solution.py:65
  80.8 9.4 %all_to_all.58 = f32[16,1,128]{2,1,0:T(1,128)S(1)} all-to-all(f32[16,1,128]{2,1,0:T(1,128)S(1)} %broadcast_in_dim.26), channel_id=1, replica_groups=mesh['sens'=2,'chip'=8,'core'=2] {'chip','core'}, dimensions={0} | all-to-all | bytes 16384 | tf_op jit(solution)/shard_map/all_to_all | solution.py:96
  92.4 18.3 %fusion.9 = (f32[256,384]{1,0:T(8,128)S(1)}, f32[256,384]{1,0:T(8,128)S(1)}) fusion(f32[64,384]{1,0:T(8,128)S(1)} %get-tuple-element.35, f32[64,384]{1,0:T(8,128)S(1)} %get-tuple-element.34, bf16[2,256,64,384]{3,2,1,0:T(8,128)(2,1)} %param.6), kind=kLoop, calls=%fused_computation.33 | loop fusion | flops 62717952 | bytes 26148864 | tf_op jit(solution)/shard_map/reduce_sum | solution.py:35
  110.7 1.5 fusion.30
  113.7 10.9 %all_to_all.59 = f32[8,16,384]{2,1,0:T(8,128)S(1)} all-to-all(f32[8,16,384]{2,1,0:T(8,128)S(1)} %bitcast_add_fusion.1), channel_id=1, replica_groups=mesh['sens'=2,'chip'=8,'core'=2] {'chip'}, dimensions={0} | all-to-all | bytes 393216 | tf_op jit(solution)/shard_map/all_to_all | solution.py:79
  125.5 10.7 %all_to_all.60 = f32[8,16,384]{2,1,0:T(8,128)S(1)} all-to-all(f32[8,16,384]{2,1,0:T(8,128)S(1)} %broadcast_in_dim.27), channel_id=1, replica_groups=mesh['sens'=2,'chip'=8,'core'=2] {'chip'}, dimensions={0} | all-to-all | bytes 393216 | tf_op jit(solution)/shard_map/all_to_all | solution.py:85
  137.7 1.5 fusion.28
  139.3 12.9 %fusion.13 = (f32[64,384]{1,0:T(8,128)S(1)}, f32[64,384]{1,0:T(8,128)S(1)}) fusion(f32[256,384]{1,0:T(8,128)S(1)} %get-tuple-element.23, f32[256,384]{1,0:T(8,128)S(1)} %get-tuple-element.22, bf16[2,256,64,384]{3,2,1,0:T(8,128)(2,1)} %param.6), kind=kLoop, calls=%fused_computation.37 | loop fusion | flops 62865408 | bytes 26148864 | tf_op jit(solution)/shard_map/reduce_sum | solution.py:46
  153.4 1.6 collective-permute-start.6
  155.0 3.3 %collective-permute-done.6 = f32[64,384]{1,0:T(8,128)S(1)} collective-permute-done((f32[64,384]{1,0:T(8,128)S(1)}, f32[64,384]{1,0:T(8,128)S(1)}, u32[]{:S(2)}, u32[]{:S(2)}) %collective-permute-start.6) | collective-permute-done | bytes 98336 | tf_op jit(solution)/shard_map/ppermute | solution.py:65
  159.6 9.4 %all_to_all.61 = f32[16,1,128]{2,1,0:T(1,128)S(1)} all-to-all(f32[16,1,128]{2,1,0:T(1,128)S(1)} %broadcast_in_dim.28), channel_id=1, replica_groups=mesh['sens'=2,'chip'=8,'core'=2] {'chip','core'}, dimensions={0} | all-to-all | bytes 16384 | tf_op jit(solution)/shard_map/all_to_all | solution.py:96
  171.3 18.3 %fusion.17 = (f32[256,384]{1,0:T(8,128)S(1)}, f32[256,384]{1,0:T(8,128)S(1)}) fusion(f32[64,384]{1,0:T(8,128)S(1)} %get-tuple-element.33, f32[64,384]{1,0:T(8,128)S(1)} %get-tuple-element.32, bf16[2,256,64,384]{3,2,1,0:T(8,128)(2,1)} %param.6), kind=kLoop, calls=%fused_computation.41 | loop fusion | flops 62717952 | bytes 26148864 | tf_op jit(solution)/shard_map/reduce_sum | solution.py:35
  189.6 1.5 fusion.26
  192.6 10.9 %all_to_all.62 = f32[8,16,384]{2,1,0:T(8,128)S(1)} all-to-all(f32[8,16,384]{2,1,0:T(8,128)S(1)} %bitcast_add_fusion), channel_id=1, replica_groups=mesh['sens'=2,'chip'=8,'core'=2] {'chip'}, dimensions={0} | all-to-all | bytes 393216 | tf_op jit(solution)/shard_map/all_to_all | solution.py:79
  204.3 10.7 %all_to_all.63 = f32[8,16,384]{2,1,0:T(8,128)S(1)} all-to-all(f32[8,16,384]{2,1,0:T(8,128)S(1)} %broadcast_in_dim.29), channel_id=1, replica_groups=mesh['sens'=2,'chip'=8,'core'=2] {'chip'}, dimensions={0} | all-to-all | bytes 393216 | tf_op jit(solution)/shard_map/all_to_all | solution.py:85
  216.6 1.5 fusion.24
  218.1 12.9 %fusion.21 = (f32[64,384]{1,0:T(8,128)S(1)}, f32[64,384]{1,0:T(8,128)S(1)}) fusion(f32[256,384]{1,0:T(8,128)S(1)} %get-tuple-element.21, f32[256,384]{1,0:T(8,128)S(1)} %get-tuple-element.20, bf16[2,256,64,384]{3,2,1,0:T(8,128)(2,1)} %param.6), kind=kLoop, calls=%fused_computation.45 | loop fusion | flops 62865408 | bytes 26148864 | tf_op jit(solution)/shard_map/reduce_sum | solution.py:46
  232.3 1.6 collective-permute-start.9
  233.9 3.3 %collective-permute-done.9 = f32[64,384]{1,0:T(8,128)S(1)} collective-permute-done((f32[64,384]{1,0:T(8,128)S(1)}, f32[64,384]{1,0:T(8,128)S(1)}, u32[]{:S(2)}, u32[]{:S(2)}) %collective-permute-start.9) | collective-permute-done | bytes 98336 | tf_op jit(solution)/shard_map/ppermute | solution.py:65
  239.2 3.5 %all-to-all-start.8 = ((f32[16,1,128]{2,1,0:T(1,128)}), f32[16,1,128]{2,1,0:T(1,128)S(1)}, u32[]{:S(2)}, u32[]{:S(2)}) async-start(f32[16,1,128]{2,1,0:T(1,128)} %broadcast_in_dim.30), calls=%async_computation.8 | async-start | bytes 16384 | tf_op jit(solution)/shard_map/all_to_all | solution.py:96
  242.7 6.3 %all-to-all-done.8 = f32[16,1,128]{2,1,0:T(1,128)S(1)} async-done(((f32[16,1,128]{2,1,0:T(1,128)}), f32[16,1,128]{2,1,0:T(1,128)S(1)}, u32[]{:S(2)}, u32[]{:S(2)}) %all-to-all-start.8) | async-done | bytes 8224 | tf_op jit(solution)/shard_map/all_to_all | solution.py:96
  (66 shorter events, 27.0 us)
Async XLA Ops:
  2.2 5.4 %collective-permute-start = (f32[32,512]{1,0:T(8,128)S(1)}, f32[32,512]{1,0:T(8,128)S(1)}, u32[]{:S(2)}, u32[]{:S(2)}) collective-permute-start(f32[32,512]{1,0:T(8,128)S(1)} %pad_maximum_fusion.4), channel_id=1, source_target_pairs={{0,16},{16,0},{1,17},{17,1},{2,18},{18,2},{3,19},{19,3},{4,20},{20... | collective-permute-start | bytes 196616 | tf_op jit(solution)/shard_map/ppermute | solution.py:58
  29.2 1.5 collective-permute-start.1
  31.4 14.4 %all-to-all-start = ((f32[8,16,384]{2,1,0:T(8,128)}), f32[8,16,384]{2,1,0:T(8,128)S(1)}, u32[]{:S(2)}, u32[]{:S(2)}) async-start(f32[8,16,384]{2,1,0:T(8,128)} %fusion.70), calls=%async_computation | async-start | bytes 393216 | tf_op jit(solution)/shard_map/all_to_all | solution.py:79
  57.4 1.4 collective-permute-start.2
  74.5 4.9 %collective-permute-start.3 = (f32[64,384]{1,0:T(8,128)S(1)}, f32[64,384]{1,0:T(8,128)S(1)}, u32[]{:S(2)}, u32[]{:S(2)}) collective-permute-start(f32[64,384]{1,0:T(8,128)S(1)} %fusion.57), channel_id=1, source_target_pairs={{0,16},{16,0},{1,17},{17,1},{2,18},{18,2},{3,19},{19,3},{4,20},{20... | collective-permute-start | bytes 294920 | tf_op jit(solution)/shard_map/ppermute | solution.py:65
  112.2 1.5 collective-permute-start.4
  136.2 1.4 collective-permute-start.5
  153.4 4.9 %collective-permute-start.6 = (f32[64,384]{1,0:T(8,128)S(1)}, f32[64,384]{1,0:T(8,128)S(1)}, u32[]{:S(2)}, u32[]{:S(2)}) collective-permute-start(f32[64,384]{1,0:T(8,128)S(1)} %fusion.61), channel_id=1, source_target_pairs={{0,16},{16,0},{1,17},{17,1},{2,18},{18,2},{3,19},{19,3},{4,20},{20... | collective-permute-start | bytes 294920 | tf_op jit(solution)/shard_map/ppermute | solution.py:65
  191.1 1.5 collective-permute-start.7
  204.3 26.7 %copy-start = (f32[16,384]{1,0:T(8,128)}, f32[16,384]{1,0:T(8,128)S(1)}, u32[]{:S(2)}) copy-start(f32[16,384]{1,0:T(8,128)S(1)} %dynamic-slice_subtract_fusion.1) | copy-start | bytes 73732
  215.1 1.4 collective-permute-start.8
  232.3 4.9 %collective-permute-start.9 = (f32[64,384]{1,0:T(8,128)S(1)}, f32[64,384]{1,0:T(8,128)S(1)}, u32[]{:S(2)}, u32[]{:S(2)}) collective-permute-start(f32[64,384]{1,0:T(8,128)S(1)} %fusion.65), channel_id=1, source_target_pairs={{0,16},{16,0},{1,17},{17,1},{2,18},{18,2},{3,19},{19,3},{4,20},{20... | collective-permute-start | bytes 294920 | tf_op jit(solution)/shard_map/ppermute | solution.py:65
  239.2 9.8 %all-to-all-start.8 = ((f32[16,1,128]{2,1,0:T(1,128)}), f32[16,1,128]{2,1,0:T(1,128)S(1)}, u32[]{:S(2)}, u32[]{:S(2)}) async-start(f32[16,1,128]{2,1,0:T(1,128)} %broadcast_in_dim.30), calls=%async_computation.8 | async-start | bytes 16384 | tf_op jit(solution)/shard_map/all_to_all | solution.py:96

commit v2 on v0

v2 whole, which is shorter than its diff:
```python
import functools
import math

import jax
import jax.numpy as jnp
import numpy as np
from jax import lax
from jax.experimental import pallas as pl
from jax.experimental.pallas import tpu as pltpu
from jax.sharding import Mesh, PartitionSpec as P

ITERS = 3

highest = lax.Precision.HIGHEST
step_rate = 0.3
epsilon = 1e-06
f32, bf16 = jnp.float32, jnp.bfloat16
LANES = 128
HALF = LANES // 2
NN, NT = ((1,), (0,)), ((1,), (1,))
VM = pl.BlockSpec(memory_space=pltpu.VMEM)
SM = pl.BlockSpec(memory_space=pltpu.SMEM)
ROWS = 16
UNROLL = 24


def table_parts(length):
    padded = 2 * length
    phases = np.outer(np.arange(length), np.arange(length)) % padded * (2.0 * math.pi / padded)
    table = np.concatenate([np.cos(phases), -np.sin(phases)], axis=0).astype(np.float32)
    high = table.astype(jnp.bfloat16)
    return jnp.asarray(np.stack([high, (table - high.astype(np.float32)).astype(jnp.bfloat16)]))


def row_weights(length):
    row = lax.broadcasted_iota(jnp.int32, (length, 1), 0)
    return jnp.where(row == 0, 0.5 / length, 1.0 / length).astype(f32)


def params(mib):
    return pltpu.CompilerParams(vmem_limit_bytes=mib << 20)


def mm(a, b, dims):
    return lax.dot_general(a, b, (dims, ((), ())), preferred_element_type=f32)


def split(x):
    high = x.astype(bf16)
    return high, (x - high.astype(f32)).astype(bf16)


def mm3(a, b, dims):
    return mm(a[0], b[0], dims) + (mm(a[0], b[1], dims) + mm(a[1], b[0], dims))


def relayout_body(k_hbm, out_ref, buf, stage, sem):
    freqs = k_hbm.shape[3]
    steps = k_hbm.shape[1] // ROWS
    same = lax.broadcasted_iota(jnp.int32, (LANES, LANES), 0) == lax.broadcasted_iota(jnp.int32, (LANES, LANES), 1)
    eye = same.astype(f32).astype(bf16)

    def copy(i, slot):
        return pltpu.make_async_copy(k_hbm.at[:, pl.ds(i * ROWS, ROWS)], buf.at[slot], sem.at[slot])

    copy(0, 0).start()

    def step(i, carry):
        slot = lax.rem(i, 2)
        copy(i, slot).wait()

        @pl.when(i + 1 < steps)
        def _():
            copy(i + 1, 1 - slot).start()

        for r in range(0, ROWS, 2):
            x = jnp.concatenate([buf[slot, c, r + j] for j in range(2) for c in range(2)], axis=0)
            for chunk in range(freqs // LANES):
                o = mm(eye, x[:, chunk * LANES:(chunk + 1) * LANES], NT)
                for j in range(2):
                    for h in range(2):
                        rows = pl.ds(chunk * HALF * ROWS + r + j, HALF, stride=ROWS)
                        stage[h, rows, :] = o[h * HALF:(h + 1) * HALF, j * LANES:(j + 1) * LANES]
        rows = pl.ds(pl.multiple_of(i * ROWS, ROWS), ROWS)
        for h in range(2):
            out_ref[:, rows, h * LANES:(h + 1) * LANES] = stage[h].reshape(freqs // 2, ROWS, LANES).astype(bf16)
        return carry

    lax.fori_loop(0, steps, step, 0)


def relayout(kernel):
    _, sensors, sources, freqs = kernel.shape
    return pl.pallas_call(
        relayout_body,
        in_specs=[pl.BlockSpec(memory_space=pl.ANY)],
        out_specs=VM,
        out_shape=pltpu.VMEM((freqs // 2, sensors, 4 * sources), bf16),
        scratch_shapes=[
            pltpu.VMEM((2, 2, ROWS, sources, freqs), bf16),
            pltpu.VMEM((2, freqs // 2 * ROWS, LANES), f32),
            pltpu.SemaphoreType.DMA((2,)),
        ],
        compiler_params=params(10),
        name="relayout",
    )(kernel)


def pair_row(chunk, h, m):
    return pl.ds(chunk * HALF * 8 + 4 * h + m, HALF, stride=8)


def contract(k_ref, lhs, res, dims):
    pairs = k_ref.shape[0]

    def step(i, carry):
        for u in range(UNROLL):
            pair = i * UNROLL + u
            rows = pl.ds(pl.multiple_of(pair * 8, 8), 8)
            a = jnp.concatenate([lhs[0, rows, :], lhs[1, rows, :]], axis=1).astype(bf16)
            o = mm(a, k_ref[pair], dims)
            res[0, rows, :] = o[:, :LANES]
            res[1, rows, :] = o[:, LANES:]
        return carry

    lax.fori_loop(0, pairs // UNROLL, step, 0)


def forward_core(param, k_ref, rig_ref, t_ref, core_ref, keep_ref, send_ref, lhs, res, terms):
    freqs, sources = param.shape[1], param.shape[0]
    slip = rig_ref[...] * jax.nn.softplus(param)
    z = mm3((t_ref[0], t_ref[1]), split(jnp.concatenate([slip, slip], axis=0)), NT)
    low = lax.broadcasted_iota(jnp.int32, (freqs, LANES), 1) < sources
    real, imag = z[:freqs], z[freqs:]
    zero = jnp.zeros((HALF, LANES), f32)
    for m, x in enumerate((jnp.where(low, real, -imag), jnp.where(low, imag, real))):
        high = x.astype(bf16).astype(f32)
        for n, v in enumerate((high, x - high)):
            for chunk in range(freqs // LANES):
                for h in range(2):
                    first = chunk * LANES + h * HALF
                    lhs[h, pair_row(chunk, h, 2 * n + m), :] = v[first:first + HALF]
                    lhs[1 - h, pair_row(chunk, h, 2 * n + m), :] = zero
    contract(k_ref, lhs, res, NT)
    w = row_weights(freqs)
    halves = []
    for m in range(2):
        parts = []
        for chunk in range(freqs // LANES):
            for h in range(2):
                high, rest = pair_row(chunk, h, m), pair_row(chunk, h, 2 + m)
                parts.append(jnp.concatenate([res[c, high, :] + res[c, rest, :] for c in range(2)], axis=1))
        halves.append(jnp.concatenate(parts, axis=0) * w)
    spectrum = jnp.concatenate(halves, axis=0).T
    terms[...] = mm3(split(spectrum), (t_ref[0], t_ref[1]), NN).reshape(terms.shape)
    core = core_ref[0]
    keep_ref[...] = terms[:, core]
    send_ref[...] = terms[:, terms.shape[1] - 1 - core]


def forward_first_body(k_ref, p_ref, rig_ref, t_ref, core_ref, keep_ref, send_ref, lhs, res, terms):
    forward_core(p_ref[...], k_ref, rig_ref, t_ref, core_ref, keep_ref, send_ref, lhs, res, terms)


def moved(param, gradient, sums, entries):
    square_sum = jnp.sum(sums[:, 0:1], axis=0, keepdims=True)
    root_mean = jnp.sqrt(square_sum / entries + epsilon)
    return param - step_rate * gradient / root_mean


def forward_next_body(entries, k_ref, p_ref, g_ref, q_ref, rig_ref, t_ref, core_ref, new_ref, keep_ref, send_ref, lhs, res, terms):
    param = moved(p_ref[...], g_ref[...], q_ref[...], entries)
    new_ref[...] = param
    forward_core(param, k_ref, rig_ref, t_ref, core_ref, keep_ref, send_ref, lhs, res, terms)


def forward(k2, param, update, scale_rows, table, core, grid_shape, entries):
    pairs, sensors, _ = k2.shape
    length = param.shape[1]
    chips, cores = grid_shape
    rows = sensors // (chips * cores)
    outs = [jax.ShapeDtypeStruct((chips, rows, length), f32)] * 2
    scratch = [
        pltpu.VMEM((2, pairs * 8, LANES), f32),
        pltpu.VMEM((2, pairs * 8, LANES), f32),
        pltpu.VMEM((chips, cores, rows, length), f32),
    ]
    if update is None:
        keep, send = pl.pallas_call(
            forward_first_body, in_specs=[VM] * 4 + [SM], out_specs=[VM] * 2, out_shape=outs,
            scratch_shapes=scratch, compiler_params=params(12), name="forward_first",
        )(k2, param, scale_rows, table, core)
        return param, keep, send
    return pl.pallas_call(
        functools.partial(forward_next_body, entries), in_specs=[VM] * 6 + [SM], out_specs=[VM] * 3,
        out_shape=[jax.ShapeDtypeStruct(param.shape, f32)] + outs,
        scratch_shapes=scratch, compiler_params=params(12), name="forward_next",
    )(k2, param, *update, scale_rows, table, core)


def adjoint_body(k_ref, mine_ref, other_ref, t_ref, core_ref, o_ref, lhs, res, full):
    freqs, sources = t_ref.shape[2], k_ref.shape[2] // 4
    core = core_ref[0]
    full[:, core] = mine_ref[...]
    full[:, full.shape[1] - 1 - core] = other_ref[...]
    misfit = full[...].reshape(k_ref.shape[1], freqs)
    spectrum = mm3((t_ref[0], t_ref[1]), split(misfit), NT)
    w = row_weights(freqs)
    for m in range(2):
        x = spectrum[m * freqs:(m + 1) * freqs] * w
        high = x.astype(bf16).astype(f32)
        for n, v in enumerate((high, x - high)):
            for chunk in range(freqs // LANES):
                for h in range(2):
                    first = chunk * LANES + h * HALF
                    for c in range(2):
                        lhs[c, pair_row(chunk, h, 2 * n + m), :] = v[first:first + HALF, c * LANES:(c + 1) * LANES]
    contract(k_ref, lhs, res, NN)
    low = lax.broadcasted_iota(jnp.int32, (HALF, LANES), 1) < sources
    parts = []
    for chunk in range(freqs // LANES):
        for h in range(2):
            real, imag = [res[h, pair_row(chunk, h, m), :] + res[h, pair_row(chunk, h, 2 + m), :] for m in range(2)]
            parts.append(jnp.where(low, real, -real) + pltpu.roll(imag, sources, 1))
    back = jnp.concatenate(parts, axis=0).T
    o_ref[...] = mm3(split(back[:sources]), (t_ref[0, :freqs], t_ref[1, :freqs]), NN) + mm3(
        split(back[sources:]), (t_ref[0, freqs:], t_ref[1, freqs:]), NN
    )


def adjoint(k2, mine, other, table, core):
    pairs, sensors, width = k2.shape
    chips, rows, length = mine.shape
    return pl.pallas_call(
        adjoint_body, in_specs=[VM] * 4 + [SM], out_specs=VM,
        out_shape=jax.ShapeDtypeStruct((width // 4, length), f32),
        scratch_shapes=[
            pltpu.VMEM((2, pairs * 8, LANES), f32),
            pltpu.VMEM((2, pairs * 8, LANES), f32),
            pltpu.VMEM((chips, sensors // (chips * rows), rows, length), f32),
        ],
        compiler_params=params(12), name="adjoint",
    )(k2, mine, other, table, core)


def gradient_body(a_ref, b_ref, p_ref, rig_ref, g_ref, q_ref):
    gradient = (a_ref[...] + b_ref[...]) * rig_ref[...] * jax.nn.sigmoid(p_ref[...])
    g_ref[...] = gradient
    total = jnp.sum(jnp.sum(gradient * gradient, axis=0, keepdims=True), axis=1, keepdims=True)
    q_ref[...] = jnp.broadcast_to(total, q_ref.shape)


def gradient_and_square(own, received, param, scale_rows, peers):
    return pl.pallas_call(
        gradient_body, in_specs=[VM] * 4, out_specs=[VM] * 2,
        out_shape=[jax.ShapeDtypeStruct(param.shape, f32), jax.ShapeDtypeStruct((peers, LANES), f32)],
        compiler_params=params(4), name="gradient",
    )(own, received, param, scale_rows)


def swap(x, axis):
    return lax.ppermute(x, axis, [(0, 1), (1, 0)])


def gather_sens(x):
    if lax.axis_size("sens") == 2:
        first = lax.axis_index("sens") == 0
        other = swap(x, "sens")
        return jnp.concatenate([jnp.where(first, x, other), jnp.where(first, other, x)], axis=0)
    return lax.all_gather(x, "sens", axis=0, tiled=True)


def to_chips(x):
    return lax.all_to_all(x, "chip", 0, 0)


def own_misfit(partial, own_observed):
    return jnp.sum(to_chips(partial), axis=0) - own_observed


def from_chips(misfit):
    return to_chips(jnp.broadcast_to(misfit[None], (lax.axis_size("chip"), *misfit.shape)))


def exchange_scalars(sums):
    return lax.all_to_all(sums, ("chip", "core"), 0, 0, tiled=True)


def plain_forward(kernel, slip):
    length = slip.shape[1]
    table = sum(table_parts(length).astype(f32))
    spectra = lax.dot_general(slip, table, (NT, ((), ())), precision=highest)
    real, imag = spectra[None, :, :length], spectra[None, :, length:]
    k_real, k_imag = kernel[0].astype(f32), kernel[1].astype(f32)
    out_real = jnp.sum(k_real * real - k_imag * imag, axis=1)
    out_imag = jnp.sum(k_real * imag + k_imag * real, axis=1)
    w = jnp.tile(row_weights(length), (2, 1))
    return jnp.dot(jnp.concatenate([out_real, out_imag], axis=1), table * w, precision=highest)


def plain_adjoint(kernel, residual):
    length = residual.shape[1]
    table = sum(table_parts(length).astype(f32))
    w = jnp.tile(row_weights(length), (2, 1))
    spectrum = lax.dot_general(residual, table * w, (NT, ((), ())), precision=highest)
    real, imag = spectrum[:, None, :length], spectrum[:, None, length:]
    k_real, k_imag = kernel[0].astype(f32), kernel[1].astype(f32)
    back_real = jnp.sum(k_real * real + k_imag * imag, axis=0)
    back_imag = jnp.sum(k_real * imag - k_imag * real, axis=0)
    return jnp.dot(jnp.concatenate([back_real, back_imag], axis=1), table, precision=highest)


def plain_iterations(param, scale_rows, kernel, own_observed, entries):
    chips, cores = lax.axis_size("chip"), lax.axis_size("core")
    length = param.shape[1]
    misfit = own_observed
    for _ in range(ITERS):
        terms = plain_forward(kernel, scale_rows * jax.nn.softplus(param)).reshape(chips, cores, -1, length)
        partial = lax.psum_scatter(terms, "core", scatter_dimension=1, tiled=False)
        misfit = own_misfit(partial, own_observed)
        residual = lax.all_gather(from_chips(misfit), "core", axis=1, tiled=False)
        back = plain_adjoint(kernel, residual.reshape(-1, length))
        gradient = lax.psum(back, "sens") * scale_rows * jax.nn.sigmoid(param)
        sums = jnp.broadcast_to(jnp.sum(gradient * gradient), (chips * cores, LANES))
        param = moved(param, gradient, exchange_scalars(sums), entries)
    return param, misfit


def iterations(param, scale_rows, kernel, own_observed, entries):
    chips, cores = lax.axis_size("chip"), lax.axis_size("core")
    core = lax.axis_index("core").reshape(1)
    table = table_parts(param.shape[1])
    k2 = relayout(kernel)
    update = None
    misfit = own_observed
    for _ in range(ITERS):
        param, keep, send = forward(k2, param, update, scale_rows, table, core, (chips, cores), entries)
        misfit = own_misfit(keep + swap(send, "core"), own_observed)
        mine = from_chips(misfit)
        back = adjoint(k2, mine, swap(mine, "core"), table, core)
        gradient, sums = gradient_and_square(back, swap(back, "sens"), param, scale_rows, chips * cores)
        update = gradient, exchange_scalars(sums)
    return moved(param, *update, entries), misfit


def local(slip_param, rigidity, kernel, observed):
    own_sources, length = slip_param.shape
    chips, cores, sens = lax.axis_size("chip"), lax.axis_size("core"), lax.axis_size("sens")
    own_count = kernel.shape[1] // (chips * cores)
    src_index = lax.axis_index("chip") * cores + lax.axis_index("core")
    own_observed = lax.dynamic_slice_in_dim(observed, src_index * own_count, own_count, 0)
    entries = own_sources * sens * chips * cores * length
    packed = gather_sens(jnp.concatenate([slip_param, jnp.broadcast_to(rigidity[:, None], (own_sources, LANES))], axis=1))
    param, scale_rows = packed[:, :length], packed[:, length:length + 1]
    fits = (
        sens == 2 and cores == 2 and kernel.shape[2] == HALF and kernel.shape[1] == 2 * LANES
        and length % LANES == 0 and (length // 2) % UNROLL == 0 and own_count % 8 == 0
    )
    run = iterations if fits else plain_iterations
    param, misfit = run(param, scale_rows, kernel, own_observed, entries)
    own_param = lax.dynamic_slice_in_dim(param, lax.axis_index("sens") * own_sources, own_sources, 0)
    return (own_param, misfit)


def solution(mesh):
    sens, src = mesh.shape["sens"], mesh.shape["src"]
    cores = 2 if src % 2 == 0 else 1
    split_mesh = Mesh(mesh.devices.reshape(sens, src // cores, cores), ("sens", "chip", "core"))
    in_specs = (
        P(("chip", "core", "sens"), None),
        P(("chip", "core", "sens")),
        P(None, "sens", ("chip", "core"), None),
        P("sens", None),
    )
    out_specs = (P(("chip", "core", "sens"), None), P(("sens", "chip", "core"), None))
    return jax.shard_map(local, mesh=split_mesh, in_specs=in_specs, out_specs=out_specs, check_vma=False)
```

time: 534 us -> 248 us (0.46)
  waiting for transfers between devices: 194 us -> 36.1 us
  blocking collectives: 196 us -> 72.8 us
  other arithmetic: 107 us -> 5.12 us
  Pallas kernels: 0 us -> 75.7 us
  local copies, waits for them, and re-layouts: 0.22 us -> 41.7 us
  matrix products: 19.1 us -> 0 us
  between operations: 16.4 us -> 1.5 us
  starting transfers between devices: 0.25 us -> 14.3 us
    reduce_scatter x6 -> x0, waiting for transfers between devices: 194 us -> none  [the longest x3 171 us: local(): summed = lax.psum_scatter(terms, 'src', scatter_dimension=0, tiled=True)]
    psum x3 -> x0, blocking collectives: 118 us -> none  [local(): square_sum = lax.psum(jnp.sum(gradient * gradient), ('sens', 'src'))]
    reduce_sum x9 -> x4, other arithmetic: 97.7 us -> 0.65 us  [the longest x1 0.6 us: moved(): square_sum = jnp.sum(sums[:, 0:1], axis=0, keepdims=True)]
    all_gather x6 -> x0, blocking collectives: 77.8 us -> none  [the longest x3 62.1 us: local(): residual = lax.all_gather(misfit, 'src', axis=0, tiled=True)]
    pallas_call x0 -> x10, Pallas kernels: none -> 75.7 us  [the longest x1 29.1 us: relayout(): pl.pallas_call(relayout_body, in_specs=[pl.BlockSpec(memory_space=pl.ANY)...]
    all_to_all x0 -> x7, blocking collectives: none -> 72.8 us  [the longest x5 54 us: to_chips(): return lax.all_to_all(x, 'chip', 0, 0)]
    unnamed x6 -> x16, local copies, waits for them, and re-layouts: 0.02 us -> 40.9 us
    ppermute x0 -> x10, waiting for transfers between devices: none -> 21.5 us  [swap(): return lax.ppermute(x, axis, [(0, 1), (1, 0)])]
  transfers between devices with their start and end apart: 6 -> 12, of which waited for: 6 -> 11; matrix products, arithmetic and copies ran while one was open for 0% -> 0% of each run, Pallas kernels for 0% -> 12%
where the time goes in v2:
time: 248 us; the launch traced here: 247 us
  Pallas kernels  75.7 us (31%)
  blocking collectives  72.8 us (29%)
  local copies, waits for them, and re-layouts  41.7 us (17%)
  waiting for transfers between devices  36.1 us (15%)
  starting transfers between devices  14.3 us (6%)
  other arithmetic  5.12 us (2%)
    all_to_all x5, blocking collectives, to_chips(): return lax.all_to_all(x, 'chip', 0, 0)  54 us
    unnamed x16, local copies, waits for them, and re-layouts  40.9 us
    pallas_call x1, Pallas kernels, relayout(): pl.pallas_call(relayout_body, in_specs=[pl.BlockSpec(memory_space=pl.ANY)...  29.1 us
    ppermute x10, waiting for transfers between devices, swap(): return lax.ppermute(x, axis, [(0, 1), (1, 0)])  21.5 us
    pallas_call x2, Pallas kernels, forward(): pl.pallas_call(functools.partial(forward_next_body, entries), in_specs=[V...  19 us
    all_to_all x2, blocking collectives, exchange_scalars(): return lax.all_to_all(sums, ('chip', 'core'), 0, 0, tiled=True)  18.8 us
    pallas_call x3, Pallas kernels, adjoint(): pl.pallas_call(adjoint_body, in_specs=[VM] * 4 + [SM], out_specs=VM, out_...  17.1 us
    pallas_call x1, Pallas kernels, forward(): pl.pallas_call(forward_first_body, in_specs=[VM] * 4 + [SM], out_specs=[V...  9.42 us
  transfers between devices with their start and end apart: 12, of which 11 were waited for; matrix products, arithmetic and copies ran while one was open for 0% of the time, Pallas kernels for 12%

profile of v2, /device:TPU:0, one launch (start us, length us, event | category | flops | bytes accessed | tf_op | source)
XLA Modules:
  0.0 247.2 jit_solution(18046525934038502182)
XLA Ops:
  2.2 3.0 %collective-permute-start = (f32[32,512]{1,0:T(8,128)S(1)}, f32[32,512]{1,0:T(8,128)S(1)}, u32[]{:S(2)}, u32[]{:S(2)}) collective-permute-start(f32[32,512]{1,0:T(8,128)S(1)} %pad_maximum_fusion), channel_id=1, source_target_pairs={{0,16},{16,0},{1,17},{17,1},{2,18},{18,2},{3,19},{19,3},{4,20},{20... | collective-permute-start | bytes 196616 | tf_op jit(solution)/shard_map/ppermute | solution.py:262
  5.1 29.1 %relayout.1.k_ref = bf16[192,256,256]{2,1,0:T(8,128)(2,1)S(1)} custom-call(bf16[2,256,64,384]{3,2,1,0:T(8,128)(2,1)} %k_hbm.1), custom_call_target="tpu_custom_call" | custom-call | tf_op jit(solution)/shard_map/relayout/pallas_call | solution.py:94
  34.3 8.3 %copy-done = bf16[192,256,256]{2,1,0:T(8,128)(2,1)} copy-done((bf16[192,256,256]{2,1,0:T(8,128)(2,1)}, bf16[192,256,256]{2,1,0:T(8,128)(2,1)S(1)}, u32[]{:S(2)}) %copy-start) | copy-done | bytes 25165848
  42.7 8.1 %copy-done.1 = bf16[192,256,256]{2,1,0:T(8,128)(2,1)S(1)} copy-done((bf16[192,256,256]{2,1,0:T(8,128)(2,1)S(1)}, bf16[192,256,256]{2,1,0:T(8,128)(2,1)}, u32[]{:S(2)}) %copy-start.1) | copy-done | bytes 25165848
  50.8 9.4 %forward_first.1 = (f32[8,16,384]{2,1,0:T(8,128)S(1)}, f32[8,16,384]{2,1,0:T(8,128)S(1)}) custom-call(bf16[192,256,256]{2,1,0:T(8,128)(2,1)S(1)} %copy-done.1, f32[64,384]{1,0:T(8,128)S(1)} %fusion.p_ref, f32[64,1]{1,0:T(8,128)S(1)} %pad_maximum_fusion.1.rig_ref, bf16[2,768,384]{2,1,0:T(8,128)(2,1)S(1)} %copy-done.5, s32[1]{0:T(128)} %bitcast.core_ref), custom_call_target="tpu_custom_call" | custom-call | tf_op jit(solution)/shard_map/forward_first/pallas_call | solution.py:189
  60.3 1.4 collective-permute-done.1
  62.5 5.8 %all-to-all-start = ((f32[8,16,384]{2,1,0:T(8,128)}), f32[8,16,384]{2,1,0:T(8,128)S(1)}, u32[]{:S(2)}, u32[]{:S(2)}) async-start(f32[8,16,384]{2,1,0:T(8,128)} %add.22), calls=%async_computation | async-start | bytes 393216 | tf_op jit(solution)/shard_map/all_to_all | solution.py:274
  68.3 8.3 %all-to-all-done = f32[8,16,384]{2,1,0:T(8,128)S(1)} async-done(((f32[8,16,384]{2,1,0:T(8,128)}), f32[8,16,384]{2,1,0:T(8,128)S(1)}, u32[]{:S(2)}, u32[]{:S(2)}) %all-to-all-start) | async-done | bytes 196640 | tf_op jit(solution)/shard_map/all_to_all | solution.py:274
  77.3 10.7 %all_to_all.64.mine_ref = f32[8,16,384]{2,1,0:T(8,128)S(1)} all-to-all(f32[8,16,384]{2,1,0:T(8,128)S(1)} %broadcast_in_dim.9), channel_id=1, replica_groups=mesh['sens'=2,'chip'=8,'core'=2] {'chip'}, dimensions={0} | all-to-all | bytes 393216 | tf_op jit(solution)/shard_map/all_to_all | solution.py:274
  88.0 1.4 collective-permute-done.2.other_ref
  89.5 8.2 %copy-done.2 = bf16[192,256,256]{2,1,0:T(8,128)(2,1)S(1)} copy-done((bf16[192,256,256]{2,1,0:T(8,128)(2,1)S(1)}, bf16[192,256,256]{2,1,0:T(8,128)(2,1)}, u32[]{:S(2)}) %copy-start.2) | copy-done | bytes 25165848
  97.6 5.7 %adjoint.3.a_ref = f32[64,384]{1,0:T(8,128)S(1)} custom-call(bf16[192,256,256]{2,1,0:T(8,128)(2,1)S(1)} %copy-done.2, f32[8,16,384]{2,1,0:T(8,128)S(1)} %all_to_all.64.mine_ref, f32[8,16,384]{2,1,0:T(8,128)S(1)} %collective-permute-done.2.other_ref, bf16[2,768,384]{2,1,0:T(8,128)(2,1)S(1)} %copy-done.5, s32[1]{0:T(128)} %bitcast.core_ref), custom_call_target="tpu_custom_call" | custom-call | tf_op jit(solution)/shard_map/adjoint/pallas_call | solution.py:234
  104.0 4.3 %collective-permute-done.3.b_ref = f32[64,384]{1,0:T(8,128)S(1)} collective-permute-done((f32[64,384]{1,0:T(8,128)S(1)}, f32[64,384]{1,0:T(8,128)S(1)}, u32[]{:S(2)}, u32[]{:S(2)}) %collective-permute-start.3) | collective-permute-done | bytes 98336 | tf_op jit(solution)/shard_map/ppermute | solution.py:262
  108.4 9.4 %all_to_all.65 = f32[16,1,128]{2,1,0:T(1,128)S(1)} all-to-all(f32[16,1,128]{2,1,0:T(1,128)S(1)} %bitcast.15), channel_id=1, replica_groups=mesh['sens'=2,'chip'=8,'core'=2] {'chip','core'}, dimensions={0} | all-to-all | bytes 16384 | tf_op jit(solution)/shard_map/all_to_all | solution.py:286
  117.8 9.5 %forward_next.2 = (f32[64,384]{1,0:T(8,128)S(1)}, f32[8,16,384]{2,1,0:T(8,128)S(1)}, f32[8,16,384]{2,1,0:T(8,128)S(1)}) custom-call(bf16[192,256,256]{2,1,0:T(8,128)(2,1)S(1)} %copy-done.2, f32[64,384]{1,0:T(8,128)S(1)} %fusion.p_ref, f32[64,384]{1,0:T(8,128)S(1)} %get-tuple-element.18.g_ref, f32[16,128]{1,0:T(8,128)S(1)} %bitcast.13, ...), custom_call_target="tpu_custom_call" | custom-call | tf_op jit(solution)/shard_map/forward_next/pallas_call | solution.py:194
  127.4 1.4 collective-permute-done.4
  128.8 10.9 %all_to_all.66 = f32[8,16,384]{2,1,0:T(8,128)S(1)} all-to-all(f32[8,16,384]{2,1,0:T(8,128)S(1)} %add.25), channel_id=1, replica_groups=mesh['sens'=2,'chip'=8,'core'=2] {'chip'}, dimensions={0} | all-to-all | bytes 393216 | tf_op jit(solution)/shard_map/all_to_all | solution.py:274
  140.6 10.7 %all_to_all.67.mine_ref = f32[8,16,384]{2,1,0:T(8,128)S(1)} all-to-all(f32[8,16,384]{2,1,0:T(8,128)S(1)} %broadcast_in_dim.10), channel_id=1, replica_groups=mesh['sens'=2,'chip'=8,'core'=2] {'chip'}, dimensions={0} | all-to-all | bytes 393216 | tf_op jit(solution)/shard_map/all_to_all | solution.py:274
  151.3 1.4 collective-permute-done.5.other_ref
  152.7 8.2 %copy-done.3 = bf16[192,256,256]{2,1,0:T(8,128)(2,1)S(1)} copy-done((bf16[192,256,256]{2,1,0:T(8,128)(2,1)S(1)}, bf16[192,256,256]{2,1,0:T(8,128)(2,1)}, u32[]{:S(2)}) %copy-start.3) | copy-done | bytes 25165848
  160.9 5.7 %adjoint.4.a_ref = f32[64,384]{1,0:T(8,128)S(1)} custom-call(bf16[192,256,256]{2,1,0:T(8,128)(2,1)S(1)} %copy-done.3, f32[8,16,384]{2,1,0:T(8,128)S(1)} %all_to_all.67.mine_ref, f32[8,16,384]{2,1,0:T(8,128)S(1)} %collective-permute-done.5.other_ref, bf16[2,768,384]{2,1,0:T(8,128)(2,1)S(1)} %copy-done.5, s32[1]{0:T(128)} %bitcast.core_ref), custom_call_target="tpu_custom_call" | custom-call | tf_op jit(solution)/shard_map/adjoint/pallas_call | solution.py:234
  167.2 4.3 %collective-permute-done.6.b_ref = f32[64,384]{1,0:T(8,128)S(1)} collective-permute-done((f32[64,384]{1,0:T(8,128)S(1)}, f32[64,384]{1,0:T(8,128)S(1)}, u32[]{:S(2)}, u32[]{:S(2)}) %collective-permute-start.6) | collective-permute-done | bytes 98336 | tf_op jit(solution)/shard_map/ppermute | solution.py:262
  171.7 9.4 %all_to_all.68 = f32[16,1,128]{2,1,0:T(1,128)S(1)} all-to-all(f32[16,1,128]{2,1,0:T(1,128)S(1)} %bitcast.16), channel_id=1, replica_groups=mesh['sens'=2,'chip'=8,'core'=2] {'chip','core'}, dimensions={0} | all-to-all | bytes 16384 | tf_op jit(solution)/shard_map/all_to_all | solution.py:286
  181.1 9.5 %forward_next.3 = (f32[64,384]{1,0:T(8,128)S(1)}, f32[8,16,384]{2,1,0:T(8,128)S(1)}, f32[8,16,384]{2,1,0:T(8,128)S(1)}) custom-call(bf16[192,256,256]{2,1,0:T(8,128)(2,1)S(1)} %copy-done.3, f32[64,384]{1,0:T(8,128)S(1)} %get-tuple-element.20.p_ref, f32[64,384]{1,0:T(8,128)S(1)} %get-tuple-element.23.g_ref, f32[16,128]{1,0:T(8,128)S(1)} %bitcast.14, ...), custom_call_target="tpu_custom_call" | custom-call | tf_op jit(solution)/shard_map/forward_next/pallas_call | solution.py:194
  192.1 10.9 %all_to_all.69 = f32[8,16,384]{2,1,0:T(8,128)S(1)} all-to-all(f32[8,16,384]{2,1,0:T(8,128)S(1)} %add.26), channel_id=1, replica_groups=mesh['sens'=2,'chip'=8,'core'=2] {'chip'}, dimensions={0} | all-to-all | bytes 393216 | tf_op jit(solution)/shard_map/all_to_all | solution.py:274
  203.8 10.7 %all_to_all.70.mine_ref = f32[8,16,384]{2,1,0:T(8,128)S(1)} all-to-all(f32[8,16,384]{2,1,0:T(8,128)S(1)} %broadcast_in_dim.11), channel_id=1, replica_groups=mesh['sens'=2,'chip'=8,'core'=2] {'chip'}, dimensions={0} | all-to-all | bytes 393216 | tf_op jit(solution)/shard_map/all_to_all | solution.py:274
  214.5 1.4 collective-permute-done.8.other_ref
  216.0 8.2 %copy-done.4 = bf16[192,256,256]{2,1,0:T(8,128)(2,1)S(1)} copy-done((bf16[192,256,256]{2,1,0:T(8,128)(2,1)S(1)}, bf16[192,256,256]{2,1,0:T(8,128)(2,1)}, u32[]{:S(2)}) %copy-start.4) | copy-done | bytes 25165848
  224.1 5.7 %adjoint.5.a_ref = f32[64,384]{1,0:T(8,128)S(1)} custom-call(bf16[192,256,256]{2,1,0:T(8,128)(2,1)S(1)} %copy-done.4, f32[8,16,384]{2,1,0:T(8,128)S(1)} %all_to_all.70.mine_ref, f32[8,16,384]{2,1,0:T(8,128)S(1)} %collective-permute-done.8.other_ref, bf16[2,768,384]{2,1,0:T(8,128)(2,1)S(1)} %copy-done.5, s32[1]{0:T(128)} %bitcast.core_ref), custom_call_target="tpu_custom_call" | custom-call | tf_op jit(solution)/shard_map/adjoint/pallas_call | solution.py:234
  230.4 4.3 %collective-permute-done.9.b_ref = f32[64,384]{1,0:T(8,128)S(1)} collective-permute-done((f32[64,384]{1,0:T(8,128)S(1)}, f32[64,384]{1,0:T(8,128)S(1)}, u32[]{:S(2)}, u32[]{:S(2)}) %collective-permute-start.9) | collective-permute-done | bytes 98336 | tf_op jit(solution)/shard_map/ppermute | solution.py:262
  235.5 3.5 %all-to-all-start.8 = ((f32[16,1,128]{2,1,0:T(1,128)}), f32[16,1,128]{2,1,0:T(1,128)S(1)}, u32[]{:S(2)}, u32[]{:S(2)}) async-start(f32[16,1,128]{2,1,0:T(1,128)} %bitcast.8), calls=%async_computation.8 | async-start | bytes 16384 | tf_op jit(solution)/shard_map/all_to_all | solution.py:286
  239.0 6.3 %all-to-all-done.8 = f32[16,1,128]{2,1,0:T(1,128)S(1)} async-done(((f32[16,1,128]{2,1,0:T(1,128)}), f32[16,1,128]{2,1,0:T(1,128)S(1)}, u32[]{:S(2)}, u32[]{:S(2)}) %all-to-all-start.8) | async-done | bytes 8224 | tf_op jit(solution)/shard_map/all_to_all | solution.py:286
  (44 shorter events, 10.5 us)
Async XLA Ops:
  2.2 40.4 %collective-permute-start = (f32[32,512]{1,0:T(8,128)S(1)}, f32[32,512]{1,0:T(8,128)S(1)}, u32[]{:S(2)}, u32[]{:S(2)}) collective-permute-start(f32[32,512]{1,0:T(8,128)S(1)} %pad_maximum_fusion), channel_id=1, source_target_pairs={{0,16},{16,0},{1,17},{17,1},{2,18},{18,2},{3,19},{19,3},{4,20},{20... | collective-permute-start | bytes 196616 | tf_op jit(solution)/shard_map/ppermute | solution.py:262
  5.1 37.5 %copy-start.6 = (f32[32,384]{1,0:T(8,128)S(1)}, f32[32,384]{1,0:T(8,128)}, u32[]{:S(2)}) copy-start(f32[32,384]{1,0:T(8,128)} %param.5) | copy-start | bytes 147460
  5.1 37.5 %copy-start.5 = (bf16[2,768,384]{2,1,0:T(8,128)(2,1)S(1)}, bf16[2,768,384]{2,1,0:T(8,128)(2,1)}, u32[]{:S(2)}) copy-start(bf16[2,768,384]{2,1,0:T(8,128)(2,1)} %constant.37.clone.t_ref) | copy-start | bytes 3538948
  34.3 8.3 %copy-start = (bf16[192,256,256]{2,1,0:T(8,128)(2,1)}, bf16[192,256,256]{2,1,0:T(8,128)(2,1)S(1)}, u32[]{:S(2)}) copy-start(bf16[192,256,256]{2,1,0:T(8,128)(2,1)S(1)} %relayout.1.k_ref) | copy-start | bytes 75497472
  42.7 8.2 %copy-start.1 = (bf16[192,256,256]{2,1,0:T(8,128)(2,1)S(1)}, bf16[192,256,256]{2,1,0:T(8,128)(2,1)}, u32[]{:S(2)}) copy-start(bf16[192,256,256]{2,1,0:T(8,128)(2,1)} %copy-done) | copy-start | bytes 75497472
  60.2 1.5 collective-permute-start.1
  62.5 14.1 %all-to-all-start = ((f32[8,16,384]{2,1,0:T(8,128)}), f32[8,16,384]{2,1,0:T(8,128)S(1)}, u32[]{:S(2)}, u32[]{:S(2)}) async-start(f32[8,16,384]{2,1,0:T(8,128)} %add.22), calls=%async_computation | async-start | bytes 393216 | tf_op jit(solution)/shard_map/all_to_all | solution.py:274
  88.0 1.4 collective-permute-start.2
  89.5 8.2 %copy-start.2 = (bf16[192,256,256]{2,1,0:T(8,128)(2,1)S(1)}, bf16[192,256,256]{2,1,0:T(8,128)(2,1)}, u32[]{:S(2)}) copy-start(bf16[192,256,256]{2,1,0:T(8,128)(2,1)} %copy-done) | copy-start | bytes 75497472
  103.3 4.9 %collective-permute-start.3 = (f32[64,384]{1,0:T(8,128)S(1)}, f32[64,384]{1,0:T(8,128)S(1)}, u32[]{:S(2)}, u32[]{:S(2)}) collective-permute-start(f32[64,384]{1,0:T(8,128)S(1)} %adjoint.3.a_ref), channel_id=1, source_target_pairs={{0,16},{16,0},{1,17},{17,1},{2,18},{18,2},{3,19},{19,3},{4,20},{20... | collective-permute-start | bytes 294920 | tf_op jit(solution)/shard_map/ppermute | solution.py:262
  127.3 1.5 collective-permute-start.4
  151.3 1.4 collective-permute-start.5
  152.7 8.2 %copy-start.3 = (bf16[192,256,256]{2,1,0:T(8,128)(2,1)S(1)}, bf16[192,256,256]{2,1,0:T(8,128)(2,1)}, u32[]{:S(2)}) copy-start(bf16[192,256,256]{2,1,0:T(8,128)(2,1)} %copy-done) | copy-start | bytes 75497472
  166.6 4.9 %collective-permute-start.6 = (f32[64,384]{1,0:T(8,128)S(1)}, f32[64,384]{1,0:T(8,128)S(1)}, u32[]{:S(2)}, u32[]{:S(2)}) collective-permute-start(f32[64,384]{1,0:T(8,128)S(1)} %adjoint.4.a_ref), channel_id=1, source_target_pairs={{0,16},{16,0},{1,17},{17,1},{2,18},{18,2},{3,19},{19,3},{4,20},{20... | collective-permute-start | bytes 294920 | tf_op jit(solution)/shard_map/ppermute | solution.py:262
  190.6 1.5 collective-permute-start.7
  203.8 43.4 %copy-start.7 = (f32[16,384]{1,0:T(8,128)}, f32[16,384]{1,0:T(8,128)S(1)}, u32[]{:S(2)}) copy-start(f32[16,384]{1,0:T(8,128)S(1)} %dynamic-slice_subtract_fusion.1) | copy-start | bytes 73732
  214.5 1.4 collective-permute-start.8
  216.0 8.2 %copy-start.4 = (bf16[192,256,256]{2,1,0:T(8,128)(2,1)S(1)}, bf16[192,256,256]{2,1,0:T(8,128)(2,1)}, u32[]{:S(2)}) copy-start(bf16[192,256,256]{2,1,0:T(8,128)(2,1)} %copy-done) | copy-start | bytes 75497472
  229.8 4.9 %collective-permute-start.9 = (f32[64,384]{1,0:T(8,128)S(1)}, f32[64,384]{1,0:T(8,128)S(1)}, u32[]{:S(2)}, u32[]{:S(2)}) collective-permute-start(f32[64,384]{1,0:T(8,128)S(1)} %adjoint.5.a_ref), channel_id=1, source_target_pairs={{0,16},{16,0},{1,17},{17,1},{2,18},{18,2},{3,19},{19,3},{4,20},{20... | collective-permute-start | bytes 294920 | tf_op jit(solution)/shard_map/ppermute | solution.py:262
  235.5 9.8 %all-to-all-start.8 = ((f32[16,1,128]{2,1,0:T(1,128)}), f32[16,1,128]{2,1,0:T(1,128)S(1)}, u32[]{:S(2)}, u32[]{:S(2)}) async-start(f32[16,1,128]{2,1,0:T(1,128)} %bitcast.8), calls=%async_computation.8 | async-start | bytes 16384 | tf_op jit(solution)/shard_map/all_to_all | solution.py:286

commit v3 on v2

--- a/solution.py
+++ b/solution.py
@@ -19,7 +19,6 @@
 HALF = LANES // 2
 NN, NT = ((1,), (0,)), ((1,), (1,))
 VM = pl.BlockSpec(memory_space=pltpu.VMEM)
-SM = pl.BlockSpec(memory_space=pltpu.SMEM)
 ROWS = 16
 UNROLL = 24
 
@@ -126,9 +125,9 @@
     lax.fori_loop(0, pairs // UNROLL, step, 0)
 
 
-def forward_core(param, k_ref, rig_ref, t_ref, core_ref, keep_ref, send_ref, lhs, res, terms):
+def forward_core(param, scale_rows, k_ref, t_ref, keep_ref, send_ref, lhs, res, terms):
     freqs, sources = param.shape[1], param.shape[0]
-    slip = rig_ref[...] * jax.nn.softplus(param)
+    slip = scale_rows * jax.nn.softplus(param)
     z = mm3((t_ref[0], t_ref[1]), split(jnp.concatenate([slip, slip], axis=0)), NT)
     low = lax.broadcasted_iota(jnp.int32, (freqs, LANES), 1) < sources
     real, imag = z[:freqs], z[freqs:]
@@ -153,13 +152,20 @@
         halves.append(jnp.concatenate(parts, axis=0) * w)
     spectrum = jnp.concatenate(halves, axis=0).T
     terms[...] = mm3(split(spectrum), (t_ref[0], t_ref[1]), NN).reshape(terms.shape)
-    core = core_ref[0]
+    core = lax.axis_index("core")
     keep_ref[...] = terms[:, core]
     send_ref[...] = terms[:, terms.shape[1] - 1 - core]
 
 
-def forward_first_body(k_ref, p_ref, rig_ref, t_ref, core_ref, keep_ref, send_ref, lhs, res, terms):
-    forward_core(p_ref[...], k_ref, rig_ref, t_ref, core_ref, keep_ref, send_ref, lhs, res, terms)
+def forward_first_body(k_ref, mine_ref, other_ref, t_ref, new_ref, rig_ref, keep_ref, send_ref, lhs, res, terms, both):
+    sens = lax.axis_index("sens")
+    both[sens] = mine_ref[...]
+    both[1 - sens] = other_ref[...]
+    packed = both[...].reshape(-1, both.shape[2])
+    length = new_ref.shape[1]
+    new_ref[...] = packed[:, :length]
+    rig_ref[...] = packed[:, length:]
+    forward_core(packed[:, :length], packed[:, length:length + 1], k_ref, t_ref, keep_ref, send_ref, lhs, res, terms)
 
 
 def moved(param, gradient, sums, entries):
@@ -168,16 +174,14 @@
     return param - step_rate * gradient / root_mean
 
 
-def forward_next_body(entries, k_ref, p_ref, g_ref, q_ref, rig_ref, t_ref, core_ref, new_ref, keep_ref, send_ref, lhs, res, terms):
+def forward_next_body(entries, k_ref, p_ref, g_ref, q_ref, rig_ref, t_ref, new_ref, keep_ref, send_ref, lhs, res, terms):
     param = moved(p_ref[...], g_ref[...], q_ref[...], entries)
     new_ref[...] = param
-    forward_core(param, k_ref, rig_ref, t_ref, core_ref, keep_ref, send_ref, lhs, res, terms)
-
-
-def forward(k2, param, update, scale_rows, table, core, grid_shape, entries):
+    forward_core(param, rig_ref[:, 0:1], k_ref, t_ref, keep_ref, send_ref, lhs, res, terms)
+
+
+def forward_spaces(k2, length, chips, cores):
     pairs, sensors, _ = k2.shape
-    length = param.shape[1]
-    chips, cores = grid_shape
     rows = sensors // (chips * cores)
     outs = [jax.ShapeDtypeStruct((chips, rows, length), f32)] * 2
     scratch = [
@@ -185,22 +189,66 @@
         pltpu.VMEM((2, pairs * 8, LANES), f32),
         pltpu.VMEM((chips, cores, rows, length), f32),
     ]
-    if update is None:
-        keep, send = pl.pallas_call(
-            forward_first_body, in_specs=[VM] * 4 + [SM], out_specs=[VM] * 2, out_shape=outs,
-            scratch_shapes=scratch, compiler_params=params(12), name="forward_first",
-        )(k2, param, scale_rows, table, core)
-        return param, keep, send
-    return pl.pallas_call(
-        functools.partial(forward_next_body, entries), in_specs=[VM] * 6 + [SM], out_specs=[VM] * 3,
+    return outs, scratch
+
+
+def forward_first(k2, mine, other, table, chips, cores):
+    sources, length = 2 * mine.shape[0], table.shape[2]
+    outs, scratch = forward_spaces(k2, length, chips, cores)
+    return pl.pallas_call(
+        forward_first_body, in_specs=[VM] * 4, out_specs=[VM] * 4,
+        out_shape=[jax.ShapeDtypeStruct((sources, length), f32), jax.ShapeDtypeStruct((sources, LANES), f32)] + outs,
+        scratch_shapes=scratch + [pltpu.VMEM((2, *mine.shape), f32)],
+        compiler_params=params(12), name="forward_first",
+    )(k2, mine, other, table)
+
+
+def forward_next(k2, param, gradient, sums, scale_rows, table, chips, cores, entries):
+    outs, scratch = forward_spaces(k2, param.shape[1], chips, cores)
+    return pl.pallas_call(
+        functools.partial(forward_next_body, entries), in_specs=[VM] * 6, out_specs=[VM] * 3,
         out_shape=[jax.ShapeDtypeStruct(param.shape, f32)] + outs,
         scratch_shapes=scratch, compiler_params=params(12), name="forward_next",
-    )(k2, param, *update, scale_rows, table, core)
-
-
-def adjoint_body(k_ref, mine_ref, other_ref, t_ref, core_ref, o_ref, lhs, res, full):
+    )(k2, param, gradient, sums, scale_rows, table)
+
+
+def misfit_body(parts_ref, obs_ref, m_ref, spread_ref):
+    chips, rows, _ = parts_ref.shape
+    first = (lax.axis_index("chip") * lax.axis_size("core") + lax.axis_index("core")) * rows
+    total = parts_ref[0]
+    for c in range(1, chips):
+        total = total + parts_ref[c]
+    misfit = total - obs_ref[pl.ds(pl.multiple_of(first, 8), rows), :]
+    m_ref[...] = misfit
+    for c in range(chips):
+        spread_ref[c] = misfit
+
+
+def misfit_and_spread(parts, observed):
+    return pl.pallas_call(
+        misfit_body, in_specs=[VM] * 2, out_specs=[VM] * 2,
+        out_shape=[jax.ShapeDtypeStruct(parts.shape[1:], f32), jax.ShapeDtypeStruct(parts.shape, f32)],
+        compiler_params=params(4), name="misfit",
+    )(parts, observed)
+
+
+def finish_body(entries, p_ref, g_ref, q_ref, o_ref):
+    rows = o_ref.shape[0]
+    own = pl.ds(pl.multiple_of(lax.axis_index("sens") * rows, 8), rows)
+    o_ref[...] = moved(p_ref[own, :], g_ref[own, :], q_ref[...], entries)
+
+
+def finish(param, gradient, sums, entries):
+    return pl.pallas_call(
+        functools.partial(finish_body, entries), in_specs=[VM] * 3, out_specs=VM,
+        out_shape=jax.ShapeDtypeStruct((param.shape[0] // 2, param.shape[1]), f32),
+        compiler_params=params(4), name="finish",
+    )(param, gradient, sums)
+
+
+def adjoint_body(k_ref, mine_ref, other_ref, t_ref, o_ref, lhs, res, full):
     freqs, sources = t_ref.shape[2], k_ref.shape[2] // 4
-    core = core_ref[0]
+    core = lax.axis_index("core")
     full[:, core] = mine_ref[...]
     full[:, full.shape[1] - 1 - core] = other_ref[...]
     misfit = full[...].reshape(k_ref.shape[1], freqs)
@@ -228,11 +276,11 @@
     )
 
 
-def adjoint(k2, mine, other, table, core):
+def adjoint(k2, mine, other, table):
     pairs, sensors, width = k2.shape
     chips, rows, length = mine.shape
     return pl.pallas_call(
-        adjoint_body, in_specs=[VM] * 4 + [SM], out_specs=VM,
+        adjoint_body, in_specs=[VM] * 4, out_specs=VM,
         out_shape=jax.ShapeDtypeStruct((width // 4, length), f32),
         scratch_shapes=[
             pltpu.VMEM((2, pairs * 8, LANES), f32),
@@ -240,11 +288,11 @@
             pltpu.VMEM((chips, sensors // (chips * rows), rows, length), f32),
         ],
         compiler_params=params(12), name="adjoint",
-    )(k2, mine, other, table, core)
+    )(k2, mine, other, table)
 
 
 def gradient_body(a_ref, b_ref, p_ref, rig_ref, g_ref, q_ref):
-    gradient = (a_ref[...] + b_ref[...]) * rig_ref[...] * jax.nn.sigmoid(p_ref[...])
+    gradient = (a_ref[...] + b_ref[...]) * rig_ref[:, 0:1] * jax.nn.sigmoid(p_ref[...])
     g_ref[...] = gradient
     total = jnp.sum(jnp.sum(gradient * gradient, axis=0, keepdims=True), axis=1, keepdims=True)
     q_ref[...] = jnp.broadcast_to(total, q_ref.shape)
@@ -262,24 +310,8 @@
     return lax.ppermute(x, axis, [(0, 1), (1, 0)])
 
 
-def gather_sens(x):
-    if lax.axis_size("sens") == 2:
-        first = lax.axis_index("sens") == 0
-        other = swap(x, "sens")
-        return jnp.concatenate([jnp.where(first, x, other), jnp.where(first, other, x)], axis=0)
-    return lax.all_gather(x, "sens", axis=0, tiled=True)
-
-
 def to_chips(x):
     return lax.all_to_all(x, "chip", 0, 0)
-
-
-def own_misfit(partial, own_observed):
-    return jnp.sum(to_chips(partial), axis=0) - own_observed
-
-
-def from_chips(misfit):
-    return to_chips(jnp.broadcast_to(misfit[None], (lax.axis_size("chip"), *misfit.shape)))
 
 
 def exchange_scalars(sums):
@@ -310,56 +342,58 @@
     return jnp.dot(jnp.concatenate([back_real, back_imag], axis=1), table, precision=highest)
 
 
-def plain_iterations(param, scale_rows, kernel, own_observed, entries):
+def plain_iterations(slip_param, rigidity, kernel, observed, entries):
     chips, cores = lax.axis_size("chip"), lax.axis_size("core")
-    length = param.shape[1]
+    own_sources, length = slip_param.shape
+    own_count = kernel.shape[1] // (chips * cores)
+    src_index = lax.axis_index("chip") * cores + lax.axis_index("core")
+    own_observed = lax.dynamic_slice_in_dim(observed, src_index * own_count, own_count, 0)
+    param = lax.all_gather(slip_param, "sens", axis=0, tiled=True)
+    scale_rows = lax.all_gather(rigidity[:, None], "sens", axis=0, tiled=True)
     misfit = own_observed
     for _ in range(ITERS):
         terms = plain_forward(kernel, scale_rows * jax.nn.softplus(param)).reshape(chips, cores, -1, length)
         partial = lax.psum_scatter(terms, "core", scatter_dimension=1, tiled=False)
-        misfit = own_misfit(partial, own_observed)
-        residual = lax.all_gather(from_chips(misfit), "core", axis=1, tiled=False)
+        misfit = jnp.sum(to_chips(partial), axis=0) - own_observed
+        spread = to_chips(jnp.broadcast_to(misfit[None], (chips, *misfit.shape)))
+        residual = lax.all_gather(spread, "core", axis=1, tiled=False)
         back = plain_adjoint(kernel, residual.reshape(-1, length))
         gradient = lax.psum(back, "sens") * scale_rows * jax.nn.sigmoid(param)
         sums = jnp.broadcast_to(jnp.sum(gradient * gradient), (chips * cores, LANES))
         param = moved(param, gradient, exchange_scalars(sums), entries)
-    return param, misfit
-
-
-def iterations(param, scale_rows, kernel, own_observed, entries):
+    return lax.dynamic_slice_in_dim(param, lax.axis_index("sens") * own_sources, own_sources, 0), misfit
+
+
+def iterations(slip_param, rigidity, kernel, observed, entries):
     chips, cores = lax.axis_size("chip"), lax.axis_size("core")
-    core = lax.axis_index("core").reshape(1)
-    table = table_parts(param.shape[1])
+    own_sources, length = slip_param.shape
+    table = table_parts(length)
+    mine = jnp.concatenate([slip_param, jnp.broadcast_to(rigidity[:, None], (own_sources, LANES))], axis=1)
+    other = swap(mine, "sens")
     k2 = relayout(kernel)
-    update = None
-    misfit = own_observed
-    for _ in range(ITERS):
-        param, keep, send = forward(k2, param, update, scale_rows, table, core, (chips, cores), entries)
-        misfit = own_misfit(keep + swap(send, "core"), own_observed)
-        mine = from_chips(misfit)
-        back = adjoint(k2, mine, swap(mine, "core"), table, core)
+    param, scale_rows, keep, send = forward_first(k2, mine, other, table, chips, cores)
+    for iteration in range(ITERS):
+        if iteration:
+            param, keep, send = forward_next(k2, param, gradient, sums, scale_rows, table, chips, cores, entries)
+        misfit, spread = misfit_and_spread(to_chips(keep + swap(send, "core")), observed)
+        near = to_chips(spread)
+        back = adjoint(k2, near, swap(near, "core"), table)
         gradient, sums = gradient_and_square(back, swap(back, "sens"), param, scale_rows, chips * cores)
-        update = gradient, exchange_scalars(sums)
-    return moved(param, *update, entries), misfit
+        sums = exchange_scalars(sums)
+    return finish(param, gradient, sums, entries), misfit
 
 
 def local(slip_param, rigidity, kernel, observed):
     own_sources, length = slip_param.shape
     chips, cores, sens = lax.axis_size("chip"), lax.axis_size("core"), lax.axis_size("sens")
     own_count = kernel.shape[1] // (chips * cores)
-    src_index = lax.axis_index("chip") * cores + lax.axis_index("core")
-    own_observed = lax.dynamic_slice_in_dim(observed, src_index * own_count, own_count, 0)
     entries = own_sources * sens * chips * cores * length
-    packed = gather_sens(jnp.concatenate([slip_param, jnp.broadcast_to(rigidity[:, None], (own_sources, LANES))], axis=1))
-    param, scale_rows = packed[:, :length], packed[:, length:length + 1]
     fits = (
         sens == 2 and cores == 2 and kernel.shape[2] == HALF and kernel.shape[1] == 2 * LANES
         and length % LANES == 0 and (length // 2) % UNROLL == 0 and own_count % 8 == 0
     )
     run = iterations if fits else plain_iterations
-    param, misfit = run(param, scale_rows, kernel, own_observed, entries)
-    own_param = lax.dynamic_slice_in_dim(param, lax.axis_index("sens") * own_sources, own_sources, 0)
-    return (own_param, misfit)
+    return run(slip_param, rigidity, kernel, observed, entries)
 
 
 def solution(mesh):

time: 248 us -> 203 us (0.82)
  local copies, waits for them, and re-layouts: 41.7 us -> 0.74 us
  blocking collectives: 72.8 us -> 96.1 us
  waiting for transfers between devices: 36.1 us -> 21.5 us
  starting transfers between devices: 14.3 us -> 4.95 us
  other arithmetic: 5.12 us -> 0.88 us
    unnamed x16 -> x4, local copies, waits for them, and re-layouts: 40.9 us -> 0.01 us
    all_to_all x2 -> x0, waiting for transfers between devices: 14.6 us -> none  [the longest x1 8.26 us: to_chips(): return lax.all_to_all(x, 'chip', 0, 0)]
    all_to_all x5 -> x6, blocking collectives: 54 us -> 67.9 us  [to_chips(): return lax.all_to_all(x, 'chip', 0, 0)]
    all_to_all x2 -> x3, blocking collectives: 18.8 us -> 28.2 us  [exchange_scalars(): return lax.all_to_all(sums, ('chip', 'core'), 0, 0, tiled=True)]
    all_to_all x2 -> x0, starting transfers between devices: 9.29 us -> none  [the longest x1 5.82 us: to_chips(): return lax.all_to_all(x, 'chip', 0, 0)]
    pallas_call x6 -> x10, Pallas kernels: 45.5 us -> 48.4 us  [the longest x2 19.1 us: forward_next(): pl.pallas_call(functools.partial(forward_next_body, entries), in_specs=[V...]
    sub x4 -> x0, other arithmetic: 2.89 us -> none  [the longest x3 2.25 us: own_misfit(): return jnp.sum(to_chips(partial), axis=0) - own_observed]
  transfers between devices with their start and end apart: 12 -> 10, of which waited for: 11 -> 9; matrix products, arithmetic and copies ran while one was open for 0% -> 0% of each run, Pallas kernels for 12% -> 14%
where the time goes in v3:
time: 203 us
  blocking collectives  96.1 us (47%)
  Pallas kernels  77.9 us (38%)
  waiting for transfers between devices  21.5 us (11%)
  starting transfers between devices  4.95 us (2%)
    all_to_all x6, blocking collectives, to_chips(): return lax.all_to_all(x, 'chip', 0, 0)  67.9 us
    pallas_call x1, Pallas kernels, relayout(): pl.pallas_call(relayout_body, in_specs=[pl.BlockSpec(memory_space=pl.ANY)...  29 us
    all_to_all x3, blocking collectives, exchange_scalars(): return lax.all_to_all(sums, ('chip', 'core'), 0, 0, tiled=True)  28.2 us
    ppermute x10, waiting for transfers between devices, swap(): return lax.ppermute(x, axis, [(0, 1), (1, 0)])  21.5 us
    pallas_call x2, Pallas kernels, forward_next(): pl.pallas_call(functools.partial(forward_next_body, entries), in_specs=[V...  19.1 us
    pallas_call x3, Pallas kernels, adjoint(): pl.pallas_call(adjoint_body, in_specs=[VM] * 4, out_specs=VM, out_shape=j...  17.2 us
    pallas_call x1, Pallas kernels, forward_first(): pl.pallas_call(forward_first_body, in_specs=[VM] * 4, out_specs=[VM] * 4,...  9.49 us
    ppermute x10, starting transfers between devices, swap(): return lax.ppermute(x, axis, [(0, 1), (1, 0)])  4.95 us
  transfers between devices with their start and end apart: 10, of which 9 were waited for; matrix products, arithmetic and copies ran while one was open for 0% of the time, Pallas kernels for 14%

profile of v3, /device:TPU:0, one launch (start us, length us, event | category | flops | bytes accessed | tf_op | source)
XLA Modules:
  0.0 202.9 jit_solution(9082993479955615478)
XLA Ops:
  0.6 0.7 broadcast_in_dim.2
  1.4 0.8 pad_maximum_fusion.mine_ref
  2.2 3.0 %collective-permute-start = (f32[32,512]{1,0:T(8,128)S(1)}, f32[32,512]{1,0:T(8,128)S(1)}, u32[]{:S(2)}, u32[]{:S(2)}) collective-permute-start(f32[32,512]{1,0:T(8,128)S(1)} %pad_maximum_fusion.mine_ref), channel_id=1, source_target_pairs={{0,16},{16,0},{1,17},{17,1},{2,18},{18,2},{3,19},{19,3},{4,20},{20... | collective-permute-start | bytes 196616 | tf_op jit(solution)/shard_map/ppermute | solution.py:310
  5.1 29.0 %relayout.1.k_ref = bf16[192,256,256]{2,1,0:T(8,128)(2,1)S(1)} custom-call(bf16[2,256,64,384]{3,2,1,0:T(8,128)(2,1)} %k_hbm.1), custom_call_target="tpu_custom_call" | custom-call | tf_op jit(solution)/shard_map/relayout/pallas_call | solution.py:93
  34.2 9.5 %forward_first.1 = (f32[64,384]{1,0:T(8,128)S(1)}, f32[64,128]{1,0:T(8,128)S(1)}, f32[8,16,384]{2,1,0:T(8,128)S(1)}, f32[8,16,384]{2,1,0:T(8,128)S(1)}) custom-call(bf16[192,256,256]{2,1,0:T(8,128)(2,1)S(1)} %relayout.1.k_ref, f32[32,512]{1,0:T(8,128)S(1)} %pad_maximum_fusion.mine_ref, f32[32,512]{1,0:T(8,128)S(1)} %collective-permute-done.other_ref, ...), custom_call_target="tpu_custom_call" | custom-call | tf_op jit(solution)/shard_map/forward_first/pallas_call | solution.py:198
  43.8 1.4 collective-permute-done.1
  45.2 13.9 %all_to_all.63.parts_ref = f32[8,16,384]{2,1,0:T(8,128)S(1)} all-to-all(f32[8,16,384]{2,1,0:T(8,128)S(1)} %add.9), channel_id=1, replica_groups=mesh['sens'=2,'chip'=8,'core'=2] {'chip'}, dimensions={0} | all-to-all | bytes 393216 | tf_op jit(solution)/shard_map/all_to_all | solution.py:314
  59.1 0.6 misfit.3
  59.8 10.7 %all_to_all.64.mine_ref = f32[8,16,384]{2,1,0:T(8,128)S(1)} all-to-all(f32[8,16,384]{2,1,0:T(8,128)S(1)} %get-tuple-element.25), channel_id=1, replica_groups=mesh['sens'=2,'chip'=8,'core'=2] {'chip'}, dimensions={0} | all-to-all | bytes 393216 | tf_op jit(solution)/shard_map/all_to_all | solution.py:314
  70.5 1.4 collective-permute-done.2.other_ref
  71.9 5.7 %adjoint.3.a_ref = f32[64,384]{1,0:T(8,128)S(1)} custom-call(bf16[192,256,256]{2,1,0:T(8,128)(2,1)S(1)} %relayout.1.k_ref, f32[8,16,384]{2,1,0:T(8,128)S(1)} %all_to_all.64.mine_ref, f32[8,16,384]{2,1,0:T(8,128)S(1)} %collective-permute-done.2.other_ref, bf16[2,768,384]{2,1,0:T(8,128)(2,1)S(1)} %copy-done), custom_call_target="tpu_custom_call" | custom-call | tf_op jit(solution)/shard_map/adjoint/pallas_call | solution.py:282
  78.3 4.3 %collective-permute-done.3.b_ref = f32[64,384]{1,0:T(8,128)S(1)} collective-permute-done((f32[64,384]{1,0:T(8,128)S(1)}, f32[64,384]{1,0:T(8,128)S(1)}, u32[]{:S(2)}, u32[]{:S(2)}) %collective-permute-start.3) | collective-permute-done | bytes 98336 | tf_op jit(solution)/shard_map/ppermute | solution.py:310
  82.7 9.4 %all_to_all.65 = f32[16,1,128]{2,1,0:T(1,128)S(1)} all-to-all(f32[16,1,128]{2,1,0:T(1,128)S(1)} %bitcast.16), channel_id=1, replica_groups=mesh['sens'=2,'chip'=8,'core'=2] {'chip','core'}, dimensions={0} | all-to-all | bytes 16384 | tf_op jit(solution)/shard_map/all_to_all | solution.py:318
  92.1 9.5 %forward_next.2 = (f32[64,384]{1,0:T(8,128)S(1)}, f32[8,16,384]{2,1,0:T(8,128)S(1)}, f32[8,16,384]{2,1,0:T(8,128)S(1)}) custom-call(bf16[192,256,256]{2,1,0:T(8,128)(2,1)S(1)} %relayout.1.k_ref, f32[64,384]{1,0:T(8,128)S(1)} %get-tuple-element.22.p_ref, f32[64,384]{1,0:T(8,128)S(1)} %get-tuple-element.27.g_ref, f32[16,128]{1,0:T(8,128)S(1)} %bitcast.12, ...), custom_call_target="tpu_custom_call" | custom-call | tf_op jit(solution)/shard_map/forward_next/pallas_call | solution.py:208
  101.8 1.4 collective-permute-done.4
  103.2 10.9 %all_to_all.66.parts_ref = f32[8,16,384]{2,1,0:T(8,128)S(1)} all-to-all(f32[8,16,384]{2,1,0:T(8,128)S(1)} %add.10), channel_id=1, replica_groups=mesh['sens'=2,'chip'=8,'core'=2] {'chip'}, dimensions={0} | all-to-all | bytes 393216 | tf_op jit(solution)/shard_map/all_to_all | solution.py:314
  114.2 0.6 misfit.4
  114.8 10.7 %all_to_all.67.mine_ref = f32[8,16,384]{2,1,0:T(8,128)S(1)} all-to-all(f32[8,16,384]{2,1,0:T(8,128)S(1)} %get-tuple-element.32), channel_id=1, replica_groups=mesh['sens'=2,'chip'=8,'core'=2] {'chip'}, dimensions={0} | all-to-all | bytes 393216 | tf_op jit(solution)/shard_map/all_to_all | solution.py:314
  125.5 1.4 collective-permute-done.5.other_ref
  126.9 5.7 %adjoint.4.a_ref = f32[64,384]{1,0:T(8,128)S(1)} custom-call(bf16[192,256,256]{2,1,0:T(8,128)(2,1)S(1)} %relayout.1.k_ref, f32[8,16,384]{2,1,0:T(8,128)S(1)} %all_to_all.67.mine_ref, f32[8,16,384]{2,1,0:T(8,128)S(1)} %collective-permute-done.5.other_ref, bf16[2,768,384]{2,1,0:T(8,128)(2,1)S(1)} %copy-done), custom_call_target="tpu_custom_call" | custom-call | tf_op jit(solution)/shard_map/adjoint/pallas_call | solution.py:282
  133.3 4.3 %collective-permute-done.6.b_ref = f32[64,384]{1,0:T(8,128)S(1)} collective-permute-done((f32[64,384]{1,0:T(8,128)S(1)}, f32[64,384]{1,0:T(8,128)S(1)}, u32[]{:S(2)}, u32[]{:S(2)}) %collective-permute-start.6) | collective-permute-done | bytes 98336 | tf_op jit(solution)/shard_map/ppermute | solution.py:310
  137.7 9.4 %all_to_all.68 = f32[16,1,128]{2,1,0:T(1,128)S(1)} all-to-all(f32[16,1,128]{2,1,0:T(1,128)S(1)} %bitcast.17), channel_id=1, replica_groups=mesh['sens'=2,'chip'=8,'core'=2] {'chip','core'}, dimensions={0} | all-to-all | bytes 16384 | tf_op jit(solution)/shard_map/all_to_all | solution.py:318
  147.1 9.5 %forward_next.3 = (f32[64,384]{1,0:T(8,128)S(1)}, f32[8,16,384]{2,1,0:T(8,128)S(1)}, f32[8,16,384]{2,1,0:T(8,128)S(1)}) custom-call(bf16[192,256,256]{2,1,0:T(8,128)(2,1)S(1)} %relayout.1.k_ref, f32[64,384]{1,0:T(8,128)S(1)} %get-tuple-element.29.p_ref, f32[64,384]{1,0:T(8,128)S(1)} %get-tuple-element.33.g_ref, f32[16,128]{1,0:T(8,128)S(1)} %bitcast.13, ...), custom_call_target="tpu_custom_call" | custom-call | tf_op jit(solution)/shard_map/forward_next/pallas_call | solution.py:208
  156.8 1.4 collective-permute-done.7
  158.2 10.9 %all_to_all.69.parts_ref = f32[8,16,384]{2,1,0:T(8,128)S(1)} all-to-all(f32[8,16,384]{2,1,0:T(8,128)S(1)} %add.11), channel_id=1, replica_groups=mesh['sens'=2,'chip'=8,'core'=2] {'chip'}, dimensions={0} | all-to-all | bytes 393216 | tf_op jit(solution)/shard_map/all_to_all | solution.py:314
  169.2 0.6 misfit.5
  169.8 10.7 %all_to_all.70.mine_ref = f32[8,16,384]{2,1,0:T(8,128)S(1)} all-to-all(f32[8,16,384]{2,1,0:T(8,128)S(1)} %get-tuple-element.38), channel_id=1, replica_groups=mesh['sens'=2,'chip'=8,'core'=2] {'chip'}, dimensions={0} | all-to-all | bytes 393216 | tf_op jit(solution)/shard_map/all_to_all | solution.py:314
  180.5 1.4 collective-permute-done.8.other_ref
  181.9 5.7 %adjoint.5.a_ref = f32[64,384]{1,0:T(8,128)S(1)} custom-call(bf16[192,256,256]{2,1,0:T(8,128)(2,1)S(1)} %relayout.1.k_ref, f32[8,16,384]{2,1,0:T(8,128)S(1)} %all_to_all.70.mine_ref, f32[8,16,384]{2,1,0:T(8,128)S(1)} %collective-permute-done.8.other_ref, bf16[2,768,384]{2,1,0:T(8,128)(2,1)S(1)} %copy-done), custom_call_target="tpu_custom_call" | custom-call | tf_op jit(solution)/shard_map/adjoint/pallas_call | solution.py:282
  188.3 4.3 %collective-permute-done.9.b_ref = f32[64,384]{1,0:T(8,128)S(1)} collective-permute-done((f32[64,384]{1,0:T(8,128)S(1)}, f32[64,384]{1,0:T(8,128)S(1)}, u32[]{:S(2)}, u32[]{:S(2)}) %collective-permute-start.9) | collective-permute-done | bytes 98336 | tf_op jit(solution)/shard_map/ppermute | solution.py:310
  192.7 9.4 %all_to_all.71 = f32[16,1,128]{2,1,0:T(1,128)S(1)} all-to-all(f32[16,1,128]{2,1,0:T(1,128)S(1)} %bitcast.15), channel_id=1, replica_groups=mesh['sens'=2,'chip'=8,'core'=2] {'chip','core'}, dimensions={0} | all-to-all | bytes 16384 | tf_op jit(solution)/shard_map/all_to_all | solution.py:318
  202.1 0.7 finish.1
  (20 shorter events, 2.6 us)
Async XLA Ops:
  2.2 32.0 %copy-start = (bf16[2,768,384]{2,1,0:T(8,128)(2,1)S(1)}, bf16[2,768,384]{2,1,0:T(8,128)(2,1)}, u32[]{:S(2)}) copy-start(bf16[2,768,384]{2,1,0:T(8,128)(2,1)} %constant.2.clone.t_ref) | copy-start | bytes 3538948
  2.2 32.0 %collective-permute-start = (f32[32,512]{1,0:T(8,128)S(1)}, f32[32,512]{1,0:T(8,128)S(1)}, u32[]{:S(2)}, u32[]{:S(2)}) collective-permute-start(f32[32,512]{1,0:T(8,128)S(1)} %pad_maximum_fusion.mine_ref), channel_id=1, source_target_pairs={{0,16},{16,0},{1,17},{17,1},{2,18},{18,2},{3,19},{19,3},{4,20},{20... | collective-permute-start | bytes 196616 | tf_op jit(solution)/shard_map/ppermute | solution.py:310
  34.2 25.0 %copy-start.1 = (f32[256,384]{1,0:T(8,128)S(1)}, f32[256,384]{1,0:T(8,128)}, u32[]{:S(2)}) copy-start(f32[256,384]{1,0:T(8,128)} %obs_ref.5) | copy-start | bytes 1179652
  43.7 1.5 collective-permute-start.1
  70.5 1.4 collective-permute-start.2
  77.7 4.9 %collective-permute-start.3 = (f32[64,384]{1,0:T(8,128)S(1)}, f32[64,384]{1,0:T(8,128)S(1)}, u32[]{:S(2)}, u32[]{:S(2)}) collective-permute-start(f32[64,384]{1,0:T(8,128)S(1)} %adjoint.3.a_ref), channel_id=1, source_target_pairs={{0,16},{16,0},{1,17},{17,1},{2,18},{18,2},{3,19},{19,3},{4,20},{20... | collective-permute-start | bytes 294920 | tf_op jit(solution)/shard_map/ppermute | solution.py:310
  101.7 1.5 collective-permute-start.4
  125.5 1.4 collective-permute-start.5
  132.7 4.9 %collective-permute-start.6 = (f32[64,384]{1,0:T(8,128)S(1)}, f32[64,384]{1,0:T(8,128)S(1)}, u32[]{:S(2)}, u32[]{:S(2)}) collective-permute-start(f32[64,384]{1,0:T(8,128)S(1)} %adjoint.4.a_ref), channel_id=1, source_target_pairs={{0,16},{16,0},{1,17},{17,1},{2,18},{18,2},{3,19},{19,3},{4,20},{20... | collective-permute-start | bytes 294920 | tf_op jit(solution)/shard_map/ppermute | solution.py:310
  156.7 1.5 collective-permute-start.7
  180.5 1.4 collective-permute-start.8
  187.7 4.9 %collective-permute-start.9 = (f32[64,384]{1,0:T(8,128)S(1)}, f32[64,384]{1,0:T(8,128)S(1)}, u32[]{:S(2)}, u32[]{:S(2)}) collective-permute-start(f32[64,384]{1,0:T(8,128)S(1)} %adjoint.5.a_ref), channel_id=1, source_target_pairs={{0,16},{16,0},{1,17},{17,1},{2,18},{18,2},{3,19},{19,3},{4,20},{20... | collective-permute-start | bytes 294920 | tf_op jit(solution)/shard_map/ppermute | solution.py:310

commit v4 on v3

--- a/solution.py
+++ b/solution.py
@@ -20,7 +20,9 @@
 NN, NT = ((1,), (0,)), ((1,), (1,))
 VM = pl.BlockSpec(memory_space=pltpu.VMEM)
 ROWS = 16
-UNROLL = 24
+PITCH = 24
+BUFFERS = 3
+UNROLL = 96
 
 
 def table_parts(length):
@@ -56,33 +58,34 @@
 def relayout_body(k_hbm, out_ref, buf, stage, sem):
     freqs = k_hbm.shape[3]
     steps = k_hbm.shape[1] // ROWS
-    same = lax.broadcasted_iota(jnp.int32, (LANES, LANES), 0) == lax.broadcasted_iota(jnp.int32, (LANES, LANES), 1)
-    eye = same.astype(f32).astype(bf16)
-
-    def copy(i, slot):
+
+    def copy(i):
+        slot = lax.rem(i, BUFFERS)
         return pltpu.make_async_copy(k_hbm.at[:, pl.ds(i * ROWS, ROWS)], buf.at[slot], sem.at[slot])
 
-    copy(0, 0).start()
+    for i in range(BUFFERS - 1):
+        copy(i).start()
 
     def step(i, carry):
-        slot = lax.rem(i, 2)
-        copy(i, slot).wait()
-
-        @pl.when(i + 1 < steps)
+        slot = lax.rem(i, BUFFERS)
+        copy(i).wait()
+
+        @pl.when(i + BUFFERS - 1 < steps)
         def _():
-            copy(i + 1, 1 - slot).start()
+            copy(i + BUFFERS - 1).start()
 
         for r in range(0, ROWS, 2):
             x = jnp.concatenate([buf[slot, c, r + j] for j in range(2) for c in range(2)], axis=0)
             for chunk in range(freqs // LANES):
-                o = mm(eye, x[:, chunk * LANES:(chunk + 1) * LANES], NT)
+                o = x[:, chunk * LANES:(chunk + 1) * LANES].T.astype(f32)
                 for j in range(2):
                     for h in range(2):
-                        rows = pl.ds(chunk * HALF * ROWS + r + j, HALF, stride=ROWS)
+                        rows = pl.ds(chunk * HALF * PITCH + r + j, HALF, stride=PITCH)
                         stage[h, rows, :] = o[h * HALF:(h + 1) * HALF, j * LANES:(j + 1) * LANES]
         rows = pl.ds(pl.multiple_of(i * ROWS, ROWS), ROWS)
         for h in range(2):
-            out_ref[:, rows, h * LANES:(h + 1) * LANES] = stage[h].reshape(freqs // 2, ROWS, LANES).astype(bf16)
+            block = stage[h].reshape(freqs // 2, PITCH, LANES)[:, :ROWS]
+            out_ref[:, rows, h * LANES:(h + 1) * LANES] = block.astype(bf16)
         return carry
 
     lax.fori_loop(0, steps, step, 0)
@@ -96,13 +99,30 @@
         out_specs=VM,
         out_shape=pltpu.VMEM((freqs // 2, sensors, 4 * sources), bf16),
         scratch_shapes=[
-            pltpu.VMEM((2, 2, ROWS, sources, freqs), bf16),
-            pltpu.VMEM((2, freqs // 2 * ROWS, LANES), f32),
-            pltpu.SemaphoreType.DMA((2,)),
+            pltpu.VMEM((BUFFERS, 2, ROWS, sources, freqs), bf16),
+            pltpu.VMEM((2, freqs // 2 * PITCH, LANES), f32),
+            pltpu.SemaphoreType.DMA((BUFFERS,)),
         ],
-        compiler_params=params(10),
+        compiler_params=params(12),
         name="relayout",
     )(kernel)
+
+
+def pack_body(p_ref, rig_ref, o_ref):
+    rows, length = p_ref.shape
+    o_ref[:, :length] = p_ref[...]
+    same = lax.broadcasted_iota(jnp.int32, (rows, rows), 0) == lax.broadcasted_iota(jnp.int32, (rows, rows), 1)
+    column = jnp.sum(jnp.where(same, jnp.broadcast_to(rig_ref[...], (rows, rows)), 0.0), axis=1, keepdims=True)
+    o_ref[:, length:] = jnp.broadcast_to(column, (rows, LANES))
+
+
+def pack(slip_param, rigidity):
+    rows, length = slip_param.shape
+    return pl.pallas_call(
+        pack_body, in_specs=[VM] * 2, out_specs=VM,
+        out_shape=jax.ShapeDtypeStruct((rows, length + LANES), f32),
+        compiler_params=params(4), name="pack",
+    )(slip_param, rigidity.reshape(1, rows))
 
 
 def pair_row(chunk, h, m):
@@ -366,9 +386,8 @@
 
 def iterations(slip_param, rigidity, kernel, observed, entries):
     chips, cores = lax.axis_size("chip"), lax.axis_size("core")
-    own_sources, length = slip_param.shape
-    table = table_parts(length)
-    mine = jnp.concatenate([slip_param, jnp.broadcast_to(rigidity[:, None], (own_sources, LANES))], axis=1)
+    table = table_parts(slip_param.shape[1])
+    mine = pack(slip_param, rigidity)
     other = swap(mine, "sens")
     k2 = relayout(kernel)
     param, scale_rows, keep, send = forward_first(k2, mine, other, table, chips, cores)

time: 203 us -> 188 us (0.926)
  Pallas kernels: 77.9 us -> 62.2 us
    pallas_call x1, Pallas kernels: 29 us -> 17.5 us  [relayout(): pl.pallas_call(relayout_body, in_specs=[pl.BlockSpec(memory_space=pl.ANY)...]
    pallas_call x3, Pallas kernels: 17.2 us -> 15.1 us  [adjoint(): pl.pallas_call(adjoint_body, in_specs=[VM] * 4, out_specs=VM, out_shape=j...]
  transfers between devices with their start and end apart: 10 -> 10, of which waited for: 9 -> 9; matrix products, arithmetic and copies ran while one was open for 0% -> 0% of each run, Pallas kernels for 14% -> 9%
where the time goes in v4:
time: 188 us; the launch traced here: 187 us
  blocking collectives  96.1 us (51%)
  Pallas kernels  62.2 us (33%)
  waiting for transfers between devices  21.5 us (11%)
  starting transfers between devices  4.98 us (3%)
    all_to_all x6, blocking collectives, to_chips(): return lax.all_to_all(x, 'chip', 0, 0)  67.9 us
    all_to_all x3, blocking collectives, exchange_scalars(): return lax.all_to_all(sums, ('chip', 'core'), 0, 0, tiled=True)  28.2 us
    ppermute x10, waiting for transfers between devices, swap(): return lax.ppermute(x, axis, [(0, 1), (1, 0)])  21.5 us
    pallas_call x2, Pallas kernels, forward_next(): pl.pallas_call(functools.partial(forward_next_body, entries), in_specs=[V...  17.7 us
    pallas_call x1, Pallas kernels, relayout(): pl.pallas_call(relayout_body, in_specs=[pl.BlockSpec(memory_space=pl.ANY)...  17.5 us
    pallas_call x3, Pallas kernels, adjoint(): pl.pallas_call(adjoint_body, in_specs=[VM] * 4, out_specs=VM, out_shape=j...  15.1 us
    pallas_call x1, Pallas kernels, forward_first(): pl.pallas_call(forward_first_body, in_specs=[VM] * 4, out_specs=[VM] * 4,...  8.8 us
    ppermute x10, starting transfers between devices, swap(): return lax.ppermute(x, axis, [(0, 1), (1, 0)])  4.98 us
  transfers between devices with their start and end apart: 10, of which 9 were waited for; matrix products, arithmetic and copies ran while one was open for 0% of the time, Pallas kernels for 9%

profile of v4, /device:TPU:0, one launch (start us, length us, event | category | flops | bytes accessed | tf_op | source)
XLA Modules:
  0.0 187.1 jit_solution(9226732708487110095)
XLA Ops:
  0.6 0.8 copy-done.2
  1.4 0.7 copy-done.3
  2.2 3.0 %collective-permute-start = (f32[32,512]{1,0:T(8,128)S(1)}, f32[32,512]{1,0:T(8,128)S(1)}, u32[]{:S(2)}, u32[]{:S(2)}) collective-permute-start(f32[32,512]{1,0:T(8,128)S(1)} %pack.1.mine_ref), channel_id=1, source_target_pairs={{0,16},{16,0},{1,17},{17,1},{2,18},{18,2},{3,19},{19,3},{4,20},{20... | collective-permute-start | bytes 196616 | tf_op jit(solution)/shard_map/ppermute | solution.py:330
  5.1 17.5 %relayout.1.k_ref = bf16[192,256,256]{2,1,0:T(8,128)(2,1)S(1)} custom-call(bf16[2,256,64,384]{3,2,1,0:T(8,128)(2,1)} %k_hbm.1), custom_call_target="tpu_custom_call" | custom-call | tf_op jit(solution)/shard_map/relayout/pallas_call | solution.py:96
  22.7 8.8 %forward_first.1 = (f32[64,384]{1,0:T(8,128)S(1)}, f32[64,128]{1,0:T(8,128)S(1)}, f32[8,16,384]{2,1,0:T(8,128)S(1)}, f32[8,16,384]{2,1,0:T(8,128)S(1)}) custom-call(bf16[192,256,256]{2,1,0:T(8,128)(2,1)S(1)} %relayout.1.k_ref, f32[32,512]{1,0:T(8,128)S(1)} %pack.1.mine_ref, f32[32,512]{1,0:T(8,128)S(1)} %collective-permute-done.other_ref, ...), custom_call_target="tpu_custom_call" | custom-call | tf_op jit(solution)/shard_map/forward_first/pallas_call | solution.py:218
  31.5 1.4 collective-permute-done.1
  33.0 13.9 %all_to_all.63.parts_ref = f32[8,16,384]{2,1,0:T(8,128)S(1)} all-to-all(f32[8,16,384]{2,1,0:T(8,128)S(1)} %add.9), channel_id=1, replica_groups=mesh['sens'=2,'chip'=8,'core'=2] {'chip'}, dimensions={0} | all-to-all | bytes 393216 | tf_op jit(solution)/shard_map/all_to_all | solution.py:334
  46.9 0.6 misfit.3
  47.5 10.7 %all_to_all.64.mine_ref = f32[8,16,384]{2,1,0:T(8,128)S(1)} all-to-all(f32[8,16,384]{2,1,0:T(8,128)S(1)} %get-tuple-element.25), channel_id=1, replica_groups=mesh['sens'=2,'chip'=8,'core'=2] {'chip'}, dimensions={0} | all-to-all | bytes 393216 | tf_op jit(solution)/shard_map/all_to_all | solution.py:334
  58.2 1.4 collective-permute-done.2.other_ref
  59.7 5.0 %adjoint.3.a_ref = f32[64,384]{1,0:T(8,128)S(1)} custom-call(bf16[192,256,256]{2,1,0:T(8,128)(2,1)S(1)} %relayout.1.k_ref, f32[8,16,384]{2,1,0:T(8,128)S(1)} %all_to_all.64.mine_ref, f32[8,16,384]{2,1,0:T(8,128)S(1)} %collective-permute-done.2.other_ref, bf16[2,768,384]{2,1,0:T(8,128)(2,1)S(1)} %copy-done), custom_call_target="tpu_custom_call" | custom-call | tf_op jit(solution)/shard_map/adjoint/pallas_call | solution.py:302
  65.3 4.3 %collective-permute-done.3.b_ref = f32[64,384]{1,0:T(8,128)S(1)} collective-permute-done((f32[64,384]{1,0:T(8,128)S(1)}, f32[64,384]{1,0:T(8,128)S(1)}, u32[]{:S(2)}, u32[]{:S(2)}) %collective-permute-start.3) | collective-permute-done | bytes 98336 | tf_op jit(solution)/shard_map/ppermute | solution.py:330
  69.8 9.4 %all_to_all.65 = f32[16,1,128]{2,1,0:T(1,128)S(1)} all-to-all(f32[16,1,128]{2,1,0:T(1,128)S(1)} %bitcast.17), channel_id=1, replica_groups=mesh['sens'=2,'chip'=8,'core'=2] {'chip','core'}, dimensions={0} | all-to-all | bytes 16384 | tf_op jit(solution)/shard_map/all_to_all | solution.py:338
  79.2 8.9 %forward_next.2 = (f32[64,384]{1,0:T(8,128)S(1)}, f32[8,16,384]{2,1,0:T(8,128)S(1)}, f32[8,16,384]{2,1,0:T(8,128)S(1)}) custom-call(bf16[192,256,256]{2,1,0:T(8,128)(2,1)S(1)} %relayout.1.k_ref, f32[64,384]{1,0:T(8,128)S(1)} %get-tuple-element.22.p_ref, f32[64,384]{1,0:T(8,128)S(1)} %get-tuple-element.27.g_ref, f32[16,128]{1,0:T(8,128)S(1)} %bitcast.13, ...), custom_call_target="tpu_custom_call" | custom-call | tf_op jit(solution)/shard_map/forward_next/pallas_call | solution.py:228
  88.1 1.4 collective-permute-done.4
  89.6 10.9 %all_to_all.66.parts_ref = f32[8,16,384]{2,1,0:T(8,128)S(1)} all-to-all(f32[8,16,384]{2,1,0:T(8,128)S(1)} %add.10), channel_id=1, replica_groups=mesh['sens'=2,'chip'=8,'core'=2] {'chip'}, dimensions={0} | all-to-all | bytes 393216 | tf_op jit(solution)/shard_map/all_to_all | solution.py:334
  100.5 0.6 misfit.4
  101.1 10.7 %all_to_all.67.mine_ref = f32[8,16,384]{2,1,0:T(8,128)S(1)} all-to-all(f32[8,16,384]{2,1,0:T(8,128)S(1)} %get-tuple-element.32), channel_id=1, replica_groups=mesh['sens'=2,'chip'=8,'core'=2] {'chip'}, dimensions={0} | all-to-all | bytes 393216 | tf_op jit(solution)/shard_map/all_to_all | solution.py:334
  111.8 1.4 collective-permute-done.5.other_ref
  113.3 5.0 %adjoint.4.a_ref = f32[64,384]{1,0:T(8,128)S(1)} custom-call(bf16[192,256,256]{2,1,0:T(8,128)(2,1)S(1)} %relayout.1.k_ref, f32[8,16,384]{2,1,0:T(8,128)S(1)} %all_to_all.67.mine_ref, f32[8,16,384]{2,1,0:T(8,128)S(1)} %collective-permute-done.5.other_ref, bf16[2,768,384]{2,1,0:T(8,128)(2,1)S(1)} %copy-done), custom_call_target="tpu_custom_call" | custom-call | tf_op jit(solution)/shard_map/adjoint/pallas_call | solution.py:302
  118.9 4.3 %collective-permute-done.6.b_ref = f32[64,384]{1,0:T(8,128)S(1)} collective-permute-done((f32[64,384]{1,0:T(8,128)S(1)}, f32[64,384]{1,0:T(8,128)S(1)}, u32[]{:S(2)}, u32[]{:S(2)}) %collective-permute-start.6) | collective-permute-done | bytes 98336 | tf_op jit(solution)/shard_map/ppermute | solution.py:330
  123.4 9.4 %all_to_all.68 = f32[16,1,128]{2,1,0:T(1,128)S(1)} all-to-all(f32[16,1,128]{2,1,0:T(1,128)S(1)} %bitcast.18), channel_id=1, replica_groups=mesh['sens'=2,'chip'=8,'core'=2] {'chip','core'}, dimensions={0} | all-to-all | bytes 16384 | tf_op jit(solution)/shard_map/all_to_all | solution.py:338
  132.8 8.8 %forward_next.3 = (f32[64,384]{1,0:T(8,128)S(1)}, f32[8,16,384]{2,1,0:T(8,128)S(1)}, f32[8,16,384]{2,1,0:T(8,128)S(1)}) custom-call(bf16[192,256,256]{2,1,0:T(8,128)(2,1)S(1)} %relayout.1.k_ref, f32[64,384]{1,0:T(8,128)S(1)} %get-tuple-element.29.p_ref, f32[64,384]{1,0:T(8,128)S(1)} %get-tuple-element.33.g_ref, f32[16,128]{1,0:T(8,128)S(1)} %bitcast.14, ...), custom_call_target="tpu_custom_call" | custom-call | tf_op jit(solution)/shard_map/forward_next/pallas_call | solution.py:228
  141.7 1.4 collective-permute-done.7
  143.2 10.9 %all_to_all.69.parts_ref = f32[8,16,384]{2,1,0:T(8,128)S(1)} all-to-all(f32[8,16,384]{2,1,0:T(8,128)S(1)} %add.11), channel_id=1, replica_groups=mesh['sens'=2,'chip'=8,'core'=2] {'chip'}, dimensions={0} | all-to-all | bytes 393216 | tf_op jit(solution)/shard_map/all_to_all | solution.py:334
  154.1 0.6 misfit.5
  154.8 10.7 %all_to_all.70.mine_ref = f32[8,16,384]{2,1,0:T(8,128)S(1)} all-to-all(f32[8,16,384]{2,1,0:T(8,128)S(1)} %get-tuple-element.38), channel_id=1, replica_groups=mesh['sens'=2,'chip'=8,'core'=2] {'chip'}, dimensions={0} | all-to-all | bytes 393216 | tf_op jit(solution)/shard_map/all_to_all | solution.py:334
  165.5 1.4 collective-permute-done.8.other_ref
  166.9 5.0 %adjoint.5.a_ref = f32[64,384]{1,0:T(8,128)S(1)} custom-call(bf16[192,256,256]{2,1,0:T(8,128)(2,1)S(1)} %relayout.1.k_ref, f32[8,16,384]{2,1,0:T(8,128)S(1)} %all_to_all.70.mine_ref, f32[8,16,384]{2,1,0:T(8,128)S(1)} %collective-permute-done.8.other_ref, bf16[2,768,384]{2,1,0:T(8,128)(2,1)S(1)} %copy-done), custom_call_target="tpu_custom_call" | custom-call | tf_op jit(solution)/shard_map/adjoint/pallas_call | solution.py:302
  172.5 4.3 %collective-permute-done.9.b_ref = f32[64,384]{1,0:T(8,128)S(1)} collective-permute-done((f32[64,384]{1,0:T(8,128)S(1)}, f32[64,384]{1,0:T(8,128)S(1)}, u32[]{:S(2)}, u32[]{:S(2)}) %collective-permute-start.9) | collective-permute-done | bytes 98336 | tf_op jit(solution)/shard_map/ppermute | solution.py:330
  177.0 9.4 %all_to_all.71 = f32[16,1,128]{2,1,0:T(1,128)S(1)} all-to-all(f32[16,1,128]{2,1,0:T(1,128)S(1)} %bitcast.16), channel_id=1, replica_groups=mesh['sens'=2,'chip'=8,'core'=2] {'chip','core'}, dimensions={0} | all-to-all | bytes 16384 | tf_op jit(solution)/shard_map/all_to_all | solution.py:338
  186.4 0.7 finish.1
  (23 shorter events, 2.7 us)
Async XLA Ops:
  0.6 0.8 copy-start.2
  1.4 0.7 copy-start.3
  2.2 20.5 %copy-start = (bf16[2,768,384]{2,1,0:T(8,128)(2,1)S(1)}, bf16[2,768,384]{2,1,0:T(8,128)(2,1)}, u32[]{:S(2)}) copy-start(bf16[2,768,384]{2,1,0:T(8,128)(2,1)} %constant.2.clone.t_ref) | copy-start | bytes 3538948
  2.2 20.5 %collective-permute-start = (f32[32,512]{1,0:T(8,128)S(1)}, f32[32,512]{1,0:T(8,128)S(1)}, u32[]{:S(2)}, u32[]{:S(2)}) collective-permute-start(f32[32,512]{1,0:T(8,128)S(1)} %pack.1.mine_ref), channel_id=1, source_target_pairs={{0,16},{16,0},{1,17},{17,1},{2,18},{18,2},{3,19},{19,3},{4,20},{20... | collective-permute-start | bytes 196616 | tf_op jit(solution)/shard_map/ppermute | solution.py:330
  22.6 24.3 %copy-start.1 = (f32[256,384]{1,0:T(8,128)S(1)}, f32[256,384]{1,0:T(8,128)}, u32[]{:S(2)}) copy-start(f32[256,384]{1,0:T(8,128)} %obs_ref.5) | copy-start | bytes 1179652
  31.5 1.5 collective-permute-start.1
  58.2 1.4 collective-permute-start.2
  64.7 4.9 %collective-permute-start.3 = (f32[64,384]{1,0:T(8,128)S(1)}, f32[64,384]{1,0:T(8,128)S(1)}, u32[]{:S(2)}, u32[]{:S(2)}) collective-permute-start(f32[64,384]{1,0:T(8,128)S(1)} %adjoint.3.a_ref), channel_id=1, source_target_pairs={{0,16},{16,0},{1,17},{17,1},{2,18},{18,2},{3,19},{19,3},{4,20},{20... | collective-permute-start | bytes 294920 | tf_op jit(solution)/shard_map/ppermute | solution.py:330
  88.0 1.5 collective-permute-start.4
  111.8 1.4 collective-permute-start.5
  118.3 4.9 %collective-permute-start.6 = (f32[64,384]{1,0:T(8,128)S(1)}, f32[64,384]{1,0:T(8,128)S(1)}, u32[]{:S(2)}, u32[]{:S(2)}) collective-permute-start(f32[64,384]{1,0:T(8,128)S(1)} %adjoint.4.a_ref), channel_id=1, source_target_pairs={{0,16},{16,0},{1,17},{17,1},{2,18},{18,2},{3,19},{19,3},{4,20},{20... | collective-permute-start | bytes 294920 | tf_op jit(solution)/shard_map/ppermute | solution.py:330
  141.7 1.5 collective-permute-start.7
  165.5 1.4 collective-permute-start.8
  171.9 4.9 %collective-permute-start.9 = (f32[64,384]{1,0:T(8,128)S(1)}, f32[64,384]{1,0:T(8,128)S(1)}, u32[]{:S(2)}, u32[]{:S(2)}) collective-permute-start(f32[64,384]{1,0:T(8,128)S(1)} %adjoint.5.a_ref), channel_id=1, source_target_pairs={{0,16},{16,0},{1,17},{17,1},{2,18},{18,2},{3,19},{19,3},{4,20},{20... | collective-permute-start | bytes 294920 | tf_op jit(solution)/shard_map/ppermute | solution.py:330

commit v5 on v4

--- a/solution.py
+++ b/solution.py
@@ -20,8 +20,8 @@
 NN, NT = ((1,), (0,)), ((1,), (1,))
 VM = pl.BlockSpec(memory_space=pltpu.VMEM)
 ROWS = 16
-PITCH = 24
-BUFFERS = 3
+PITCH = 196
+BUFFERS = 6
 UNROLL = 96
 
 
@@ -57,35 +57,45 @@
 
 def relayout_body(k_hbm, out_ref, buf, stage, sem):
     freqs = k_hbm.shape[3]
+    pairs = freqs // 2
     steps = k_hbm.shape[1] // ROWS
-
-    def copy(i):
+    same = lax.broadcasted_iota(jnp.int32, (LANES, LANES), 0) == lax.broadcasted_iota(jnp.int32, (LANES, LANES), 1)
+    eye = same.astype(f32).astype(bf16)
+
+    def copies(i):
         slot = lax.rem(i, BUFFERS)
-        return pltpu.make_async_copy(k_hbm.at[:, pl.ds(i * ROWS, ROWS)], buf.at[slot], sem.at[slot])
+        rows = pl.ds(i * ROWS, ROWS)
+        return [pltpu.make_async_copy(k_hbm.at[c, rows], buf.at[slot, c], sem.at[slot, c]) for c in range(2)]
+
+    def start(i):
+        for copy in copies(i):
+            copy.start()
 
     for i in range(BUFFERS - 1):
-        copy(i).start()
+        start(i)
 
     def step(i, carry):
         slot = lax.rem(i, BUFFERS)
-        copy(i).wait()
+        for copy in copies(i):
+            copy.wait()
 
         @pl.when(i + BUFFERS - 1 < steps)
         def _():
-            copy(i + BUFFERS - 1).start()
+            start(i + BUFFERS - 1)
 
         for r in range(0, ROWS, 2):
             x = jnp.concatenate([buf[slot, c, r + j] for j in range(2) for c in range(2)], axis=0)
             for chunk in range(freqs // LANES):
-                o = x[:, chunk * LANES:(chunk + 1) * LANES].T.astype(f32)
+                part = x[:, chunk * LANES:(chunk + 1) * LANES]
+                o = mm(eye, part, NT) if r % 4 == 0 else part.T.astype(f32)
                 for j in range(2):
                     for h in range(2):
-                        rows = pl.ds(chunk * HALF * PITCH + r + j, HALF, stride=PITCH)
+                        rows = pl.ds((r + j) * PITCH + chunk * HALF, HALF)
                         stage[h, rows, :] = o[h * HALF:(h + 1) * HALF, j * LANES:(j + 1) * LANES]
         rows = pl.ds(pl.multiple_of(i * ROWS, ROWS), ROWS)
         for h in range(2):
-            block = stage[h].reshape(freqs // 2, PITCH, LANES)[:, :ROWS]
-            out_ref[:, rows, h * LANES:(h + 1) * LANES] = block.astype(bf16)
+            for pair in range(pairs):
+                out_ref[h, pair, rows, :] = stage[h, pl.ds(pair, ROWS, stride=PITCH), :].astype(bf16)
         return carry
 
     lax.fori_loop(0, steps, step, 0)
@@ -97,13 +107,13 @@
         relayout_body,
         in_specs=[pl.BlockSpec(memory_space=pl.ANY)],
         out_specs=VM,
-        out_shape=pltpu.VMEM((freqs // 2, sensors, 4 * sources), bf16),
+        out_shape=pltpu.VMEM((2, freqs // 2, sensors, 2 * sources), bf16),
         scratch_shapes=[
             pltpu.VMEM((BUFFERS, 2, ROWS, sources, freqs), bf16),
-            pltpu.VMEM((2, freqs // 2 * PITCH, LANES), f32),
-            pltpu.SemaphoreType.DMA((BUFFERS,)),
+            pltpu.VMEM((2, ROWS * PITCH, LANES), f32),
+            pltpu.SemaphoreType.DMA((BUFFERS, 2)),
         ],
-        compiler_params=params(12),
+        compiler_params=params(16),
         name="relayout",
     )(kernel)
 
@@ -130,14 +140,21 @@
 
 
 def contract(k_ref, lhs, res, dims):
-    pairs = k_ref.shape[0]
+    pairs = k_ref.shape[1]
+
+    def tile(pair):
+        return jnp.concatenate([k_ref[0, pair], k_ref[1, pair]], axis=1)
+
+    def turned(pair):
+        blocks = [[k_ref[h, pair, c * LANES:(c + 1) * LANES, :].T for c in range(2)] for h in range(2)]
+        return jnp.concatenate([jnp.concatenate(row, axis=1) for row in blocks], axis=0)
 
     def step(i, carry):
         for u in range(UNROLL):
             pair = i * UNROLL + u
             rows = pl.ds(pl.multiple_of(pair * 8, 8), 8)
             a = jnp.concatenate([lhs[0, rows, :], lhs[1, rows, :]], axis=1).astype(bf16)
-            o = mm(a, k_ref[pair], dims)
+            o = mm(a, turned(pair), NN) if dims == NT and u % 3 else mm(a, tile(pair), dims)
             res[0, rows, :] = o[:, :LANES]
             res[1, rows, :] = o[:, LANES:]
         return carry
@@ -201,7 +218,7 @@
 
 
 def forward_spaces(k2, length, chips, cores):
-    pairs, sensors, _ = k2.shape
+    _, pairs, sensors, _ = k2.shape
     rows = sensors // (chips * cores)
     outs = [jax.ShapeDtypeStruct((chips, rows, length), f32)] * 2
     scratch = [
@@ -267,11 +284,11 @@
 
 
 def adjoint_body(k_ref, mine_ref, other_ref, t_ref, o_ref, lhs, res, full):
-    freqs, sources = t_ref.shape[2], k_ref.shape[2] // 4
+    freqs, sources = t_ref.shape[2], k_ref.shape[3] // 2
     core = lax.axis_index("core")
     full[:, core] = mine_ref[...]
     full[:, full.shape[1] - 1 - core] = other_ref[...]
-    misfit = full[...].reshape(k_ref.shape[1], freqs)
+    misfit = full[...].reshape(k_ref.shape[2], freqs)
     spectrum = mm3((t_ref[0], t_ref[1]), split(misfit), NT)
     w = row_weights(freqs)
     for m in range(2):
@@ -297,11 +314,11 @@
 
 
 def adjoint(k2, mine, other, table):
-    pairs, sensors, width = k2.shape
+    _, pairs, sensors, width = k2.shape
     chips, rows, length = mine.shape
     return pl.pallas_call(
         adjoint_body, in_specs=[VM] * 4, out_specs=VM,
-        out_shape=jax.ShapeDtypeStruct((width // 4, length), f32),
+        out_shape=jax.ShapeDtypeStruct((width // 2, length), f32),
         scratch_shapes=[
             pltpu.VMEM((2, pairs * 8, LANES), f32),
             pltpu.VMEM((2, pairs * 8, LANES), f32),

time: 188 us -> 176 us (0.936)
  Pallas kernels: 62.2 us -> 50 us
    pallas_call x1, Pallas kernels: 17.5 us -> 11.5 us  [relayout(): pl.pallas_call(relayout_body, in_specs=[pl.BlockSpec(memory_space=pl.ANY)...]
    pallas_call x2, Pallas kernels: 17.7 us -> 13.6 us  [forward_next(): pl.pallas_call(functools.partial(forward_next_body, entries), in_specs=[V...]
    pallas_call x1, Pallas kernels: 8.8 us -> 6.73 us  [forward_first(): pl.pallas_call(forward_first_body, in_specs=[VM] * 4, out_specs=[VM] * 4,...]
  transfers between devices with their start and end apart: 10 -> 10, of which waited for: 9 -> 9; matrix products, arithmetic and copies ran while one was open for 0% -> 0% of each run, Pallas kernels for 9% -> 7%
where the time goes in v5:
time: 176 us; the launch traced here: 175 us
  blocking collectives  96.3 us (55%)
  Pallas kernels  50 us (28%)
  waiting for transfers between devices  21.5 us (12%)
  starting transfers between devices  4.98 us (3%)
    all_to_all x6, blocking collectives, to_chips(): return lax.all_to_all(x, 'chip', 0, 0)  68 us
    all_to_all x3, blocking collectives, exchange_scalars(): return lax.all_to_all(sums, ('chip', 'core'), 0, 0, tiled=True)  28.3 us
    ppermute x10, waiting for transfers between devices, swap(): return lax.ppermute(x, axis, [(0, 1), (1, 0)])  21.5 us
    pallas_call x3, Pallas kernels, adjoint(): pl.pallas_call(adjoint_body, in_specs=[VM] * 4, out_specs=VM, out_shape=j...  15.1 us
    pallas_call x2, Pallas kernels, forward_next(): pl.pallas_call(functools.partial(forward_next_body, entries), in_specs=[V...  13.6 us
    pallas_call x1, Pallas kernels, relayout(): pl.pallas_call(relayout_body, in_specs=[pl.BlockSpec(memory_space=pl.ANY)...  11.5 us
    pallas_call x1, Pallas kernels, forward_first(): pl.pallas_call(forward_first_body, in_specs=[VM] * 4, out_specs=[VM] * 4,...  6.73 us
    ppermute x10, starting transfers between devices, swap(): return lax.ppermute(x, axis, [(0, 1), (1, 0)])  4.98 us
  transfers between devices with their start and end apart: 10, of which 9 were waited for; matrix products, arithmetic and copies ran while one was open for 0% of the time, Pallas kernels for 7%

profile of v5, /device:TPU:0, one launch (start us, length us, event | category | flops | bytes accessed | tf_op | source)
XLA Modules:
  0.0 175.1 jit_solution(10897609361614266669)
XLA Ops:
  0.6 0.8 copy-done.2
  1.4 0.7 copy-done.3
  2.2 3.0 %collective-permute-start = (f32[32,512]{1,0:T(8,128)S(1)}, f32[32,512]{1,0:T(8,128)S(1)}, u32[]{:S(2)}, u32[]{:S(2)}) collective-permute-start(f32[32,512]{1,0:T(8,128)S(1)} %pack.1.mine_ref), channel_id=1, source_target_pairs={{0,16},{16,0},{1,17},{17,1},{2,18},{18,2},{3,19},{19,3},{4,20},{20... | collective-permute-start | bytes 196616 | tf_op jit(solution)/shard_map/ppermute | solution.py:347
  5.1 11.5 %relayout.1.k_ref = bf16[2,192,256,128]{3,2,1,0:T(8,128)(2,1)S(1)} custom-call(bf16[2,256,64,384]{3,2,1,0:T(8,128)(2,1)} %k_hbm.1), custom_call_target="tpu_custom_call" | custom-call | tf_op jit(solution)/shard_map/relayout/pallas_call | solution.py:106
  16.6 6.7 %forward_first.1 = (f32[64,384]{1,0:T(8,128)S(1)}, f32[64,128]{1,0:T(8,128)S(1)}, f32[8,16,384]{2,1,0:T(8,128)S(1)}, f32[8,16,384]{2,1,0:T(8,128)S(1)}) custom-call(bf16[2,192,256,128]{3,2,1,0:T(8,128)(2,1)S(1)} %relayout.1.k_ref, f32[32,512]{1,0:T(8,128)S(1)} %pack.1.mine_ref, f32[32,512]{1,0:T(8,128)S(1)} %collective-permute-done.other_ref, ...), custom_call_target="tpu_custom_call" | custom-call | tf_op jit(solution)/shard_map/forward_first/pallas_call | solution.py:235
  23.5 1.4 collective-permute-done.1
  24.9 13.9 %all_to_all.63.parts_ref = f32[8,16,384]{2,1,0:T(8,128)S(1)} all-to-all(f32[8,16,384]{2,1,0:T(8,128)S(1)} %add.9), channel_id=1, replica_groups=mesh['sens'=2,'chip'=8,'core'=2] {'chip'}, dimensions={0} | all-to-all | bytes 393216 | tf_op jit(solution)/shard_map/all_to_all | solution.py:351
  38.8 0.6 misfit.3
  39.4 10.7 %all_to_all.64.mine_ref = f32[8,16,384]{2,1,0:T(8,128)S(1)} all-to-all(f32[8,16,384]{2,1,0:T(8,128)S(1)} %get-tuple-element.25), channel_id=1, replica_groups=mesh['sens'=2,'chip'=8,'core'=2] {'chip'}, dimensions={0} | all-to-all | bytes 393216 | tf_op jit(solution)/shard_map/all_to_all | solution.py:351
  50.2 1.4 collective-permute-done.2.other_ref
  51.6 5.0 %adjoint.3.a_ref = f32[64,384]{1,0:T(8,128)S(1)} custom-call(bf16[2,192,256,128]{3,2,1,0:T(8,128)(2,1)S(1)} %relayout.1.k_ref, f32[8,16,384]{2,1,0:T(8,128)S(1)} %all_to_all.64.mine_ref, f32[8,16,384]{2,1,0:T(8,128)S(1)} %collective-permute-done.2.other_ref, bf16[2,768,384]{2,1,0:T(8,128)(2,1)S(1)} %copy-done), custom_call_target="tpu_custom_call" | custom-call | tf_op jit(solution)/shard_map/adjoint/pallas_call | solution.py:319
  57.2 4.3 %collective-permute-done.3.b_ref = f32[64,384]{1,0:T(8,128)S(1)} collective-permute-done((f32[64,384]{1,0:T(8,128)S(1)}, f32[64,384]{1,0:T(8,128)S(1)}, u32[]{:S(2)}, u32[]{:S(2)}) %collective-permute-start.3) | collective-permute-done | bytes 98336 | tf_op jit(solution)/shard_map/ppermute | solution.py:347
  61.7 9.4 %all_to_all.65 = f32[16,1,128]{2,1,0:T(1,128)S(1)} all-to-all(f32[16,1,128]{2,1,0:T(1,128)S(1)} %bitcast.17), channel_id=1, replica_groups=mesh['sens'=2,'chip'=8,'core'=2] {'chip','core'}, dimensions={0} | all-to-all | bytes 16384 | tf_op jit(solution)/shard_map/all_to_all | solution.py:355
  71.1 6.8 %forward_next.2 = (f32[64,384]{1,0:T(8,128)S(1)}, f32[8,16,384]{2,1,0:T(8,128)S(1)}, f32[8,16,384]{2,1,0:T(8,128)S(1)}) custom-call(bf16[2,192,256,128]{3,2,1,0:T(8,128)(2,1)S(1)} %relayout.1.k_ref, f32[64,384]{1,0:T(8,128)S(1)} %get-tuple-element.22.p_ref, f32[64,384]{1,0:T(8,128)S(1)} %get-tuple-element.27.g_ref, f32[16,128]{1,0:T(8,128)S(1)} %bitcast.13, ...), custom_call_target="tpu_custom_call" | custom-call | tf_op jit(solution)/shard_map/forward_next/pallas_call | solution.py:245
  78.0 1.4 collective-permute-done.4
  79.4 10.9 %all_to_all.66.parts_ref = f32[8,16,384]{2,1,0:T(8,128)S(1)} all-to-all(f32[8,16,384]{2,1,0:T(8,128)S(1)} %add.10), channel_id=1, replica_groups=mesh['sens'=2,'chip'=8,'core'=2] {'chip'}, dimensions={0} | all-to-all | bytes 393216 | tf_op jit(solution)/shard_map/all_to_all | solution.py:351
  90.4 0.6 misfit.4
  91.0 10.7 %all_to_all.67.mine_ref = f32[8,16,384]{2,1,0:T(8,128)S(1)} all-to-all(f32[8,16,384]{2,1,0:T(8,128)S(1)} %get-tuple-element.32), channel_id=1, replica_groups=mesh['sens'=2,'chip'=8,'core'=2] {'chip'}, dimensions={0} | all-to-all | bytes 393216 | tf_op jit(solution)/shard_map/all_to_all | solution.py:351
  101.7 1.4 collective-permute-done.5.other_ref
  103.1 5.0 %adjoint.4.a_ref = f32[64,384]{1,0:T(8,128)S(1)} custom-call(bf16[2,192,256,128]{3,2,1,0:T(8,128)(2,1)S(1)} %relayout.1.k_ref, f32[8,16,384]{2,1,0:T(8,128)S(1)} %all_to_all.67.mine_ref, f32[8,16,384]{2,1,0:T(8,128)S(1)} %collective-permute-done.5.other_ref, bf16[2,768,384]{2,1,0:T(8,128)(2,1)S(1)} %copy-done), custom_call_target="tpu_custom_call" | custom-call | tf_op jit(solution)/shard_map/adjoint/pallas_call | solution.py:319
  108.8 4.3 %collective-permute-done.6.b_ref = f32[64,384]{1,0:T(8,128)S(1)} collective-permute-done((f32[64,384]{1,0:T(8,128)S(1)}, f32[64,384]{1,0:T(8,128)S(1)}, u32[]{:S(2)}, u32[]{:S(2)}) %collective-permute-start.6) | collective-permute-done | bytes 98336 | tf_op jit(solution)/shard_map/ppermute | solution.py:347
  113.2 9.4 %all_to_all.68 = f32[16,1,128]{2,1,0:T(1,128)S(1)} all-to-all(f32[16,1,128]{2,1,0:T(1,128)S(1)} %bitcast.18), channel_id=1, replica_groups=mesh['sens'=2,'chip'=8,'core'=2] {'chip','core'}, dimensions={0} | all-to-all | bytes 16384 | tf_op jit(solution)/shard_map/all_to_all | solution.py:355
  122.7 6.8 %forward_next.3 = (f32[64,384]{1,0:T(8,128)S(1)}, f32[8,16,384]{2,1,0:T(8,128)S(1)}, f32[8,16,384]{2,1,0:T(8,128)S(1)}) custom-call(bf16[2,192,256,128]{3,2,1,0:T(8,128)(2,1)S(1)} %relayout.1.k_ref, f32[64,384]{1,0:T(8,128)S(1)} %get-tuple-element.29.p_ref, f32[64,384]{1,0:T(8,128)S(1)} %get-tuple-element.33.g_ref, f32[16,128]{1,0:T(8,128)S(1)} %bitcast.14, ...), custom_call_target="tpu_custom_call" | custom-call | tf_op jit(solution)/shard_map/forward_next/pallas_call | solution.py:245
  129.5 1.4 collective-permute-done.7
  131.0 10.9 %all_to_all.69.parts_ref = f32[8,16,384]{2,1,0:T(8,128)S(1)} all-to-all(f32[8,16,384]{2,1,0:T(8,128)S(1)} %add.11), channel_id=1, replica_groups=mesh['sens'=2,'chip'=8,'core'=2] {'chip'}, dimensions={0} | all-to-all | bytes 393216 | tf_op jit(solution)/shard_map/all_to_all | solution.py:351
  141.9 0.6 misfit.5
  142.6 10.8 %all_to_all.70.mine_ref = f32[8,16,384]{2,1,0:T(8,128)S(1)} all-to-all(f32[8,16,384]{2,1,0:T(8,128)S(1)} %get-tuple-element.38), channel_id=1, replica_groups=mesh['sens'=2,'chip'=8,'core'=2] {'chip'}, dimensions={0} | all-to-all | bytes 393216 | tf_op jit(solution)/shard_map/all_to_all | solution.py:351
  153.4 1.4 collective-permute-done.8.other_ref
  154.8 5.0 %adjoint.5.a_ref = f32[64,384]{1,0:T(8,128)S(1)} custom-call(bf16[2,192,256,128]{3,2,1,0:T(8,128)(2,1)S(1)} %relayout.1.k_ref, f32[8,16,384]{2,1,0:T(8,128)S(1)} %all_to_all.70.mine_ref, f32[8,16,384]{2,1,0:T(8,128)S(1)} %collective-permute-done.8.other_ref, bf16[2,768,384]{2,1,0:T(8,128)(2,1)S(1)} %copy-done), custom_call_target="tpu_custom_call" | custom-call | tf_op jit(solution)/shard_map/adjoint/pallas_call | solution.py:319
  160.5 4.3 %collective-permute-done.9.b_ref = f32[64,384]{1,0:T(8,128)S(1)} collective-permute-done((f32[64,384]{1,0:T(8,128)S(1)}, f32[64,384]{1,0:T(8,128)S(1)}, u32[]{:S(2)}, u32[]{:S(2)}) %collective-permute-start.9) | collective-permute-done | bytes 98336 | tf_op jit(solution)/shard_map/ppermute | solution.py:347
  164.9 9.5 %all_to_all.71 = f32[16,1,128]{2,1,0:T(1,128)S(1)} all-to-all(f32[16,1,128]{2,1,0:T(1,128)S(1)} %bitcast.16), channel_id=1, replica_groups=mesh['sens'=2,'chip'=8,'core'=2] {'chip','core'}, dimensions={0} | all-to-all | bytes 16384 | tf_op jit(solution)/shard_map/all_to_all | solution.py:355
  174.4 0.7 finish.1
  (23 shorter events, 2.7 us)
Async XLA Ops:
  0.6 0.8 copy-start.2
  1.4 0.7 copy-start.3
  2.2 14.5 %copy-start = (bf16[2,768,384]{2,1,0:T(8,128)(2,1)S(1)}, bf16[2,768,384]{2,1,0:T(8,128)(2,1)}, u32[]{:S(2)}) copy-start(bf16[2,768,384]{2,1,0:T(8,128)(2,1)} %constant.2.clone.t_ref) | copy-start | bytes 3538948
  2.2 14.5 %collective-permute-start = (f32[32,512]{1,0:T(8,128)S(1)}, f32[32,512]{1,0:T(8,128)S(1)}, u32[]{:S(2)}, u32[]{:S(2)}) collective-permute-start(f32[32,512]{1,0:T(8,128)S(1)} %pack.1.mine_ref), channel_id=1, source_target_pairs={{0,16},{16,0},{1,17},{17,1},{2,18},{18,2},{3,19},{19,3},{4,20},{20... | collective-permute-start | bytes 196616 | tf_op jit(solution)/shard_map/ppermute | solution.py:347
  16.6 22.2 %copy-start.1 = (f32[256,384]{1,0:T(8,128)S(1)}, f32[256,384]{1,0:T(8,128)}, u32[]{:S(2)}) copy-start(f32[256,384]{1,0:T(8,128)} %obs_ref.5) | copy-start | bytes 1179652
  23.4 1.5 collective-permute-start.1
  50.2 1.4 collective-permute-start.2
  56.6 4.9 %collective-permute-start.3 = (f32[64,384]{1,0:T(8,128)S(1)}, f32[64,384]{1,0:T(8,128)S(1)}, u32[]{:S(2)}, u32[]{:S(2)}) collective-permute-start(f32[64,384]{1,0:T(8,128)S(1)} %adjoint.3.a_ref), channel_id=1, source_target_pairs={{0,16},{16,0},{1,17},{17,1},{2,18},{18,2},{3,19},{19,3},{4,20},{20... | collective-permute-start | bytes 294920 | tf_op jit(solution)/shard_map/ppermute | solution.py:347
  77.9 1.5 collective-permute-start.4
  101.7 1.4 collective-permute-start.5
  108.2 4.9 %collective-permute-start.6 = (f32[64,384]{1,0:T(8,128)S(1)}, f32[64,384]{1,0:T(8,128)S(1)}, u32[]{:S(2)}, u32[]{:S(2)}) collective-permute-start(f32[64,384]{1,0:T(8,128)S(1)} %adjoint.4.a_ref), channel_id=1, source_target_pairs={{0,16},{16,0},{1,17},{17,1},{2,18},{18,2},{3,19},{19,3},{4,20},{20... | collective-permute-start | bytes 294920 | tf_op jit(solution)/shard_map/ppermute | solution.py:347
  129.4 1.5 collective-permute-start.7
  153.4 1.4 collective-permute-start.8
  159.9 4.9 %collective-permute-start.9 = (f32[64,384]{1,0:T(8,128)S(1)}, f32[64,384]{1,0:T(8,128)S(1)}, u32[]{:S(2)}, u32[]{:S(2)}) collective-permute-start(f32[64,384]{1,0:T(8,128)S(1)} %adjoint.5.a_ref), channel_id=1, source_target_pairs={{0,16},{16,0},{1,17},{17,1},{2,18},{18,2},{3,19},{19,3},{4,20},{20... | collective-permute-start | bytes 294920 | tf_op jit(solution)/shard_map/ppermute | solution.py:347

commit v6 on v5

--- a/solution.py
+++ b/solution.py
@@ -118,45 +118,26 @@
     )(kernel)
 
 
-def pack_body(p_ref, rig_ref, o_ref):
-    rows, length = p_ref.shape
-    o_ref[:, :length] = p_ref[...]
-    same = lax.broadcasted_iota(jnp.int32, (rows, rows), 0) == lax.broadcasted_iota(jnp.int32, (rows, rows), 1)
-    column = jnp.sum(jnp.where(same, jnp.broadcast_to(rig_ref[...], (rows, rows)), 0.0), axis=1, keepdims=True)
-    o_ref[:, length:] = jnp.broadcast_to(column, (rows, LANES))
-
-
-def pack(slip_param, rigidity):
-    rows, length = slip_param.shape
-    return pl.pallas_call(
-        pack_body, in_specs=[VM] * 2, out_specs=VM,
-        out_shape=jax.ShapeDtypeStruct((rows, length + LANES), f32),
-        compiler_params=params(4), name="pack",
-    )(slip_param, rigidity.reshape(1, rows))
-
-
 def pair_row(chunk, h, m):
     return pl.ds(chunk * HALF * 8 + 4 * h + m, HALF, stride=8)
 
 
-def contract(k_ref, lhs, res, dims):
-    pairs = k_ref.shape[1]
-
-    def tile(pair):
-        return jnp.concatenate([k_ref[0, pair], k_ref[1, pair]], axis=1)
-
-    def turned(pair):
-        blocks = [[k_ref[h, pair, c * LANES:(c + 1) * LANES, :].T for c in range(2)] for h in range(2)]
-        return jnp.concatenate([jnp.concatenate(row, axis=1) for row in blocks], axis=0)
+def tile(k_ref, pair):
+    return jnp.concatenate([k_ref[0, pair], k_ref[1, pair]], axis=1)
+
+
+def turned(k_ref, pair):
+    blocks = [[k_ref[h, pair, c * LANES:(c + 1) * LANES, :].T for c in range(2)] for h in range(2)]
+    return jnp.concatenate([jnp.concatenate(row, axis=1) for row in blocks], axis=0)
+
+
+def each_pair(pairs, body):
+    first = lax.broadcasted_iota(jnp.int32, (8, LANES), 0) < 4
 
     def step(i, carry):
         for u in range(UNROLL):
             pair = i * UNROLL + u
-            rows = pl.ds(pl.multiple_of(pair * 8, 8), 8)
-            a = jnp.concatenate([lhs[0, rows, :], lhs[1, rows, :]], axis=1).astype(bf16)
-            o = mm(a, turned(pair), NN) if dims == NT and u % 3 else mm(a, tile(pair), dims)
-            res[0, rows, :] = o[:, :LANES]
-            res[1, rows, :] = o[:, LANES:]
+            body(u, pair, pl.ds(pl.multiple_of(pair * 8, 8), 8), first)
         return carry
 
     lax.fori_loop(0, pairs // UNROLL, step, 0)
@@ -164,20 +145,27 @@
 
 def forward_core(param, scale_rows, k_ref, t_ref, keep_ref, send_ref, lhs, res, terms):
     freqs, sources = param.shape[1], param.shape[0]
-    slip = scale_rows * jax.nn.softplus(param)
-    z = mm3((t_ref[0], t_ref[1]), split(jnp.concatenate([slip, slip], axis=0)), NT)
+    high, rest = split(scale_rows * jax.nn.softplus(param))
+    z = mm(t_ref[0], jnp.concatenate([high, high, rest, rest], axis=0), NT)
+    z = z[:, :LANES] + (z[:, LANES:] + mm(t_ref[1], jnp.concatenate([high, high], axis=0), NT))
     low = lax.broadcasted_iota(jnp.int32, (freqs, LANES), 1) < sources
     real, imag = z[:freqs], z[freqs:]
-    zero = jnp.zeros((HALF, LANES), f32)
     for m, x in enumerate((jnp.where(low, real, -imag), jnp.where(low, imag, real))):
         high = x.astype(bf16).astype(f32)
         for n, v in enumerate((high, x - high)):
             for chunk in range(freqs // LANES):
                 for h in range(2):
                     first = chunk * LANES + h * HALF
-                    lhs[h, pair_row(chunk, h, 2 * n + m), :] = v[first:first + HALF]
-                    lhs[1 - h, pair_row(chunk, h, 2 * n + m), :] = zero
-    contract(k_ref, lhs, res, NT)
+                    lhs[pair_row(chunk, h, 2 * n + m), :] = v[first:first + HALF]
+
+    def body(u, pair, rows, first):
+        v = lhs[rows, :]
+        a = jnp.concatenate([jnp.where(first, v, 0.0), jnp.where(first, 0.0, v)], axis=1).astype(bf16)
+        o = mm(a, turned(k_ref, pair), NN) if u % 3 else mm(a, tile(k_ref, pair), NT)
+        res[0, rows, :] = o[:, :LANES]
+        res[1, rows, :] = o[:, LANES:]
+
+    each_pair(k_ref.shape[1], body)
     w = row_weights(freqs)
     halves = []
     for m in range(2):
@@ -194,15 +182,19 @@
     send_ref[...] = terms[:, terms.shape[1] - 1 - core]
 
 
-def forward_first_body(k_ref, mine_ref, other_ref, t_ref, new_ref, rig_ref, keep_ref, send_ref, lhs, res, terms, both):
+def forward_first_body(k_ref, mine_ref, other_ref, rig_mine_ref, rig_other_ref, t_ref, new_ref, rig_ref, keep_ref, send_ref, lhs, res, terms, both, scales):
     sens = lax.axis_index("sens")
-    both[sens] = mine_ref[...]
-    both[1 - sens] = other_ref[...]
-    packed = both[...].reshape(-1, both.shape[2])
-    length = new_ref.shape[1]
-    new_ref[...] = packed[:, :length]
-    rig_ref[...] = packed[:, length:]
-    forward_core(packed[:, :length], packed[:, length:length + 1], k_ref, t_ref, keep_ref, send_ref, lhs, res, terms)
+    rows = mine_ref.shape[0]
+    same = lax.broadcasted_iota(jnp.int32, (rows, rows), 0) == lax.broadcasted_iota(jnp.int32, (rows, rows), 1)
+    for place, p_ref, r_ref in ((sens, mine_ref, rig_mine_ref), (1 - sens, other_ref, rig_other_ref)):
+        both[place] = p_ref[...]
+        column = jnp.sum(jnp.where(same, jnp.broadcast_to(r_ref[...], (rows, rows)), 0.0), axis=1, keepdims=True)
+        scales[place] = jnp.broadcast_to(column, (rows, LANES))
+    param = both[...].reshape(new_ref.shape)
+    scale_rows = scales[...].reshape(rig_ref.shape)
+    new_ref[...] = param
+    rig_ref[...] = scale_rows
+    forward_core(param, scale_rows[:, 0:1], k_ref, t_ref, keep_ref, send_ref, lhs, res, terms)
 
 
 def moved(param, gradient, sums, entries):
@@ -222,22 +214,22 @@
     rows = sensors // (chips * cores)
     outs = [jax.ShapeDtypeStruct((chips, rows, length), f32)] * 2
     scratch = [
-        pltpu.VMEM((2, pairs * 8, LANES), f32),
+        pltpu.VMEM((pairs * 8, LANES), f32),
         pltpu.VMEM((2, pairs * 8, LANES), f32),
         pltpu.VMEM((chips, cores, rows, length), f32),
     ]
     return outs, scratch
 
 
-def forward_first(k2, mine, other, table, chips, cores):
+def forward_first(k2, mine, other, rig_mine, rig_other, table, chips, cores):
     sources, length = 2 * mine.shape[0], table.shape[2]
     outs, scratch = forward_spaces(k2, length, chips, cores)
     return pl.pallas_call(
-        forward_first_body, in_specs=[VM] * 4, out_specs=[VM] * 4,
+        forward_first_body, in_specs=[VM] * 6, out_specs=[VM] * 4,
         out_shape=[jax.ShapeDtypeStruct((sources, length), f32), jax.ShapeDtypeStruct((sources, LANES), f32)] + outs,
-        scratch_shapes=scratch + [pltpu.VMEM((2, *mine.shape), f32)],
+        scratch_shapes=scratch + [pltpu.VMEM((2, *mine.shape), f32), pltpu.VMEM((2, mine.shape[0], LANES), f32)],
         compiler_params=params(12), name="forward_first",
-    )(k2, mine, other, table)
+    )(k2, mine, other, rig_mine, rig_other, table)
 
 
 def forward_next(k2, param, gradient, sums, scale_rows, table, chips, cores, entries):
@@ -261,10 +253,11 @@
         spread_ref[c] = misfit
 
 
-def misfit_and_spread(parts, observed):
+def misfit_and_spread(parts, observed, last):
+    space = jax.ShapeDtypeStruct if last else pltpu.VMEM
     return pl.pallas_call(
         misfit_body, in_specs=[VM] * 2, out_specs=[VM] * 2,
-        out_shape=[jax.ShapeDtypeStruct(parts.shape[1:], f32), jax.ShapeDtypeStruct(parts.shape, f32)],
+        out_shape=[space(parts.shape[1:], f32), jax.ShapeDtypeStruct(parts.shape, f32)],
         compiler_params=params(4), name="misfit",
     )(parts, observed)
 
@@ -300,12 +293,18 @@
                     first = chunk * LANES + h * HALF
                     for c in range(2):
                         lhs[c, pair_row(chunk, h, 2 * n + m), :] = v[first:first + HALF, c * LANES:(c + 1) * LANES]
-    contract(k_ref, lhs, res, NN)
+
+    def body(u, pair, rows, first):
+        a = jnp.concatenate([lhs[0, rows, :], lhs[1, rows, :]], axis=1).astype(bf16)
+        o = mm(a, tile(k_ref, pair), NN)
+        res[rows, :] = jnp.where(first, o[:, :LANES], o[:, LANES:])
+
+    each_pair(k_ref.shape[1], body)
     low = lax.broadcasted_iota(jnp.int32, (HALF, LANES), 1) < sources
     parts = []
     for chunk in range(freqs // LANES):
         for h in range(2):
-            real, imag = [res[h, pair_row(chunk, h, m), :] + res[h, pair_row(chunk, h, 2 + m), :] for m in range(2)]
+            real, imag = [res[pair_row(chunk, h, m), :] + res[pair_row(chunk, h, 2 + m), :] for m in range(2)]
             parts.append(jnp.where(low, real, -real) + pltpu.roll(imag, sources, 1))
     back = jnp.concatenate(parts, axis=0).T
     o_ref[...] = mm3(split(back[:sources]), (t_ref[0, :freqs], t_ref[1, :freqs]), NN) + mm3(
@@ -321,7 +320,7 @@
         out_shape=jax.ShapeDtypeStruct((width // 2, length), f32),
         scratch_shapes=[
             pltpu.VMEM((2, pairs * 8, LANES), f32),
-            pltpu.VMEM((2, pairs * 8, LANES), f32),
+            pltpu.VMEM((pairs * 8, LANES), f32),
             pltpu.VMEM((chips, sensors // (chips * rows), rows, length), f32),
         ],
         compiler_params=params(12), name="adjoint",
@@ -404,14 +403,14 @@
 def iterations(slip_param, rigidity, kernel, observed, entries):
     chips, cores = lax.axis_size("chip"), lax.axis_size("core")
     table = table_parts(slip_param.shape[1])
-    mine = pack(slip_param, rigidity)
-    other = swap(mine, "sens")
+    scales = rigidity.reshape(1, -1)
+    others, other_scales = swap(slip_param, "sens"), swap(scales, "sens")
     k2 = relayout(kernel)
-    param, scale_rows, keep, send = forward_first(k2, mine, other, table, chips, cores)
+    param, scale_rows, keep, send = forward_first(k2, slip_param, others, scales, other_scales, table, chips, cores)
     for iteration in range(ITERS):
         if iteration:
             param, keep, send = forward_next(k2, param, gradient, sums, scale_rows, table, chips, cores, entries)
-        misfit, spread = misfit_and_spread(to_chips(keep + swap(send, "core")), observed)
+        misfit, spread = misfit_and_spread(to_chips(keep + swap(send, "core")), observed, iteration == ITERS - 1)
         near = to_chips(spread)
         back = adjoint(k2, near, swap(near, "core"), table)
         gradient, sums = gradient_and_square(back, swap(back, "sens"), param, scale_rows, chips * cores)

time: 176 us -> 174 us (0.989)
  starting transfers between devices: 4.98 us -> 8.01 us
  waiting for transfers between devices: 21.5 us -> 18.7 us
    ppermute x10 -> x11, starting transfers between devices: 4.98 us -> 8.01 us  [swap(): return lax.ppermute(x, axis, [(0, 1), (1, 0)])]
    ppermute x10 -> x11, waiting for transfers between devices: 21.5 us -> 18.7 us  [swap(): return lax.ppermute(x, axis, [(0, 1), (1, 0)])]
    pallas_call x2 -> x1, Pallas kernels: 6.81 us -> 6.59 us  [forward_first(): pl.pallas_call(forward_first_body, in_specs=[VM] * 6, out_specs=[VM] * 4,...]
  transfers between devices with their start and end apart: 10 -> 11, of which waited for: 9 -> 9; matrix products, arithmetic and copies ran while one was open for 0% -> 0% of each run, Pallas kernels for 7% -> 7%
where the time goes in v6:
time: 174 us; the launch traced here: 173 us
  blocking collectives  96.5 us (55%)
  Pallas kernels  49.5 us (28%)
  waiting for transfers between devices  18.7 us (11%)
  starting transfers between devices  8.01 us (5%)
    all_to_all x6, blocking collectives, to_chips(): return lax.all_to_all(x, 'chip', 0, 0)  68.3 us
    all_to_all x3, blocking collectives, exchange_scalars(): return lax.all_to_all(sums, ('chip', 'core'), 0, 0, tiled=True)  28.2 us
    ppermute x11, waiting for transfers between devices, swap(): return lax.ppermute(x, axis, [(0, 1), (1, 0)])  18.7 us
    pallas_call x3, Pallas kernels, adjoint(): pl.pallas_call(adjoint_body, in_specs=[VM] * 4, out_specs=VM, out_shape=j...  15.1 us
    pallas_call x2, Pallas kernels, forward_next(): pl.pallas_call(functools.partial(forward_next_body, entries), in_specs=[V...  13.1 us
    pallas_call x1, Pallas kernels, relayout(): pl.pallas_call(relayout_body, in_specs=[pl.BlockSpec(memory_space=pl.ANY)...  11.5 us
    ppermute x11, starting transfers between devices, swap(): return lax.ppermute(x, axis, [(0, 1), (1, 0)])  8.01 us
    pallas_call x1, Pallas kernels, forward_first(): pl.pallas_call(forward_first_body, in_specs=[VM] * 6, out_specs=[VM] * 4,...  6.59 us
  transfers between devices with their start and end apart: 11, of which 9 were waited for; matrix products, arithmetic and copies ran while one was open for 0% of the time, Pallas kernels for 7%

profile of v6, /device:TPU:0, one launch (start us, length us, event | category | flops | bytes accessed | tf_op | source)
XLA Modules:
  0.0 173.5 jit_solution(17804803181440301128)
XLA Ops:
  0.6 3.0 %collective-permute-start = (f32[32,384]{1,0:T(8,128)}, f32[32,384]{1,0:T(8,128)S(1)}, u32[]{:S(2)}, u32[]{:S(2)}) collective-permute-start(f32[32,384]{1,0:T(8,128)} %mine_ref.1), channel_id=1, source_target_pairs={{0,16},{16,0},{1,17},{17,1},{2,18},{18,2},{3,19},{19,3},{4,20},{20... | collective-permute-start | bytes 147464 | tf_op jit(solution)/shard_map/ppermute | solution.py:346
  3.8 11.5 %relayout.1.k_ref = bf16[2,192,256,128]{3,2,1,0:T(8,128)(2,1)S(1)} custom-call(bf16[2,256,64,384]{3,2,1,0:T(8,128)(2,1)} %k_hbm.1), custom_call_target="tpu_custom_call" | custom-call | tf_op jit(solution)/shard_map/relayout/pallas_call | solution.py:106
  15.4 6.6 %forward_first.1 = (f32[64,384]{1,0:T(8,128)S(1)}, f32[64,128]{1,0:T(8,128)S(1)}, f32[8,16,384]{2,1,0:T(8,128)S(1)}, f32[8,16,384]{2,1,0:T(8,128)S(1)}) custom-call(bf16[2,192,256,128]{3,2,1,0:T(8,128)(2,1)S(1)} %relayout.1.k_ref, f32[32,384]{1,0:T(8,128)S(1)} %copy-done.2, f32[32,384]{1,0:T(8,128)S(1)} %collective-permute-done.other_ref, ...), custom_call_target="tpu_custom_call" | custom-call | tf_op jit(solution)/shard_map/forward_first/pallas_call | solution.py:227
  22.1 1.4 collective-permute-done.2
  23.5 14.3 %all_to_all.63.parts_ref = f32[8,16,384]{2,1,0:T(8,128)S(1)} all-to-all(f32[8,16,384]{2,1,0:T(8,128)S(1)} %add.9), channel_id=1, replica_groups=mesh['sens'=2,'chip'=8,'core'=2] {'chip'}, dimensions={0} | all-to-all | bytes 393216 | tf_op jit(solution)/shard_map/all_to_all | solution.py:350
  37.8 0.6 misfit.3
  38.4 10.7 %all_to_all.64.mine_ref = f32[8,16,384]{2,1,0:T(8,128)S(1)} all-to-all(f32[8,16,384]{2,1,0:T(8,128)S(1)} %get-tuple-element.25), channel_id=1, replica_groups=mesh['sens'=2,'chip'=8,'core'=2] {'chip'}, dimensions={0} | all-to-all | bytes 393216 | tf_op jit(solution)/shard_map/all_to_all | solution.py:350
  49.1 1.4 collective-permute-done.3.other_ref
  50.6 5.0 %adjoint.3.a_ref = f32[64,384]{1,0:T(8,128)S(1)} custom-call(bf16[2,192,256,128]{3,2,1,0:T(8,128)(2,1)S(1)} %relayout.1.k_ref, f32[8,16,384]{2,1,0:T(8,128)S(1)} %all_to_all.64.mine_ref, f32[8,16,384]{2,1,0:T(8,128)S(1)} %collective-permute-done.3.other_ref, bf16[2,768,384]{2,1,0:T(8,128)(2,1)S(1)} %copy-done), custom_call_target="tpu_custom_call" | custom-call | tf_op jit(solution)/shard_map/adjoint/pallas_call | solution.py:318
  55.6 1.5 collective-permute-start.4
  57.2 3.4 %collective-permute-done.4.b_ref = f32[64,384]{1,0:T(8,128)S(1)} collective-permute-done((f32[64,384]{1,0:T(8,128)S(1)}, f32[64,384]{1,0:T(8,128)S(1)}, u32[]{:S(2)}, u32[]{:S(2)}) %collective-permute-start.4) | collective-permute-done | bytes 98336 | tf_op jit(solution)/shard_map/ppermute | solution.py:346
  60.7 9.4 %all_to_all.65 = f32[16,1,128]{2,1,0:T(1,128)S(1)} all-to-all(f32[16,1,128]{2,1,0:T(1,128)S(1)} %bitcast.17), channel_id=1, replica_groups=mesh['sens'=2,'chip'=8,'core'=2] {'chip','core'}, dimensions={0} | all-to-all | bytes 16384 | tf_op jit(solution)/shard_map/all_to_all | solution.py:354
  70.1 6.6 %forward_next.2 = (f32[64,384]{1,0:T(8,128)S(1)}, f32[8,16,384]{2,1,0:T(8,128)S(1)}, f32[8,16,384]{2,1,0:T(8,128)S(1)}) custom-call(bf16[2,192,256,128]{3,2,1,0:T(8,128)(2,1)S(1)} %relayout.1.k_ref, f32[64,384]{1,0:T(8,128)S(1)} %get-tuple-element.22.p_ref, f32[64,384]{1,0:T(8,128)S(1)} %get-tuple-element.27.g_ref, f32[16,128]{1,0:T(8,128)S(1)} %bitcast.13, ...), custom_call_target="tpu_custom_call" | custom-call | tf_op jit(solution)/shard_map/forward_next/pallas_call | solution.py:237
  76.7 1.4 collective-permute-done.5
  78.2 10.9 %all_to_all.66.parts_ref = f32[8,16,384]{2,1,0:T(8,128)S(1)} all-to-all(f32[8,16,384]{2,1,0:T(8,128)S(1)} %add.10), channel_id=1, replica_groups=mesh['sens'=2,'chip'=8,'core'=2] {'chip'}, dimensions={0} | all-to-all | bytes 393216 | tf_op jit(solution)/shard_map/all_to_all | solution.py:350
  89.1 0.6 misfit.4
  89.8 10.7 %all_to_all.67.mine_ref = f32[8,16,384]{2,1,0:T(8,128)S(1)} all-to-all(f32[8,16,384]{2,1,0:T(8,128)S(1)} %get-tuple-element.32), channel_id=1, replica_groups=mesh['sens'=2,'chip'=8,'core'=2] {'chip'}, dimensions={0} | all-to-all | bytes 393216 | tf_op jit(solution)/shard_map/all_to_all | solution.py:350
  100.5 1.4 collective-permute-done.6.other_ref
  101.9 5.0 %adjoint.4.a_ref = f32[64,384]{1,0:T(8,128)S(1)} custom-call(bf16[2,192,256,128]{3,2,1,0:T(8,128)(2,1)S(1)} %relayout.1.k_ref, f32[8,16,384]{2,1,0:T(8,128)S(1)} %all_to_all.67.mine_ref, f32[8,16,384]{2,1,0:T(8,128)S(1)} %collective-permute-done.6.other_ref, bf16[2,768,384]{2,1,0:T(8,128)(2,1)S(1)} %copy-done), custom_call_target="tpu_custom_call" | custom-call | tf_op jit(solution)/shard_map/adjoint/pallas_call | solution.py:318
  106.9 1.6 collective-permute-start.7
  108.5 3.4 %collective-permute-done.7.b_ref = f32[64,384]{1,0:T(8,128)S(1)} collective-permute-done((f32[64,384]{1,0:T(8,128)S(1)}, f32[64,384]{1,0:T(8,128)S(1)}, u32[]{:S(2)}, u32[]{:S(2)}) %collective-permute-start.7) | collective-permute-done | bytes 98336 | tf_op jit(solution)/shard_map/ppermute | solution.py:346
  112.0 9.4 %all_to_all.68 = f32[16,1,128]{2,1,0:T(1,128)S(1)} all-to-all(f32[16,1,128]{2,1,0:T(1,128)S(1)} %bitcast.18), channel_id=1, replica_groups=mesh['sens'=2,'chip'=8,'core'=2] {'chip','core'}, dimensions={0} | all-to-all | bytes 16384 | tf_op jit(solution)/shard_map/all_to_all | solution.py:354
  121.4 6.6 %forward_next.3 = (f32[64,384]{1,0:T(8,128)S(1)}, f32[8,16,384]{2,1,0:T(8,128)S(1)}, f32[8,16,384]{2,1,0:T(8,128)S(1)}) custom-call(bf16[2,192,256,128]{3,2,1,0:T(8,128)(2,1)S(1)} %relayout.1.k_ref, f32[64,384]{1,0:T(8,128)S(1)} %get-tuple-element.29.p_ref, f32[64,384]{1,0:T(8,128)S(1)} %get-tuple-element.33.g_ref, f32[16,128]{1,0:T(8,128)S(1)} %bitcast.14, ...), custom_call_target="tpu_custom_call" | custom-call | tf_op jit(solution)/shard_map/forward_next/pallas_call | solution.py:237
  128.1 1.4 collective-permute-done.8
  129.5 10.9 %all_to_all.69.parts_ref = f32[8,16,384]{2,1,0:T(8,128)S(1)} all-to-all(f32[8,16,384]{2,1,0:T(8,128)S(1)} %add.11), channel_id=1, replica_groups=mesh['sens'=2,'chip'=8,'core'=2] {'chip'}, dimensions={0} | all-to-all | bytes 393216 | tf_op jit(solution)/shard_map/all_to_all | solution.py:350
  141.1 10.7 %all_to_all.70.mine_ref = f32[8,16,384]{2,1,0:T(8,128)S(1)} all-to-all(f32[8,16,384]{2,1,0:T(8,128)S(1)} %get-tuple-element.38), channel_id=1, replica_groups=mesh['sens'=2,'chip'=8,'core'=2] {'chip'}, dimensions={0} | all-to-all | bytes 393216 | tf_op jit(solution)/shard_map/all_to_all | solution.py:350
  151.8 1.4 collective-permute-done.9.other_ref
  153.3 5.0 %adjoint.5.a_ref = f32[64,384]{1,0:T(8,128)S(1)} custom-call(bf16[2,192,256,128]{3,2,1,0:T(8,128)(2,1)S(1)} %relayout.1.k_ref, f32[8,16,384]{2,1,0:T(8,128)S(1)} %all_to_all.70.mine_ref, f32[8,16,384]{2,1,0:T(8,128)S(1)} %collective-permute-done.9.other_ref, bf16[2,768,384]{2,1,0:T(8,128)(2,1)S(1)} %copy-done), custom_call_target="tpu_custom_call" | custom-call | tf_op jit(solution)/shard_map/adjoint/pallas_call | solution.py:318
  158.3 1.5 collective-permute-start.10
  159.8 3.4 %collective-permute-done.10.b_ref = f32[64,384]{1,0:T(8,128)S(1)} collective-permute-done((f32[64,384]{1,0:T(8,128)S(1)}, f32[64,384]{1,0:T(8,128)S(1)}, u32[]{:S(2)}, u32[]{:S(2)}) %collective-permute-start.10) | collective-permute-done | bytes 98336 | tf_op jit(solution)/shard_map/ppermute | solution.py:346
  163.4 9.4 %all_to_all.71 = f32[16,1,128]{2,1,0:T(1,128)S(1)} all-to-all(f32[16,1,128]{2,1,0:T(1,128)S(1)} %bitcast.16), channel_id=1, replica_groups=mesh['sens'=2,'chip'=8,'core'=2] {'chip','core'}, dimensions={0} | all-to-all | bytes 16384 | tf_op jit(solution)/shard_map/all_to_all | solution.py:354
  172.8 0.7 finish.1
  (24 shorter events, 1.6 us)
Async XLA Ops:
  0.6 14.7 %collective-permute-start = (f32[32,384]{1,0:T(8,128)}, f32[32,384]{1,0:T(8,128)S(1)}, u32[]{:S(2)}, u32[]{:S(2)}) collective-permute-start(f32[32,384]{1,0:T(8,128)} %mine_ref.1), channel_id=1, source_target_pairs={{0,16},{16,0},{1,17},{17,1},{2,18},{18,2},{3,19},{19,3},{4,20},{20... | collective-permute-start | bytes 147464 | tf_op jit(solution)/shard_map/ppermute | solution.py:346
  3.7 11.7 %copy-start = (bf16[2,768,384]{2,1,0:T(8,128)(2,1)S(1)}, bf16[2,768,384]{2,1,0:T(8,128)(2,1)}, u32[]{:S(2)}) copy-start(bf16[2,768,384]{2,1,0:T(8,128)(2,1)} %constant.2.clone.t_ref) | copy-start | bytes 3538948
  3.7 11.7 %copy-start.2 = (f32[32,384]{1,0:T(8,128)S(1)}, f32[32,384]{1,0:T(8,128)}, u32[]{:S(2)}) copy-start(f32[32,384]{1,0:T(8,128)} %mine_ref.1) | copy-start | bytes 147460
  3.7 11.7 %copy-start.3 = (f32[32]{0:T(128)S(1)}, f32[32]{0:T(128)}, u32[]{:S(2)}) copy-start(f32[32]{0:T(128)} %param.6) | copy-start | bytes 388
  3.7 11.7 %collective-permute-start.1 = (f32[1,32]{1,0:T(1,128)}, f32[1,32]{1,0:T(1,128)S(1)}, u32[]{:S(2)}, u32[]{:S(2)}) collective-permute-start(f32[1,32]{1,0:T(1,128)} %bitcast.19), channel_id=1, source_target_pairs={{0,16},{16,0},{1,17},{17,1},{2,18},{18,2},{3,19},{19,3},{4,20},{20... | collective-permute-start | bytes 392 | tf_op jit(solution)/shard_map/ppermute | solution.py:346
  15.3 22.5 %copy-start.1 = (f32[256,384]{1,0:T(8,128)S(1)}, f32[256,384]{1,0:T(8,128)}, u32[]{:S(2)}) copy-start(f32[256,384]{1,0:T(8,128)} %obs_ref.5) | copy-start | bytes 1179652
  22.0 1.5 collective-permute-start.2
  49.1 1.4 collective-permute-start.3
  55.6 4.9 %collective-permute-start.4 = (f32[64,384]{1,0:T(8,128)S(1)}, f32[64,384]{1,0:T(8,128)S(1)}, u32[]{:S(2)}, u32[]{:S(2)}) collective-permute-start(f32[64,384]{1,0:T(8,128)S(1)} %adjoint.3.a_ref), channel_id=1, source_target_pairs={{0,16},{16,0},{1,17},{17,1},{2,18},{18,2},{3,19},{19,3},{4,20},{20... | collective-permute-start | bytes 294920 | tf_op jit(solution)/shard_map/ppermute | solution.py:346
  76.7 1.5 collective-permute-start.5
  100.5 1.4 collective-permute-start.6
  106.9 4.9 %collective-permute-start.7 = (f32[64,384]{1,0:T(8,128)S(1)}, f32[64,384]{1,0:T(8,128)S(1)}, u32[]{:S(2)}, u32[]{:S(2)}) collective-permute-start(f32[64,384]{1,0:T(8,128)S(1)} %adjoint.4.a_ref), channel_id=1, source_target_pairs={{0,16},{16,0},{1,17},{17,1},{2,18},{18,2},{3,19},{19,3},{4,20},{20... | collective-permute-start | bytes 294920 | tf_op jit(solution)/shard_map/ppermute | solution.py:346
  128.0 1.5 collective-permute-start.8
  151.8 1.4 collective-permute-start.9
  158.3 4.9 %collective-permute-start.10 = (f32[64,384]{1,0:T(8,128)S(1)}, f32[64,384]{1,0:T(8,128)S(1)}, u32[]{:S(2)}, u32[]{:S(2)}) collective-permute-start(f32[64,384]{1,0:T(8,128)S(1)} %adjoint.5.a_ref), channel_id=1, source_target_pairs={{0,16},{16,0},{1,17},{17,1},{2,18},{18,2},{3,19},{19,3},{4,20},{20... | collective-permute-start | bytes 294920 | tf_op jit(solution)/shard_map/ppermute | solution.py:346

commit v7 on v6

--- a/solution.py
+++ b/solution.py
@@ -55,16 +55,17 @@
     return mm(a[0], b[0], dims) + (mm(a[0], b[1], dims) + mm(a[1], b[0], dims))
 
 
-def relayout_body(k_hbm, out_ref, buf, stage, sem):
+def relayout_body(cores, k_hbm, out_ref, buf, stage, sem):
     freqs = k_hbm.shape[3]
     pairs = freqs // 2
     steps = k_hbm.shape[1] // ROWS
+    chips = steps // cores
     same = lax.broadcasted_iota(jnp.int32, (LANES, LANES), 0) == lax.broadcasted_iota(jnp.int32, (LANES, LANES), 1)
     eye = same.astype(f32).astype(bf16)
 
     def copies(i):
         slot = lax.rem(i, BUFFERS)
-        rows = pl.ds(i * ROWS, ROWS)
+        rows = pl.ds((lax.rem(i, chips) * cores + lax.div(i, chips)) * ROWS, ROWS)
         return [pltpu.make_async_copy(k_hbm.at[c, rows], buf.at[slot, c], sem.at[slot, c]) for c in range(2)]
 
     def start(i):
@@ -101,10 +102,10 @@
     lax.fori_loop(0, steps, step, 0)
 
 
-def relayout(kernel):
+def relayout(kernel, cores):
     _, sensors, sources, freqs = kernel.shape
     return pl.pallas_call(
-        relayout_body,
+        functools.partial(relayout_body, cores),
         in_specs=[pl.BlockSpec(memory_space=pl.ANY)],
         out_specs=VM,
         out_shape=pltpu.VMEM((2, freqs // 2, sensors, 2 * sources), bf16),
@@ -178,8 +179,8 @@
     spectrum = jnp.concatenate(halves, axis=0).T
     terms[...] = mm3(split(spectrum), (t_ref[0], t_ref[1]), NN).reshape(terms.shape)
     core = lax.axis_index("core")
-    keep_ref[...] = terms[:, core]
-    send_ref[...] = terms[:, terms.shape[1] - 1 - core]
+    keep_ref[...] = terms[core]
+    send_ref[...] = terms[1 - core]
 
 
 def forward_first_body(k_ref, mine_ref, other_ref, rig_mine_ref, rig_other_ref, t_ref, new_ref, rig_ref, keep_ref, send_ref, lhs, res, terms, both, scales):
@@ -216,7 +217,7 @@
     scratch = [
         pltpu.VMEM((pairs * 8, LANES), f32),
         pltpu.VMEM((2, pairs * 8, LANES), f32),
-        pltpu.VMEM((chips, cores, rows, length), f32),
+        pltpu.VMEM((cores, chips, rows, length), f32),
     ]
     return outs, scratch
 
@@ -241,23 +242,25 @@
     )(k2, param, gradient, sums, scale_rows, table)
 
 
-def misfit_body(parts_ref, obs_ref, m_ref, spread_ref):
+def misfit_body(parts_ref, obs_ref, spread_ref, m_ref=None):
     chips, rows, _ = parts_ref.shape
     first = (lax.axis_index("chip") * lax.axis_size("core") + lax.axis_index("core")) * rows
     total = parts_ref[0]
     for c in range(1, chips):
         total = total + parts_ref[c]
     misfit = total - obs_ref[pl.ds(pl.multiple_of(first, 8), rows), :]
-    m_ref[...] = misfit
     for c in range(chips):
         spread_ref[c] = misfit
+    if m_ref is not None:
+        m_ref[...] = misfit
 
 
 def misfit_and_spread(parts, observed, last):
-    space = jax.ShapeDtypeStruct if last else pltpu.VMEM
-    return pl.pallas_call(
-        misfit_body, in_specs=[VM] * 2, out_specs=[VM] * 2,
-        out_shape=[space(parts.shape[1:], f32), jax.ShapeDtypeStruct(parts.shape, f32)],
+    outs = [jax.ShapeDtypeStruct(parts.shape, f32)]
+    if last:
+        outs.append(jax.ShapeDtypeStruct(parts.shape[1:], f32))
+    return pl.pallas_call(
+        misfit_body, in_specs=[VM] * 2, out_specs=[VM] * len(outs), out_shape=outs,
         compiler_params=params(4), name="misfit",
     )(parts, observed)
 
@@ -276,13 +279,12 @@
     )(param, gradient, sums)
 
 
-def adjoint_body(k_ref, mine_ref, other_ref, t_ref, o_ref, lhs, res, full):
-    freqs, sources = t_ref.shape[2], k_ref.shape[3] // 2
-    core = lax.axis_index("core")
-    full[:, core] = mine_ref[...]
-    full[:, full.shape[1] - 1 - core] = other_ref[...]
-    misfit = full[...].reshape(k_ref.shape[2], freqs)
-    spectrum = mm3((t_ref[0], t_ref[1]), split(misfit), NT)
+def adjoint_half(core, m_ref, k_ref, t_ref, lhs, store):
+    freqs = t_ref.shape[2]
+    sensors = k_ref.shape[2] // 2
+    high, rest = split(m_ref[...].reshape(sensors, freqs))
+    both = mm(t_ref[0], jnp.concatenate([high, rest], axis=0), NT)
+    spectrum = both[:, :LANES] + (both[:, LANES:] + mm(t_ref[1], high, NT))
     w = row_weights(freqs)
     for m in range(2):
         x = spectrum[m * freqs:(m + 1) * freqs] * w
@@ -291,15 +293,31 @@
             for chunk in range(freqs // LANES):
                 for h in range(2):
                     first = chunk * LANES + h * HALF
-                    for c in range(2):
-                        lhs[c, pair_row(chunk, h, 2 * n + m), :] = v[first:first + HALF, c * LANES:(c + 1) * LANES]
+                    lhs[pair_row(chunk, h, 2 * n + m), :] = v[first:first + HALF]
+    own = pl.ds(pl.multiple_of(core * sensors, LANES), sensors)
 
     def body(u, pair, rows, first):
-        a = jnp.concatenate([lhs[0, rows, :], lhs[1, rows, :]], axis=1).astype(bf16)
-        o = mm(a, tile(k_ref, pair), NN)
-        res[rows, :] = jnp.where(first, o[:, :LANES], o[:, LANES:])
+        k = jnp.concatenate([k_ref[0, pair, own, :], k_ref[1, pair, own, :]], axis=1)
+        o = mm(lhs[rows, :].astype(bf16), k, NN)
+        store(rows, jnp.where(first, o[:, :LANES], o[:, LANES:]))
 
     each_pair(k_ref.shape[1], body)
+
+
+def adjoint_mine_body(k_ref, m_ref, t_ref, part_ref, lhs):
+    def store(rows, value):
+        part_ref[rows, :] = value
+
+    adjoint_half(lax.axis_index("core"), m_ref, k_ref, t_ref, lhs, store)
+
+
+def adjoint_other_body(k_ref, m_ref, part_ref, t_ref, o_ref, lhs, res):
+    freqs, sources = t_ref.shape[2], k_ref.shape[3] // 2
+
+    def store(rows, value):
+        res[rows, :] = part_ref[rows, :] + value
+
+    adjoint_half(1 - lax.axis_index("core"), m_ref, k_ref, t_ref, lhs, store)
     low = lax.broadcasted_iota(jnp.int32, (HALF, LANES), 1) < sources
     parts = []
     for chunk in range(freqs // LANES):
@@ -312,19 +330,25 @@
     )
 
 
-def adjoint(k2, mine, other, table):
+def adjoint_mine(k2, mine, table):
     _, pairs, sensors, width = k2.shape
-    chips, rows, length = mine.shape
-    return pl.pallas_call(
-        adjoint_body, in_specs=[VM] * 4, out_specs=VM,
-        out_shape=jax.ShapeDtypeStruct((width // 2, length), f32),
-        scratch_shapes=[
-            pltpu.VMEM((2, pairs * 8, LANES), f32),
-            pltpu.VMEM((pairs * 8, LANES), f32),
-            pltpu.VMEM((chips, sensors // (chips * rows), rows, length), f32),
-        ],
-        compiler_params=params(12), name="adjoint",
-    )(k2, mine, other, table)
+    spent = pl.CostEstimate(flops=16 * pairs * sensors * width, bytes_accessed=2 * pairs * sensors * width, transcendentals=0)
+    return pl.pallas_call(
+        adjoint_mine_body, in_specs=[VM] * 3, out_specs=VM,
+        out_shape=pltpu.VMEM((pairs * 8, LANES), f32),
+        scratch_shapes=[pltpu.VMEM((pairs * 8, LANES), f32)],
+        cost_estimate=spent, compiler_params=params(8), name="adjoint_mine",
+    )(k2, mine, table)
+
+
+def adjoint_other(k2, other, part, table):
+    _, pairs, _, width = k2.shape
+    return pl.pallas_call(
+        adjoint_other_body, in_specs=[VM] * 4, out_specs=VM,
+        out_shape=jax.ShapeDtypeStruct((width // 2, table.shape[2]), f32),
+        scratch_shapes=[pltpu.VMEM((pairs * 8, LANES), f32), pltpu.VMEM((pairs * 8, LANES), f32)],
+        compiler_params=params(8), name="adjoint_other",
+    )(k2, other, part, table)
 
 
 def gradient_body(a_ref, b_ref, p_ref, rig_ref, g_ref, q_ref):
@@ -405,17 +429,18 @@
     table = table_parts(slip_param.shape[1])
     scales = rigidity.reshape(1, -1)
     others, other_scales = swap(slip_param, "sens"), swap(scales, "sens")
-    k2 = relayout(kernel)
+    k2 = relayout(kernel, cores)
     param, scale_rows, keep, send = forward_first(k2, slip_param, others, scales, other_scales, table, chips, cores)
     for iteration in range(ITERS):
         if iteration:
             param, keep, send = forward_next(k2, param, gradient, sums, scale_rows, table, chips, cores, entries)
-        misfit, spread = misfit_and_spread(to_chips(keep + swap(send, "core")), observed, iteration == ITERS - 1)
+        spread, *misfit = misfit_and_spread(to_chips(keep + swap(send, "core")), observed, iteration == ITERS - 1)
         near = to_chips(spread)
-        back = adjoint(k2, near, swap(near, "core"), table)
+        far = swap(near, "core")
+        back = adjoint_other(k2, far, adjoint_mine(k2, near, table), table)
         gradient, sums = gradient_and_square(back, swap(back, "sens"), param, scale_rows, chips * cores)
         sums = exchange_scalars(sums)
-    return finish(param, gradient, sums, entries), misfit
+    return finish(param, gradient, sums, entries), misfit[0]
 
 
 def local(slip_param, rigidity, kernel, observed):
@@ -425,7 +450,7 @@
     entries = own_sources * sens * chips * cores * length
     fits = (
         sens == 2 and cores == 2 and kernel.shape[2] == HALF and kernel.shape[1] == 2 * LANES
-        and length % LANES == 0 and (length // 2) % UNROLL == 0 and own_count % 8 == 0
+        and length % LANES == 0 and (length // 2) % UNROLL == 0 and own_count == ROWS
     )
     run = iterations if fits else plain_iterations
     return run(slip_param, rigidity, kernel, observed, entries)

time: 174 us -> 171 us (0.983)
  waiting for transfers between devices: 18.7 us -> 15.5 us
    ppermute x11, waiting for transfers between devices: 18.7 us -> 15.5 us  [swap(): return lax.ppermute(x, axis, [(0, 1), (1, 0)])]
    pallas_call x7 -> x10, Pallas kernels: 28.5 us -> 29 us  [the longest x1 11.5 us: relayout(): pl.pallas_call(functools.partial(relayout_body, cores), in_specs=[pl.Bloc...]
  transfers between devices with their start and end apart: 11 -> 11, of which waited for: 9 -> 6; matrix products, arithmetic and copies ran while one was open for 0% -> 0% of each run, Pallas kernels for 7% -> 11%
where the time goes in v7:
time: 171 us
  blocking collectives  96.7 us (57%)
  Pallas kernels  49.9 us (29%)
  waiting for transfers between devices  15.5 us (9%)
  starting transfers between devices  8 us (5%)
    all_to_all x6, blocking collectives, to_chips(): return lax.all_to_all(x, 'chip', 0, 0)  68.4 us
    all_to_all x3, blocking collectives, exchange_scalars(): return lax.all_to_all(sums, ('chip', 'core'), 0, 0, tiled=True)  28.3 us
    ppermute x11, waiting for transfers between devices, swap(): return lax.ppermute(x, axis, [(0, 1), (1, 0)])  15.5 us
    pallas_call x2, Pallas kernels, forward_next(): pl.pallas_call(functools.partial(forward_next_body, entries), in_specs=[V...  13.1 us
    pallas_call x1, Pallas kernels, relayout(): pl.pallas_call(functools.partial(relayout_body, cores), in_specs=[pl.Bloc...  11.5 us
    pallas_call x3, Pallas kernels, adjoint_other(): pl.pallas_call(adjoint_other_body, in_specs=[VM] * 4, out_specs=VM, out_s...  9.27 us
    ppermute x11, starting transfers between devices, swap(): return lax.ppermute(x, axis, [(0, 1), (1, 0)])  8 us
    pallas_call x3, Pallas kernels, adjoint_mine(): pl.pallas_call(adjoint_mine_body, in_specs=[VM] * 3, out_specs=VM, out_sh...  7.54 us
  transfers between devices with their start and end apart: 11, of which 6 were waited for; matrix products, arithmetic and copies ran while one was open for 0% of the time, Pallas kernels for 11%

profile of v7, /device:TPU:0, one launch (start us, length us, event | category | flops | bytes accessed | tf_op | source)
XLA Modules:
  0.0 171.0 jit_solution(8315122293892090075)
XLA Ops:
  0.6 3.0 %collective-permute-start = (f32[32,384]{1,0:T(8,128)}, f32[32,384]{1,0:T(8,128)S(1)}, u32[]{:S(2)}, u32[]{:S(2)}) collective-permute-start(f32[32,384]{1,0:T(8,128)} %mine_ref.1), channel_id=1, source_target_pairs={{0,16},{16,0},{1,17},{17,1},{2,18},{18,2},{3,19},{19,3},{4,20},{20... | collective-permute-start | bytes 147464 | tf_op jit(solution)/shard_map/ppermute | solution.py:370
  3.8 11.5 %relayout.1.k_ref = bf16[2,192,256,128]{3,2,1,0:T(8,128)(2,1)S(1)} custom-call(bf16[2,256,64,384]{3,2,1,0:T(8,128)(2,1)} %k_hbm.1), custom_call_target="tpu_custom_call" | custom-call | tf_op jit(solution)/shard_map/relayout/pallas_call | solution.py:107
  15.4 6.6 %forward_first.1 = (f32[64,384]{1,0:T(8,128)S(1)}, f32[64,128]{1,0:T(8,128)S(1)}, f32[8,16,384]{2,1,0:T(8,128)S(1)}, f32[8,16,384]{2,1,0:T(8,128)S(1)}) custom-call(bf16[2,192,256,128]{3,2,1,0:T(8,128)(2,1)S(1)} %relayout.1.k_ref, f32[32,384]{1,0:T(8,128)S(1)} %copy-done.2, f32[32,384]{1,0:T(8,128)S(1)} %collective-permute-done.other_ref, ...), custom_call_target="tpu_custom_call" | custom-call | tf_op jit(solution)/shard_map/forward_first/pallas_call | solution.py:228
  22.0 1.4 collective-permute-done.2
  23.5 14.3 %all_to_all.63.parts_ref = f32[8,16,384]{2,1,0:T(8,128)S(1)} all-to-all(f32[8,16,384]{2,1,0:T(8,128)S(1)} %add.9), channel_id=1, replica_groups=mesh['sens'=2,'chip'=8,'core'=2] {'chip'}, dimensions={0} | all-to-all | bytes 393216 | tf_op jit(solution)/shard_map/all_to_all | solution.py:374
  37.8 10.7 %all_to_all.64.m_ref = f32[8,16,384]{2,1,0:T(8,128)S(1)} all-to-all(f32[8,16,384]{2,1,0:T(8,128)S(1)} %misfit.3), channel_id=1, replica_groups=mesh['sens'=2,'chip'=8,'core'=2] {'chip'}, dimensions={0} | all-to-all | bytes 393216 | tf_op jit(solution)/shard_map/all_to_all | solution.py:374
  48.5 2.5 %adjoint_mine.3.part_ref = f32[1536,128]{1,0:T(8,128)S(1)} custom-call(bf16[2,192,256,128]{3,2,1,0:T(8,128)(2,1)S(1)} %relayout.1.k_ref, f32[8,16,384]{2,1,0:T(8,128)S(1)} %all_to_all.64.m_ref, bf16[2,768,384]{2,1,0:T(8,128)(2,1)S(1)} %copy-done), custom_call_target="tpu_custom_call" | custom-call | flops 100663296 | bytes 12582912 | tf_op jit(solution)/shard_map/adjoint_mine/pallas_call | solution.py:336
  51.0 3.1 %adjoint_other.3.a_ref = f32[64,384]{1,0:T(8,128)S(1)} custom-call(bf16[2,192,256,128]{3,2,1,0:T(8,128)(2,1)S(1)} %relayout.1.k_ref, f32[8,16,384]{2,1,0:T(8,128)S(1)} %collective-permute-done.3.m_ref, f32[1536,128]{1,0:T(8,128)S(1)} %adjoint_mine.3.part_ref, bf16[2,768,384]{2,1,0:T(8,128)(2,1)S(1)} %copy-done), custom_call_target="tpu_custom_call" | custom-call | tf_op jit(solution)/shard_map/adjoint_other/pallas_call | solution.py:346
  54.1 1.5 collective-permute-start.4
  55.7 3.7 %collective-permute-done.4.b_ref = f32[64,384]{1,0:T(8,128)S(1)} collective-permute-done((f32[64,384]{1,0:T(8,128)S(1)}, f32[64,384]{1,0:T(8,128)S(1)}, u32[]{:S(2)}, u32[]{:S(2)}) %collective-permute-start.4) | collective-permute-done | bytes 98336 | tf_op jit(solution)/shard_map/ppermute | solution.py:370
  59.6 9.4 %all_to_all.65 = f32[16,1,128]{2,1,0:T(1,128)S(1)} all-to-all(f32[16,1,128]{2,1,0:T(1,128)S(1)} %bitcast.17), channel_id=1, replica_groups=mesh['sens'=2,'chip'=8,'core'=2] {'chip','core'}, dimensions={0} | all-to-all | bytes 16384 | tf_op jit(solution)/shard_map/all_to_all | solution.py:378
  69.0 6.6 %forward_next.2 = (f32[64,384]{1,0:T(8,128)S(1)}, f32[8,16,384]{2,1,0:T(8,128)S(1)}, f32[8,16,384]{2,1,0:T(8,128)S(1)}) custom-call(bf16[2,192,256,128]{3,2,1,0:T(8,128)(2,1)S(1)} %relayout.1.k_ref, f32[64,384]{1,0:T(8,128)S(1)} %get-tuple-element.20.p_ref, f32[64,384]{1,0:T(8,128)S(1)} %get-tuple-element.24.g_ref, f32[16,128]{1,0:T(8,128)S(1)} %bitcast.13, ...), custom_call_target="tpu_custom_call" | custom-call | tf_op jit(solution)/shard_map/forward_next/pallas_call | solution.py:238
  75.6 1.4 collective-permute-done.5
  77.1 10.9 %all_to_all.66.parts_ref = f32[8,16,384]{2,1,0:T(8,128)S(1)} all-to-all(f32[8,16,384]{2,1,0:T(8,128)S(1)} %add.10), channel_id=1, replica_groups=mesh['sens'=2,'chip'=8,'core'=2] {'chip'}, dimensions={0} | all-to-all | bytes 393216 | tf_op jit(solution)/shard_map/all_to_all | solution.py:374
  88.0 10.7 %all_to_all.67.m_ref = f32[8,16,384]{2,1,0:T(8,128)S(1)} all-to-all(f32[8,16,384]{2,1,0:T(8,128)S(1)} %misfit.4), channel_id=1, replica_groups=mesh['sens'=2,'chip'=8,'core'=2] {'chip'}, dimensions={0} | all-to-all | bytes 393216 | tf_op jit(solution)/shard_map/all_to_all | solution.py:374
  98.8 2.5 %adjoint_mine.4.part_ref = f32[1536,128]{1,0:T(8,128)S(1)} custom-call(bf16[2,192,256,128]{3,2,1,0:T(8,128)(2,1)S(1)} %relayout.1.k_ref, f32[8,16,384]{2,1,0:T(8,128)S(1)} %all_to_all.67.m_ref, bf16[2,768,384]{2,1,0:T(8,128)(2,1)S(1)} %copy-done), custom_call_target="tpu_custom_call" | custom-call | flops 100663296 | bytes 12582912 | tf_op jit(solution)/shard_map/adjoint_mine/pallas_call | solution.py:336
  101.3 3.1 %adjoint_other.4.a_ref = f32[64,384]{1,0:T(8,128)S(1)} custom-call(bf16[2,192,256,128]{3,2,1,0:T(8,128)(2,1)S(1)} %relayout.1.k_ref, f32[8,16,384]{2,1,0:T(8,128)S(1)} %collective-permute-done.6.m_ref, f32[1536,128]{1,0:T(8,128)S(1)} %adjoint_mine.4.part_ref, bf16[2,768,384]{2,1,0:T(8,128)(2,1)S(1)} %copy-done), custom_call_target="tpu_custom_call" | custom-call | tf_op jit(solution)/shard_map/adjoint_other/pallas_call | solution.py:346
  104.4 1.5 collective-permute-start.7
  105.9 3.7 %collective-permute-done.7.b_ref = f32[64,384]{1,0:T(8,128)S(1)} collective-permute-done((f32[64,384]{1,0:T(8,128)S(1)}, f32[64,384]{1,0:T(8,128)S(1)}, u32[]{:S(2)}, u32[]{:S(2)}) %collective-permute-start.7) | collective-permute-done | bytes 98336 | tf_op jit(solution)/shard_map/ppermute | solution.py:370
  109.8 9.4 %all_to_all.68 = f32[16,1,128]{2,1,0:T(1,128)S(1)} all-to-all(f32[16,1,128]{2,1,0:T(1,128)S(1)} %bitcast.18), channel_id=1, replica_groups=mesh['sens'=2,'chip'=8,'core'=2] {'chip','core'}, dimensions={0} | all-to-all | bytes 16384 | tf_op jit(solution)/shard_map/all_to_all | solution.py:378
  119.2 6.6 %forward_next.3 = (f32[64,384]{1,0:T(8,128)S(1)}, f32[8,16,384]{2,1,0:T(8,128)S(1)}, f32[8,16,384]{2,1,0:T(8,128)S(1)}) custom-call(bf16[2,192,256,128]{3,2,1,0:T(8,128)(2,1)S(1)} %relayout.1.k_ref, f32[64,384]{1,0:T(8,128)S(1)} %get-tuple-element.26.p_ref, f32[64,384]{1,0:T(8,128)S(1)} %get-tuple-element.29.g_ref, f32[16,128]{1,0:T(8,128)S(1)} %bitcast.14, ...), custom_call_target="tpu_custom_call" | custom-call | tf_op jit(solution)/shard_map/forward_next/pallas_call | solution.py:238
  125.9 1.4 collective-permute-done.8
  127.3 10.9 %all_to_all.69.parts_ref = f32[8,16,384]{2,1,0:T(8,128)S(1)} all-to-all(f32[8,16,384]{2,1,0:T(8,128)S(1)} %add.11), channel_id=1, replica_groups=mesh['sens'=2,'chip'=8,'core'=2] {'chip'}, dimensions={0} | all-to-all | bytes 393216 | tf_op jit(solution)/shard_map/all_to_all | solution.py:374
  138.3 0.6 misfit.5
  138.9 10.8 %all_to_all.70.m_ref = f32[8,16,384]{2,1,0:T(8,128)S(1)} all-to-all(f32[8,16,384]{2,1,0:T(8,128)S(1)} %get-tuple-element.34), channel_id=1, replica_groups=mesh['sens'=2,'chip'=8,'core'=2] {'chip'}, dimensions={0} | all-to-all | bytes 393216 | tf_op jit(solution)/shard_map/all_to_all | solution.py:374
  149.7 2.5 %adjoint_mine.5.part_ref = f32[1536,128]{1,0:T(8,128)S(1)} custom-call(bf16[2,192,256,128]{3,2,1,0:T(8,128)(2,1)S(1)} %relayout.1.k_ref, f32[8,16,384]{2,1,0:T(8,128)S(1)} %all_to_all.70.m_ref, bf16[2,768,384]{2,1,0:T(8,128)(2,1)S(1)} %copy-done), custom_call_target="tpu_custom_call" | custom-call | flops 100663296 | bytes 12582912 | tf_op jit(solution)/shard_map/adjoint_mine/pallas_call | solution.py:336
  152.3 3.1 %adjoint_other.5.a_ref = f32[64,384]{1,0:T(8,128)S(1)} custom-call(bf16[2,192,256,128]{3,2,1,0:T(8,128)(2,1)S(1)} %relayout.1.k_ref, f32[8,16,384]{2,1,0:T(8,128)S(1)} %collective-permute-done.9.m_ref, f32[1536,128]{1,0:T(8,128)S(1)} %adjoint_mine.5.part_ref, bf16[2,768,384]{2,1,0:T(8,128)(2,1)S(1)} %copy-done), custom_call_target="tpu_custom_call" | custom-call | tf_op jit(solution)/shard_map/adjoint_other/pallas_call | solution.py:346
  155.4 1.5 collective-permute-start.10
  156.9 3.7 %collective-permute-done.10.b_ref = f32[64,384]{1,0:T(8,128)S(1)} collective-permute-done((f32[64,384]{1,0:T(8,128)S(1)}, f32[64,384]{1,0:T(8,128)S(1)}, u32[]{:S(2)}, u32[]{:S(2)}) %collective-permute-start.10) | collective-permute-done | bytes 98336 | tf_op jit(solution)/shard_map/ppermute | solution.py:370
  160.6 0.2 gradient.5
  160.8 9.5 %all_to_all.71 = f32[16,1,128]{2,1,0:T(1,128)S(1)} all-to-all(f32[16,1,128]{2,1,0:T(1,128)S(1)} %bitcast.16), channel_id=1, replica_groups=mesh['sens'=2,'chip'=8,'core'=2] {'chip','core'}, dimensions={0} | all-to-all | bytes 16384 | tf_op jit(solution)/shard_map/all_to_all | solution.py:378
  170.3 0.7 finish.1
  (27 shorter events, 0.8 us)
Async XLA Ops:
  0.6 14.7 %collective-permute-start = (f32[32,384]{1,0:T(8,128)}, f32[32,384]{1,0:T(8,128)S(1)}, u32[]{:S(2)}, u32[]{:S(2)}) collective-permute-start(f32[32,384]{1,0:T(8,128)} %mine_ref.1), channel_id=1, source_target_pairs={{0,16},{16,0},{1,17},{17,1},{2,18},{18,2},{3,19},{19,3},{4,20},{20... | collective-permute-start | bytes 147464 | tf_op jit(solution)/shard_map/ppermute | solution.py:370
  3.7 11.7 %copy-start = (bf16[2,768,384]{2,1,0:T(8,128)(2,1)S(1)}, bf16[2,768,384]{2,1,0:T(8,128)(2,1)}, u32[]{:S(2)}) copy-start(bf16[2,768,384]{2,1,0:T(8,128)(2,1)} %constant.2.clone.t_ref) | copy-start | bytes 3538948
  3.7 11.7 %copy-start.2 = (f32[32,384]{1,0:T(8,128)S(1)}, f32[32,384]{1,0:T(8,128)}, u32[]{:S(2)}) copy-start(f32[32,384]{1,0:T(8,128)} %mine_ref.1) | copy-start | bytes 147460
  3.7 11.7 %copy-start.3 = (f32[32]{0:T(128)S(1)}, f32[32]{0:T(128)}, u32[]{:S(2)}) copy-start(f32[32]{0:T(128)} %param.6) | copy-start | bytes 388
  3.7 11.7 %collective-permute-start.1 = (f32[1,32]{1,0:T(1,128)}, f32[1,32]{1,0:T(1,128)S(1)}, u32[]{:S(2)}, u32[]{:S(2)}) collective-permute-start(f32[1,32]{1,0:T(1,128)} %bitcast.19), channel_id=1, source_target_pairs={{0,16},{16,0},{1,17},{17,1},{2,18},{18,2},{3,19},{19,3},{4,20},{20... | collective-permute-start | bytes 392 | tf_op jit(solution)/shard_map/ppermute | solution.py:370
  15.3 22.4 %copy-start.1 = (f32[256,384]{1,0:T(8,128)S(1)}, f32[256,384]{1,0:T(8,128)}, u32[]{:S(2)}) copy-start(f32[256,384]{1,0:T(8,128)} %obs_ref.5) | copy-start | bytes 1179652
  22.0 1.5 collective-permute-start.2
  48.5 2.5 %collective-permute-start.3 = (f32[8,16,384]{2,1,0:T(8,128)S(1)}, f32[8,16,384]{2,1,0:T(8,128)S(1)}, u32[]{:S(2)}, u32[]{:S(2)}) collective-permute-start(f32[8,16,384]{2,1,0:T(8,128)S(1)} %all_to_all.64.m_ref), channel_id=1, source_target_pairs={{0,1},{1,0},{2,3},{3,2},{4,5},{5,4},{6,7},{7,6},{8,9},{9,8},{10,11... | collective-permute-start | bytes 589832 | tf_op jit(solution)/shard_map/ppermute | solution.py:370
  54.1 5.3 %collective-permute-start.4 = (f32[64,384]{1,0:T(8,128)S(1)}, f32[64,384]{1,0:T(8,128)S(1)}, u32[]{:S(2)}, u32[]{:S(2)}) collective-permute-start(f32[64,384]{1,0:T(8,128)S(1)} %adjoint_other.3.a_ref), channel_id=1, source_target_pairs={{0,16},{16,0},{1,17},{17,1},{2,18},{18,2},{3,19},{19,3},{4,20},{20... | collective-permute-start | bytes 294920 | tf_op jit(solution)/shard_map/ppermute | solution.py:370
  75.5 1.5 collective-permute-start.5
  98.8 2.5 %collective-permute-start.6 = (f32[8,16,384]{2,1,0:T(8,128)S(1)}, f32[8,16,384]{2,1,0:T(8,128)S(1)}, u32[]{:S(2)}, u32[]{:S(2)}) collective-permute-start(f32[8,16,384]{2,1,0:T(8,128)S(1)} %all_to_all.67.m_ref), channel_id=1, source_target_pairs={{0,1},{1,0},{2,3},{3,2},{4,5},{5,4},{6,7},{7,6},{8,9},{9,8},{10,11... | collective-permute-start | bytes 589832 | tf_op jit(solution)/shard_map/ppermute | solution.py:370
  104.4 5.3 %collective-permute-start.7 = (f32[64,384]{1,0:T(8,128)S(1)}, f32[64,384]{1,0:T(8,128)S(1)}, u32[]{:S(2)}, u32[]{:S(2)}) collective-permute-start(f32[64,384]{1,0:T(8,128)S(1)} %adjoint_other.4.a_ref), channel_id=1, source_target_pairs={{0,16},{16,0},{1,17},{17,1},{2,18},{18,2},{3,19},{19,3},{4,20},{20... | collective-permute-start | bytes 294920 | tf_op jit(solution)/shard_map/ppermute | solution.py:370
  125.8 1.5 collective-permute-start.8
  149.7 2.5 %collective-permute-start.9 = (f32[8,16,384]{2,1,0:T(8,128)S(1)}, f32[8,16,384]{2,1,0:T(8,128)S(1)}, u32[]{:S(2)}, u32[]{:S(2)}) collective-permute-start(f32[8,16,384]{2,1,0:T(8,128)S(1)} %all_to_all.70.m_ref), channel_id=1, source_target_pairs={{0,1},{1,0},{2,3},{3,2},{4,5},{5,4},{6,7},{7,6},{8,9},{9,8},{10,11... | collective-permute-start | bytes 589832 | tf_op jit(solution)/shard_map/ppermute | solution.py:370
  155.4 5.3 %collective-permute-start.10 = (f32[64,384]{1,0:T(8,128)S(1)}, f32[64,384]{1,0:T(8,128)S(1)}, u32[]{:S(2)}, u32[]{:S(2)}) collective-permute-start(f32[64,384]{1,0:T(8,128)S(1)} %adjoint_other.5.a_ref), channel_id=1, source_target_pairs={{0,16},{16,0},{1,17},{17,1},{2,18},{18,2},{3,19},{19,3},{4,20},{20... | collective-permute-start | bytes 294920 | tf_op jit(solution)/shard_map/ppermute | solution.py:370

commit v8 on v7

--- a/solution.py
+++ b/solution.py
@@ -23,6 +23,7 @@
 PITCH = 196
 BUFFERS = 6
 UNROLL = 96
+ADJOINT_UNROLL = 64
 
 
 def table_parts(length):
@@ -132,19 +133,19 @@
     return jnp.concatenate([jnp.concatenate(row, axis=1) for row in blocks], axis=0)
 
 
-def each_pair(pairs, body):
+def each_pair(pairs, unroll, body):
     first = lax.broadcasted_iota(jnp.int32, (8, LANES), 0) < 4
 
     def step(i, carry):
-        for u in range(UNROLL):
-            pair = i * UNROLL + u
+        for u in range(unroll):
+            pair = i * unroll + u
             body(u, pair, pl.ds(pl.multiple_of(pair * 8, 8), 8), first)
         return carry
 
-    lax.fori_loop(0, pairs // UNROLL, step, 0)
-
-
-def forward_core(param, scale_rows, k_ref, t_ref, keep_ref, send_ref, lhs, res, terms):
+    lax.fori_loop(0, pairs // unroll, step, 0)
+
+
+def forward_core(param, scale_rows, k_ref, t_ref, res, send_ref, lhs):
     freqs, sources = param.shape[1], param.shape[0]
     high, rest = split(scale_rows * jax.nn.softplus(param))
     z = mm(t_ref[0], jnp.concatenate([high, high, rest, rest], axis=0), NT)
@@ -166,24 +167,37 @@
         res[0, rows, :] = o[:, :LANES]
         res[1, rows, :] = o[:, LANES:]
 
-    each_pair(k_ref.shape[1], body)
+    each_pair(k_ref.shape[1], UNROLL, body)
+    send_ref[...] = predicted(res, 1 - lax.axis_index("core"), t_ref).reshape(send_ref.shape)
+
+
+def predicted(res, core, t_ref):
+    freqs = t_ref.shape[2]
     w = row_weights(freqs)
     halves = []
     for m in range(2):
         parts = []
         for chunk in range(freqs // LANES):
             for h in range(2):
-                high, rest = pair_row(chunk, h, m), pair_row(chunk, h, 2 + m)
-                parts.append(jnp.concatenate([res[c, high, :] + res[c, rest, :] for c in range(2)], axis=1))
+                parts.append(res[core, pair_row(chunk, h, m), :] + res[core, pair_row(chunk, h, 2 + m), :])
         halves.append(jnp.concatenate(parts, axis=0) * w)
     spectrum = jnp.concatenate(halves, axis=0).T
-    terms[...] = mm3(split(spectrum), (t_ref[0], t_ref[1]), NN).reshape(terms.shape)
-    core = lax.axis_index("core")
-    keep_ref[...] = terms[core]
-    send_ref[...] = terms[1 - core]
-
-
-def forward_first_body(k_ref, mine_ref, other_ref, rig_mine_ref, rig_other_ref, t_ref, new_ref, rig_ref, keep_ref, send_ref, lhs, res, terms, both, scales):
+    return mm3(split(spectrum), (t_ref[0], t_ref[1]), NN)
+
+
+def keep_body(res_ref, t_ref, keep_ref):
+    keep_ref[...] = predicted(res_ref, lax.axis_index("core"), t_ref).reshape(keep_ref.shape)
+
+
+def kept_terms(res, send, table):
+    spent = pl.CostEstimate(flops=12 * res.size * table.shape[2], bytes_accessed=8 * res.size, transcendentals=0)
+    return pl.pallas_call(
+        keep_body, in_specs=[VM] * 2, out_specs=VM, out_shape=jax.ShapeDtypeStruct(send.shape, f32),
+        cost_estimate=spent, compiler_params=params(4), name="keep",
+    )(res, table)
+
+
+def forward_first_body(k_ref, mine_ref, other_ref, rig_mine_ref, rig_other_ref, t_ref, new_ref, rig_ref, res, send_ref, lhs, both, scales):
     sens = lax.axis_index("sens")
     rows = mine_ref.shape[0]
     same = lax.broadcasted_iota(jnp.int32, (rows, rows), 0) == lax.broadcasted_iota(jnp.int32, (rows, rows), 1)
@@ -195,7 +209,7 @@
     scale_rows = scales[...].reshape(rig_ref.shape)
     new_ref[...] = param
     rig_ref[...] = scale_rows
-    forward_core(param, scale_rows[:, 0:1], k_ref, t_ref, keep_ref, send_ref, lhs, res, terms)
+    forward_core(param, scale_rows[:, 0:1], k_ref, t_ref, res, send_ref, lhs)
 
 
 def moved(param, gradient, sums, entries):
@@ -204,21 +218,17 @@
     return param - step_rate * gradient / root_mean
 
 
-def forward_next_body(entries, k_ref, p_ref, g_ref, q_ref, rig_ref, t_ref, new_ref, keep_ref, send_ref, lhs, res, terms):
+def forward_next_body(entries, k_ref, p_ref, g_ref, q_ref, rig_ref, t_ref, new_ref, res, send_ref, lhs):
     param = moved(p_ref[...], g_ref[...], q_ref[...], entries)
     new_ref[...] = param
-    forward_core(param, rig_ref[:, 0:1], k_ref, t_ref, keep_ref, send_ref, lhs, res, terms)
+    forward_core(param, rig_ref[:, 0:1], k_ref, t_ref, res, send_ref, lhs)
 
 
 def forward_spaces(k2, length, chips, cores):
     _, pairs, sensors, _ = k2.shape
     rows = sensors // (chips * cores)
-    outs = [jax.ShapeDtypeStruct((chips, rows, length), f32)] * 2
-    scratch = [
-        pltpu.VMEM((pairs * 8, LANES), f32),
-        pltpu.VMEM((2, pairs * 8, LANES), f32),
-        pltpu.VMEM((cores, chips, rows, length), f32),
-    ]
+    outs = [pltpu.VMEM((2, pairs * 8, LANES), f32), jax.ShapeDtypeStruct((chips, rows, length), f32)]
+    scratch = [pltpu.VMEM((pairs * 8, LANES), f32)]
     return outs, scratch
 
 
@@ -301,7 +311,7 @@
         o = mm(lhs[rows, :].astype(bf16), k, NN)
         store(rows, jnp.where(first, o[:, :LANES], o[:, LANES:]))
 
-    each_pair(k_ref.shape[1], body)
+    each_pair(k_ref.shape[1], ADJOINT_UNROLL, body)
 
 
 def adjoint_mine_body(k_ref, m_ref, t_ref, part_ref, lhs):
@@ -430,11 +440,11 @@
     scales = rigidity.reshape(1, -1)
     others, other_scales = swap(slip_param, "sens"), swap(scales, "sens")
     k2 = relayout(kernel, cores)
-    param, scale_rows, keep, send = forward_first(k2, slip_param, others, scales, other_scales, table, chips, cores)
+    param, scale_rows, res, send = forward_first(k2, slip_param, others, scales, other_scales, table, chips, cores)
     for iteration in range(ITERS):
         if iteration:
-            param, keep, send = forward_next(k2, param, gradient, sums, scale_rows, table, chips, cores, entries)
-        spread, *misfit = misfit_and_spread(to_chips(keep + swap(send, "core")), observed, iteration == ITERS - 1)
+            param, res, send = forward_next(k2, param, gradient, sums, scale_rows, table, chips, cores, entries)
+        spread, *misfit = misfit_and_spread(to_chips(kept_terms(res, send, table) + swap(send, "core")), observed, iteration == ITERS - 1)
         near = to_chips(spread)
         far = swap(near, "core")
         back = adjoint_other(k2, far, adjoint_mine(k2, near, table), table)
@@ -450,7 +460,7 @@
     entries = own_sources * sens * chips * cores * length
     fits = (
         sens == 2 and cores == 2 and kernel.shape[2] == HALF and kernel.shape[1] == 2 * LANES
-        and length % LANES == 0 and (length // 2) % UNROLL == 0 and own_count == ROWS
+        and length % LANES == 0 and (length // 2) % UNROLL == 0 and (length // 2) % ADJOINT_UNROLL == 0 and own_count == ROWS
     )
     run = iterations if fits else plain_iterations
     return run(slip_param, rigidity, kernel, observed, entries)

time: 171 us -> 170 us (level)
  waiting for transfers between devices: 15.5 us -> 13.7 us
    ppermute x11, waiting for transfers between devices: 15.5 us -> 13.7 us  [swap(): return lax.ppermute(x, axis, [(0, 1), (1, 0)])]
    pallas_call x0 -> x3, Pallas kernels: none -> 1.72 us  [kept_terms(): pl.pallas_call(keep_body, in_specs=[VM] * 2, out_specs=VM, out_shape=jax....]
  transfers between devices with their start and end apart: 11 -> 11, of which waited for: 6 -> 6; matrix products, arithmetic and copies ran while one was open for 0% -> 0% of each run, Pallas kernels for 11% -> 12%
where the time goes in v8:
time: 170 us
  blocking collectives  96.5 us (57%)
  Pallas kernels  50.9 us (30%)
  waiting for transfers between devices  13.7 us (8%)
  starting transfers between devices  8.02 us (5%)
    all_to_all x6, blocking collectives, to_chips(): return lax.all_to_all(x, 'chip', 0, 0)  68.3 us
    all_to_all x3, blocking collectives, exchange_scalars(): return lax.all_to_all(sums, ('chip', 'core'), 0, 0, tiled=True)  28.2 us
    ppermute x11, waiting for transfers between devices, swap(): return lax.ppermute(x, axis, [(0, 1), (1, 0)])  13.7 us
    pallas_call x2, Pallas kernels, forward_next(): pl.pallas_call(functools.partial(forward_next_body, entries), in_specs=[V...  12.1 us
    pallas_call x1, Pallas kernels, relayout(): pl.pallas_call(functools.partial(relayout_body, cores), in_specs=[pl.Bloc...  11.5 us
    pallas_call x3, Pallas kernels, adjoint_other(): pl.pallas_call(adjoint_other_body, in_specs=[VM] * 4, out_specs=VM, out_s...  9.62 us
    ppermute x11, starting transfers between devices, swap(): return lax.ppermute(x, axis, [(0, 1), (1, 0)])  8.02 us
    pallas_call x3, Pallas kernels, adjoint_mine(): pl.pallas_call(adjoint_mine_body, in_specs=[VM] * 3, out_specs=VM, out_sh...  7.88 us
  transfers between devices with their start and end apart: 11, of which 6 were waited for; matrix products, arithmetic and copies ran while one was open for 0% of the time, Pallas kernels for 12%

profile of v8, /device:TPU:0, one launch (start us, length us, event | category | flops | bytes accessed | tf_op | source)
XLA Modules:
  0.0 170.0 jit_solution(13572097559202589840)
XLA Ops:
  0.6 3.0 %collective-permute-start = (f32[32,384]{1,0:T(8,128)}, f32[32,384]{1,0:T(8,128)S(1)}, u32[]{:S(2)}, u32[]{:S(2)}) collective-permute-start(f32[32,384]{1,0:T(8,128)} %mine_ref.1), channel_id=1, source_target_pairs={{0,16},{16,0},{1,17},{17,1},{2,18},{18,2},{3,19},{19,3},{4,20},{20... | collective-permute-start | bytes 147464 | tf_op jit(solution)/shard_map/ppermute | solution.py:380
  3.8 11.5 %relayout.1.k_ref = bf16[2,192,256,128]{3,2,1,0:T(8,128)(2,1)S(1)} custom-call(bf16[2,256,64,384]{3,2,1,0:T(8,128)(2,1)} %k_hbm.1), custom_call_target="tpu_custom_call" | custom-call | tf_op jit(solution)/shard_map/relayout/pallas_call | solution.py:108
  15.4 6.1 %forward_first.1 = (f32[64,384]{1,0:T(8,128)S(1)}, f32[64,128]{1,0:T(8,128)S(1)}, f32[2,1536,128]{2,1,0:T(8,128)S(1)}, f32[8,16,384]{2,1,0:T(8,128)S(1)}) custom-call(bf16[2,192,256,128]{3,2,1,0:T(8,128)(2,1)S(1)} %relayout.1.k_ref, f32[32,384]{1,0:T(8,128)S(1)} %copy-done.2, f32[32,384]{1,0:T(8,128)S(1)} %collective-permute-done.other_ref, ...), custom_call_target="tpu_custom_call" | custom-call | tf_op jit(solution)/shard_map/forward_first/pallas_call | solution.py:238
  21.6 0.6 keep.3
  22.1 0.8 collective-permute-done.2
  23.0 14.3 %all_to_all.63.parts_ref = f32[8,16,384]{2,1,0:T(8,128)S(1)} all-to-all(f32[8,16,384]{2,1,0:T(8,128)S(1)} %add.9), channel_id=1, replica_groups=mesh['sens'=2,'chip'=8,'core'=2] {'chip'}, dimensions={0} | all-to-all | bytes 393216 | tf_op jit(solution)/shard_map/all_to_all | solution.py:384
  37.3 10.7 %all_to_all.64.m_ref = f32[8,16,384]{2,1,0:T(8,128)S(1)} all-to-all(f32[8,16,384]{2,1,0:T(8,128)S(1)} %misfit.3), channel_id=1, replica_groups=mesh['sens'=2,'chip'=8,'core'=2] {'chip'}, dimensions={0} | all-to-all | bytes 393216 | tf_op jit(solution)/shard_map/all_to_all | solution.py:384
  48.0 2.6 %adjoint_mine.3.part_ref = f32[1536,128]{1,0:T(8,128)S(1)} custom-call(bf16[2,192,256,128]{3,2,1,0:T(8,128)(2,1)S(1)} %relayout.1.k_ref, f32[8,16,384]{2,1,0:T(8,128)S(1)} %all_to_all.64.m_ref, bf16[2,768,384]{2,1,0:T(8,128)(2,1)S(1)} %copy-done), custom_call_target="tpu_custom_call" | custom-call | flops 100663296 | bytes 12582912 | tf_op jit(solution)/shard_map/adjoint_mine/pallas_call | solution.py:346
  50.7 3.2 %adjoint_other.3.a_ref = f32[64,384]{1,0:T(8,128)S(1)} custom-call(bf16[2,192,256,128]{3,2,1,0:T(8,128)(2,1)S(1)} %relayout.1.k_ref, f32[8,16,384]{2,1,0:T(8,128)S(1)} %collective-permute-done.3.m_ref, f32[1536,128]{1,0:T(8,128)S(1)} %adjoint_mine.3.part_ref, bf16[2,768,384]{2,1,0:T(8,128)(2,1)S(1)} %copy-done), custom_call_target="tpu_custom_call" | custom-call | tf_op jit(solution)/shard_map/adjoint_other/pallas_call | solution.py:356
  53.9 1.6 collective-permute-start.4
  55.4 3.7 %collective-permute-done.4.b_ref = f32[64,384]{1,0:T(8,128)S(1)} collective-permute-done((f32[64,384]{1,0:T(8,128)S(1)}, f32[64,384]{1,0:T(8,128)S(1)}, u32[]{:S(2)}, u32[]{:S(2)}) %collective-permute-start.4) | collective-permute-done | bytes 98336 | tf_op jit(solution)/shard_map/ppermute | solution.py:380
  59.3 9.4 %all_to_all.65 = f32[16,1,128]{2,1,0:T(1,128)S(1)} all-to-all(f32[16,1,128]{2,1,0:T(1,128)S(1)} %bitcast.17), channel_id=1, replica_groups=mesh['sens'=2,'chip'=8,'core'=2] {'chip','core'}, dimensions={0} | all-to-all | bytes 16384 | tf_op jit(solution)/shard_map/all_to_all | solution.py:388
  68.7 6.1 %forward_next.2 = (f32[64,384]{1,0:T(8,128)S(1)}, f32[2,1536,128]{2,1,0:T(8,128)S(1)}, f32[8,16,384]{2,1,0:T(8,128)S(1)}) custom-call(bf16[2,192,256,128]{3,2,1,0:T(8,128)(2,1)S(1)} %relayout.1.k_ref, f32[64,384]{1,0:T(8,128)S(1)} %get-tuple-element.20.p_ref, f32[64,384]{1,0:T(8,128)S(1)} %get-tuple-element.24.g_ref, f32[16,128]{1,0:T(8,128)S(1)} %bitcast.13, ...), custom_call_target="tpu_custom_call" | custom-call | tf_op jit(solution)/shard_map/forward_next/pallas_call | solution.py:248
  75.4 0.8 collective-permute-done.5
  76.3 10.9 %all_to_all.66.parts_ref = f32[8,16,384]{2,1,0:T(8,128)S(1)} all-to-all(f32[8,16,384]{2,1,0:T(8,128)S(1)} %add.10), channel_id=1, replica_groups=mesh['sens'=2,'chip'=8,'core'=2] {'chip'}, dimensions={0} | all-to-all | bytes 393216 | tf_op jit(solution)/shard_map/all_to_all | solution.py:384
  87.3 10.7 %all_to_all.67.m_ref = f32[8,16,384]{2,1,0:T(8,128)S(1)} all-to-all(f32[8,16,384]{2,1,0:T(8,128)S(1)} %misfit.4), channel_id=1, replica_groups=mesh['sens'=2,'chip'=8,'core'=2] {'chip'}, dimensions={0} | all-to-all | bytes 393216 | tf_op jit(solution)/shard_map/all_to_all | solution.py:384
  98.0 2.6 %adjoint_mine.4.part_ref = f32[1536,128]{1,0:T(8,128)S(1)} custom-call(bf16[2,192,256,128]{3,2,1,0:T(8,128)(2,1)S(1)} %relayout.1.k_ref, f32[8,16,384]{2,1,0:T(8,128)S(1)} %all_to_all.67.m_ref, bf16[2,768,384]{2,1,0:T(8,128)(2,1)S(1)} %copy-done), custom_call_target="tpu_custom_call" | custom-call | flops 100663296 | bytes 12582912 | tf_op jit(solution)/shard_map/adjoint_mine/pallas_call | solution.py:346
  100.6 3.2 %adjoint_other.4.a_ref = f32[64,384]{1,0:T(8,128)S(1)} custom-call(bf16[2,192,256,128]{3,2,1,0:T(8,128)(2,1)S(1)} %relayout.1.k_ref, f32[8,16,384]{2,1,0:T(8,128)S(1)} %collective-permute-done.6.m_ref, f32[1536,128]{1,0:T(8,128)S(1)} %adjoint_mine.4.part_ref, bf16[2,768,384]{2,1,0:T(8,128)(2,1)S(1)} %copy-done), custom_call_target="tpu_custom_call" | custom-call | tf_op jit(solution)/shard_map/adjoint_other/pallas_call | solution.py:356
  103.8 1.6 collective-permute-start.7
  105.4 3.7 %collective-permute-done.7.b_ref = f32[64,384]{1,0:T(8,128)S(1)} collective-permute-done((f32[64,384]{1,0:T(8,128)S(1)}, f32[64,384]{1,0:T(8,128)S(1)}, u32[]{:S(2)}, u32[]{:S(2)}) %collective-permute-start.7) | collective-permute-done | bytes 98336 | tf_op jit(solution)/shard_map/ppermute | solution.py:380
  109.3 9.4 %all_to_all.68 = f32[16,1,128]{2,1,0:T(1,128)S(1)} all-to-all(f32[16,1,128]{2,1,0:T(1,128)S(1)} %bitcast.18), channel_id=1, replica_groups=mesh['sens'=2,'chip'=8,'core'=2] {'chip','core'}, dimensions={0} | all-to-all | bytes 16384 | tf_op jit(solution)/shard_map/all_to_all | solution.py:388
  118.7 6.1 %forward_next.3 = (f32[64,384]{1,0:T(8,128)S(1)}, f32[2,1536,128]{2,1,0:T(8,128)S(1)}, f32[8,16,384]{2,1,0:T(8,128)S(1)}) custom-call(bf16[2,192,256,128]{3,2,1,0:T(8,128)(2,1)S(1)} %relayout.1.k_ref, f32[64,384]{1,0:T(8,128)S(1)} %get-tuple-element.26.p_ref, f32[64,384]{1,0:T(8,128)S(1)} %get-tuple-element.29.g_ref, f32[16,128]{1,0:T(8,128)S(1)} %bitcast.14, ...), custom_call_target="tpu_custom_call" | custom-call | tf_op jit(solution)/shard_map/forward_next/pallas_call | solution.py:248
  125.4 0.9 collective-permute-done.8
  126.3 10.9 %all_to_all.69.parts_ref = f32[8,16,384]{2,1,0:T(8,128)S(1)} all-to-all(f32[8,16,384]{2,1,0:T(8,128)S(1)} %add.11), channel_id=1, replica_groups=mesh['sens'=2,'chip'=8,'core'=2] {'chip'}, dimensions={0} | all-to-all | bytes 393216 | tf_op jit(solution)/shard_map/all_to_all | solution.py:384
  137.3 0.6 misfit.5
  137.9 10.7 %all_to_all.70.m_ref = f32[8,16,384]{2,1,0:T(8,128)S(1)} all-to-all(f32[8,16,384]{2,1,0:T(8,128)S(1)} %get-tuple-element.34), channel_id=1, replica_groups=mesh['sens'=2,'chip'=8,'core'=2] {'chip'}, dimensions={0} | all-to-all | bytes 393216 | tf_op jit(solution)/shard_map/all_to_all | solution.py:384
  148.6 2.6 %adjoint_mine.5.part_ref = f32[1536,128]{1,0:T(8,128)S(1)} custom-call(bf16[2,192,256,128]{3,2,1,0:T(8,128)(2,1)S(1)} %relayout.1.k_ref, f32[8,16,384]{2,1,0:T(8,128)S(1)} %all_to_all.70.m_ref, bf16[2,768,384]{2,1,0:T(8,128)(2,1)S(1)} %copy-done), custom_call_target="tpu_custom_call" | custom-call | flops 100663296 | bytes 12582912 | tf_op jit(solution)/shard_map/adjoint_mine/pallas_call | solution.py:346
  151.2 3.2 %adjoint_other.5.a_ref = f32[64,384]{1,0:T(8,128)S(1)} custom-call(bf16[2,192,256,128]{3,2,1,0:T(8,128)(2,1)S(1)} %relayout.1.k_ref, f32[8,16,384]{2,1,0:T(8,128)S(1)} %collective-permute-done.9.m_ref, f32[1536,128]{1,0:T(8,128)S(1)} %adjoint_mine.5.part_ref, bf16[2,768,384]{2,1,0:T(8,128)(2,1)S(1)} %copy-done), custom_call_target="tpu_custom_call" | custom-call | tf_op jit(solution)/shard_map/adjoint_other/pallas_call | solution.py:356
  154.4 1.6 collective-permute-start.10
  156.0 3.7 %collective-permute-done.10.b_ref = f32[64,384]{1,0:T(8,128)S(1)} collective-permute-done((f32[64,384]{1,0:T(8,128)S(1)}, f32[64,384]{1,0:T(8,128)S(1)}, u32[]{:S(2)}, u32[]{:S(2)}) %collective-permute-start.10) | collective-permute-done | bytes 98336 | tf_op jit(solution)/shard_map/ppermute | solution.py:380
  159.9 9.4 %all_to_all.71 = f32[16,1,128]{2,1,0:T(1,128)S(1)} all-to-all(f32[16,1,128]{2,1,0:T(1,128)S(1)} %bitcast.16), channel_id=1, replica_groups=mesh['sens'=2,'chip'=8,'core'=2] {'chip','core'}, dimensions={0} | all-to-all | bytes 16384 | tf_op jit(solution)/shard_map/all_to_all | solution.py:388
  169.3 0.7 finish.1
  (30 shorter events, 2.1 us)
Async XLA Ops:
  0.6 14.7 %collective-permute-start = (f32[32,384]{1,0:T(8,128)}, f32[32,384]{1,0:T(8,128)S(1)}, u32[]{:S(2)}, u32[]{:S(2)}) collective-permute-start(f32[32,384]{1,0:T(8,128)} %mine_ref.1), channel_id=1, source_target_pairs={{0,16},{16,0},{1,17},{17,1},{2,18},{18,2},{3,19},{19,3},{4,20},{20... | collective-permute-start | bytes 147464 | tf_op jit(solution)/shard_map/ppermute | solution.py:380
  3.7 11.7 %copy-start = (bf16[2,768,384]{2,1,0:T(8,128)(2,1)S(1)}, bf16[2,768,384]{2,1,0:T(8,128)(2,1)}, u32[]{:S(2)}) copy-start(bf16[2,768,384]{2,1,0:T(8,128)(2,1)} %constant.2.clone.t_ref) | copy-start | bytes 3538948
  3.7 11.7 %copy-start.2 = (f32[32,384]{1,0:T(8,128)S(1)}, f32[32,384]{1,0:T(8,128)}, u32[]{:S(2)}) copy-start(f32[32,384]{1,0:T(8,128)} %mine_ref.1) | copy-start | bytes 147460
  3.7 11.7 %copy-start.3 = (f32[32]{0:T(128)S(1)}, f32[32]{0:T(128)}, u32[]{:S(2)}) copy-start(f32[32]{0:T(128)} %param.6) | copy-start | bytes 388
  3.7 11.7 %collective-permute-start.1 = (f32[1,32]{1,0:T(1,128)}, f32[1,32]{1,0:T(1,128)S(1)}, u32[]{:S(2)}, u32[]{:S(2)}) collective-permute-start(f32[1,32]{1,0:T(1,128)} %bitcast.19), channel_id=1, source_target_pairs={{0,16},{16,0},{1,17},{17,1},{2,18},{18,2},{3,19},{19,3},{4,20},{20... | collective-permute-start | bytes 392 | tf_op jit(solution)/shard_map/ppermute | solution.py:380
  21.5 1.5 collective-permute-start.2
  21.5 15.7 %copy-start.1 = (f32[256,384]{1,0:T(8,128)S(1)}, f32[256,384]{1,0:T(8,128)}, u32[]{:S(2)}) copy-start(f32[256,384]{1,0:T(8,128)} %obs_ref.5) | copy-start | bytes 1179652
  48.0 2.6 %collective-permute-start.3 = (f32[8,16,384]{2,1,0:T(8,128)S(1)}, f32[8,16,384]{2,1,0:T(8,128)S(1)}, u32[]{:S(2)}, u32[]{:S(2)}) collective-permute-start(f32[8,16,384]{2,1,0:T(8,128)S(1)} %all_to_all.64.m_ref), channel_id=1, source_target_pairs={{0,1},{1,0},{2,3},{3,2},{4,5},{5,4},{6,7},{7,6},{8,9},{9,8},{10,11... | collective-permute-start | bytes 589832 | tf_op jit(solution)/shard_map/ppermute | solution.py:380
  53.9 5.3 %collective-permute-start.4 = (f32[64,384]{1,0:T(8,128)S(1)}, f32[64,384]{1,0:T(8,128)S(1)}, u32[]{:S(2)}, u32[]{:S(2)}) collective-permute-start(f32[64,384]{1,0:T(8,128)S(1)} %adjoint_other.3.a_ref), channel_id=1, source_target_pairs={{0,16},{16,0},{1,17},{17,1},{2,18},{18,2},{3,19},{19,3},{4,20},{20... | collective-permute-start | bytes 294920 | tf_op jit(solution)/shard_map/ppermute | solution.py:380
  74.8 1.5 collective-permute-start.5
  98.0 2.6 %collective-permute-start.6 = (f32[8,16,384]{2,1,0:T(8,128)S(1)}, f32[8,16,384]{2,1,0:T(8,128)S(1)}, u32[]{:S(2)}, u32[]{:S(2)}) collective-permute-start(f32[8,16,384]{2,1,0:T(8,128)S(1)} %all_to_all.67.m_ref), channel_id=1, source_target_pairs={{0,1},{1,0},{2,3},{3,2},{4,5},{5,4},{6,7},{7,6},{8,9},{9,8},{10,11... | collective-permute-start | bytes 589832 | tf_op jit(solution)/shard_map/ppermute | solution.py:380
  103.8 5.3 %collective-permute-start.7 = (f32[64,384]{1,0:T(8,128)S(1)}, f32[64,384]{1,0:T(8,128)S(1)}, u32[]{:S(2)}, u32[]{:S(2)}) collective-permute-start(f32[64,384]{1,0:T(8,128)S(1)} %adjoint_other.4.a_ref), channel_id=1, source_target_pairs={{0,16},{16,0},{1,17},{17,1},{2,18},{18,2},{3,19},{19,3},{4,20},{20... | collective-permute-start | bytes 294920 | tf_op jit(solution)/shard_map/ppermute | solution.py:380
  124.8 1.5 collective-permute-start.8
  148.6 2.6 %collective-permute-start.9 = (f32[8,16,384]{2,1,0:T(8,128)S(1)}, f32[8,16,384]{2,1,0:T(8,128)S(1)}, u32[]{:S(2)}, u32[]{:S(2)}) collective-permute-start(f32[8,16,384]{2,1,0:T(8,128)S(1)} %all_to_all.70.m_ref), channel_id=1, source_target_pairs={{0,1},{1,0},{2,3},{3,2},{4,5},{5,4},{6,7},{7,6},{8,9},{9,8},{10,11... | collective-permute-start | bytes 589832 | tf_op jit(solution)/shard_map/ppermute | solution.py:380
  154.4 5.3 %collective-permute-start.10 = (f32[64,384]{1,0:T(8,128)S(1)}, f32[64,384]{1,0:T(8,128)S(1)}, u32[]{:S(2)}, u32[]{:S(2)}) collective-permute-start(f32[64,384]{1,0:T(8,128)S(1)} %adjoint_other.5.a_ref), channel_id=1, source_target_pairs={{0,16},{16,0},{1,17},{17,1},{2,18},{18,2},{3,19},{19,3},{4,20},{20... | collective-permute-start | bytes 294920 | tf_op jit(solution)/shard_map/ppermute | solution.py:380

commit v9 on v8

--- a/solution.py
+++ b/solution.py
@@ -129,7 +129,10 @@
 
 
 def turned(k_ref, pair):
-    blocks = [[k_ref[h, pair, c * LANES:(c + 1) * LANES, :].T for c in range(2)] for h in range(2)]
+    return [[k_ref[h, pair, c * LANES:(c + 1) * LANES, :].T for c in range(2)] for h in range(2)]
+
+
+def joined(blocks):
     return jnp.concatenate([jnp.concatenate(row, axis=1) for row in blocks], axis=0)
 
 
@@ -145,7 +148,7 @@
     lax.fori_loop(0, pairs // unroll, step, 0)
 
 
-def forward_core(param, scale_rows, k_ref, t_ref, res, send_ref, lhs):
+def forward_core(param, scale_rows, product, k_ref, t_ref, res, send_ref, lhs):
     freqs, sources = param.shape[1], param.shape[0]
     high, rest = split(scale_rows * jax.nn.softplus(param))
     z = mm(t_ref[0], jnp.concatenate([high, high, rest, rest], axis=0), NT)
@@ -163,7 +166,7 @@
     def body(u, pair, rows, first):
         v = lhs[rows, :]
         a = jnp.concatenate([jnp.where(first, v, 0.0), jnp.where(first, 0.0, v)], axis=1).astype(bf16)
-        o = mm(a, turned(k_ref, pair), NN) if u % 3 else mm(a, tile(k_ref, pair), NT)
+        o = product(a, u, pair)
         res[0, rows, :] = o[:, :LANES]
         res[1, rows, :] = o[:, LANES:]
 
@@ -197,7 +200,7 @@
     )(res, table)
 
 
-def forward_first_body(k_ref, mine_ref, other_ref, rig_mine_ref, rig_other_ref, t_ref, new_ref, rig_ref, res, send_ref, lhs, both, scales):
+def forward_first_body(k_ref, mine_ref, other_ref, rig_mine_ref, rig_other_ref, t_ref, kept_ref, new_ref, rig_ref, res, send_ref, lhs, both, scales):
     sens = lax.axis_index("sens")
     rows = mine_ref.shape[0]
     same = lax.broadcasted_iota(jnp.int32, (rows, rows), 0) == lax.broadcasted_iota(jnp.int32, (rows, rows), 1)
@@ -209,7 +212,18 @@
     scale_rows = scales[...].reshape(rig_ref.shape)
     new_ref[...] = param
     rig_ref[...] = scale_rows
-    forward_core(param, scale_rows[:, 0:1], k_ref, t_ref, res, send_ref, lhs)
+
+    def product(a, u, pair):
+        if u % 12 in (0, 3, 6, 11):
+            return mm(a, tile(k_ref, pair), NT)
+        blocks = turned(k_ref, pair)
+        if u % 4 == 1:
+            for h in range(2):
+                for c in range(2):
+                    kept_ref[c, pair // 4, h * LANES:(h + 1) * LANES, :] = blocks[h][c]
+        return mm(a, joined(blocks), NN)
+
+    forward_core(param, scale_rows[:, 0:1], product, k_ref, t_ref, res, send_ref, lhs)
 
 
 def moved(param, gradient, sums, entries):
@@ -218,10 +232,18 @@
     return param - step_rate * gradient / root_mean
 
 
-def forward_next_body(entries, k_ref, p_ref, g_ref, q_ref, rig_ref, t_ref, new_ref, res, send_ref, lhs):
+def forward_next_body(entries, k_ref, kept_ref, p_ref, g_ref, q_ref, rig_ref, t_ref, new_ref, res, send_ref, lhs):
     param = moved(p_ref[...], g_ref[...], q_ref[...], entries)
     new_ref[...] = param
-    forward_core(param, rig_ref[:, 0:1], k_ref, t_ref, res, send_ref, lhs)
+
+    def product(a, u, pair):
+        if u % 4 == 1:
+            return mm(a, tile(kept_ref, pair // 4), NN)
+        if u % 6 == 0:
+            return mm(a, tile(k_ref, pair), NT)
+        return mm(a, joined(turned(k_ref, pair)), NN)
+
+    forward_core(param, rig_ref[:, 0:1], product, k_ref, t_ref, res, send_ref, lhs)
 
 
 def forward_spaces(k2, length, chips, cores):
@@ -236,20 +258,20 @@
     sources, length = 2 * mine.shape[0], table.shape[2]
     outs, scratch = forward_spaces(k2, length, chips, cores)
     return pl.pallas_call(
-        forward_first_body, in_specs=[VM] * 6, out_specs=[VM] * 4,
-        out_shape=[jax.ShapeDtypeStruct((sources, length), f32), jax.ShapeDtypeStruct((sources, LANES), f32)] + outs,
+        forward_first_body, in_specs=[VM] * 6, out_specs=[VM] * 5,
+        out_shape=[pltpu.VMEM((2, k2.shape[1] // 4, 2 * k2.shape[3], k2.shape[2] // 2), bf16), jax.ShapeDtypeStruct((sources, length), f32), jax.ShapeDtypeStruct((sources, LANES), f32)] + outs,
         scratch_shapes=scratch + [pltpu.VMEM((2, *mine.shape), f32), pltpu.VMEM((2, mine.shape[0], LANES), f32)],
-        compiler_params=params(12), name="forward_first",
+        compiler_params=params(6), name="forward_first",
     )(k2, mine, other, rig_mine, rig_other, table)
 
 
-def forward_next(k2, param, gradient, sums, scale_rows, table, chips, cores, entries):
+def forward_next(k2, kept, param, gradient, sums, scale_rows, table, chips, cores, entries):
     outs, scratch = forward_spaces(k2, param.shape[1], chips, cores)
     return pl.pallas_call(
-        functools.partial(forward_next_body, entries), in_specs=[VM] * 6, out_specs=[VM] * 3,
+        functools.partial(forward_next_body, entries), in_specs=[VM] * 7, out_specs=[VM] * 3,
         out_shape=[jax.ShapeDtypeStruct(param.shape, f32)] + outs,
-        scratch_shapes=scratch, compiler_params=params(12), name="forward_next",
-    )(k2, param, gradient, sums, scale_rows, table)
+        scratch_shapes=scratch, compiler_params=params(6), name="forward_next",
+    )(k2, kept, param, gradient, sums, scale_rows, table)
 
 
 def misfit_body(parts_ref, obs_ref, spread_ref, m_ref=None):
@@ -347,7 +369,7 @@
         adjoint_mine_body, in_specs=[VM] * 3, out_specs=VM,
         out_shape=pltpu.VMEM((pairs * 8, LANES), f32),
         scratch_shapes=[pltpu.VMEM((pairs * 8, LANES), f32)],
-        cost_estimate=spent, compiler_params=params(8), name="adjoint_mine",
+        cost_estimate=spent, compiler_params=params(6), name="adjoint_mine",
     )(k2, mine, table)
 
 
@@ -357,7 +379,7 @@
         adjoint_other_body, in_specs=[VM] * 4, out_specs=VM,
         out_shape=jax.ShapeDtypeStruct((width // 2, table.shape[2]), f32),
         scratch_shapes=[pltpu.VMEM((pairs * 8, LANES), f32), pltpu.VMEM((pairs * 8, LANES), f32)],
-        compiler_params=params(8), name="adjoint_other",
+        compiler_params=params(6), name="adjoint_other",
     )(k2, other, part, table)
 
 
@@ -440,10 +462,10 @@
     scales = rigidity.reshape(1, -1)
     others, other_scales = swap(slip_param, "sens"), swap(scales, "sens")
     k2 = relayout(kernel, cores)
-    param, scale_rows, res, send = forward_first(k2, slip_param, others, scales, other_scales, table, chips, cores)
+    kept, param, scale_rows, res, send = forward_first(k2, slip_param, others, scales, other_scales, table, chips, cores)
     for iteration in range(ITERS):
         if iteration:
-            param, res, send = forward_next(k2, param, gradient, sums, scale_rows, table, chips, cores, entries)
+            param, res, send = forward_next(k2, kept, param, gradient, sums, scale_rows, table, chips, cores, entries)
         spread, *misfit = misfit_and_spread(to_chips(kept_terms(res, send, table) + swap(send, "core")), observed, iteration == ITERS - 1)
         near = to_chips(spread)
         far = swap(near, "core")

time: 170 us -> 170 us (level)
  no operation moved by 1% of the time
where the time goes in v9:
time: 170 us; the launch traced here: 169 us
  blocking collectives  96.5 us (57%)
  Pallas kernels  50.2 us (30%)
  waiting for transfers between devices  13.7 us (8%)
  starting transfers between devices  8.04 us (5%)
    all_to_all x6, blocking collectives, to_chips(): return lax.all_to_all(x, 'chip', 0, 0)  68.3 us
    all_to_all x3, blocking collectives, exchange_scalars(): return lax.all_to_all(sums, ('chip', 'core'), 0, 0, tiled=True)  28.2 us
    ppermute x11, waiting for transfers between devices, swap(): return lax.ppermute(x, axis, [(0, 1), (1, 0)])  13.7 us
    pallas_call x1, Pallas kernels, relayout(): pl.pallas_call(functools.partial(relayout_body, cores), in_specs=[pl.Bloc...  11.5 us
    pallas_call x2, Pallas kernels, forward_next(): pl.pallas_call(functools.partial(forward_next_body, entries), in_specs=[V...  11.2 us
    pallas_call x3, Pallas kernels, adjoint_other(): pl.pallas_call(adjoint_other_body, in_specs=[VM] * 4, out_specs=VM, out_s...  9.61 us
    ppermute x11, starting transfers between devices, swap(): return lax.ppermute(x, axis, [(0, 1), (1, 0)])  8.04 us
    pallas_call x3, Pallas kernels, adjoint_mine(): pl.pallas_call(adjoint_mine_body, in_specs=[VM] * 3, out_specs=VM, out_sh...  7.88 us
  transfers between devices with their start and end apart: 11, of which 6 were waited for; matrix products, arithmetic and copies ran while one was open for 0% of the time, Pallas kernels for 12%

profile of v9, /device:TPU:0, one launch (start us, length us, event | category | flops | bytes accessed | tf_op | source)
XLA Modules:
  0.0 169.3 jit_solution(16233419210088249705)
XLA Ops:
  0.6 3.0 %collective-permute-start = (f32[32,384]{1,0:T(8,128)}, f32[32,384]{1,0:T(8,128)S(1)}, u32[]{:S(2)}, u32[]{:S(2)}) collective-permute-start(f32[32,384]{1,0:T(8,128)} %mine_ref.1), channel_id=1, source_target_pairs={{0,16},{16,0},{1,17},{17,1},{2,18},{18,2},{3,19},{19,3},{4,20},{20... | collective-permute-start | bytes 147464 | tf_op jit(solution)/shard_map/ppermute | solution.py:402
  3.8 11.5 %relayout.1.k_ref = bf16[2,192,256,128]{3,2,1,0:T(8,128)(2,1)S(1)} custom-call(bf16[2,256,64,384]{3,2,1,0:T(8,128)(2,1)} %k_hbm.1), custom_call_target="tpu_custom_call" | custom-call | tf_op jit(solution)/shard_map/relayout/pallas_call | solution.py:108
  15.4 6.3 %forward_first.1 = (bf16[2,48,256,128]{3,2,1,0:T(8,128)(2,1)S(1)}, f32[64,384]{1,0:T(8,128)S(1)}, f32[64,128]{1,0:T(8,128)S(1)}, f32[2,1536,128]{2,1,0:T(8,128)S(1)}, f32[8,16,384]{2,1,0:T(8,128)S(1)}) custom-call(bf16[2,192,256,128]{3,2,1,0:T(8,128)(2,1)S(1)} %relayout.1.k_ref, f32[32,384]{1,0:T(8,128)S(1)} %copy-done.2, ...), custom_call_target="tpu_custom_call" | custom-call | tf_op jit(solution)/shard_map/forward_first/pallas_call | solution.py:260
  21.8 0.6 keep.3
  22.4 0.8 collective-permute-done.2
  23.2 14.3 %all_to_all.63.parts_ref = f32[8,16,384]{2,1,0:T(8,128)S(1)} all-to-all(f32[8,16,384]{2,1,0:T(8,128)S(1)} %add.9), channel_id=1, replica_groups=mesh['sens'=2,'chip'=8,'core'=2] {'chip'}, dimensions={0} | all-to-all | bytes 393216 | tf_op jit(solution)/shard_map/all_to_all | solution.py:406
  37.5 10.7 %all_to_all.64.m_ref = f32[8,16,384]{2,1,0:T(8,128)S(1)} all-to-all(f32[8,16,384]{2,1,0:T(8,128)S(1)} %misfit.3), channel_id=1, replica_groups=mesh['sens'=2,'chip'=8,'core'=2] {'chip'}, dimensions={0} | all-to-all | bytes 393216 | tf_op jit(solution)/shard_map/all_to_all | solution.py:406
  48.2 2.6 %adjoint_mine.3.part_ref = f32[1536,128]{1,0:T(8,128)S(1)} custom-call(bf16[2,192,256,128]{3,2,1,0:T(8,128)(2,1)S(1)} %relayout.1.k_ref, f32[8,16,384]{2,1,0:T(8,128)S(1)} %all_to_all.64.m_ref, bf16[2,768,384]{2,1,0:T(8,128)(2,1)S(1)} %copy-done), custom_call_target="tpu_custom_call" | custom-call | flops 100663296 | bytes 12582912 | tf_op jit(solution)/shard_map/adjoint_mine/pallas_call | solution.py:368
  50.9 3.2 %adjoint_other.3.a_ref = f32[64,384]{1,0:T(8,128)S(1)} custom-call(bf16[2,192,256,128]{3,2,1,0:T(8,128)(2,1)S(1)} %relayout.1.k_ref, f32[8,16,384]{2,1,0:T(8,128)S(1)} %collective-permute-done.3.m_ref, f32[1536,128]{1,0:T(8,128)S(1)} %adjoint_mine.3.part_ref, bf16[2,768,384]{2,1,0:T(8,128)(2,1)S(1)} %copy-done), custom_call_target="tpu_custom_call" | custom-call | tf_op jit(solution)/shard_map/adjoint_other/pallas_call | solution.py:378
  54.1 1.6 collective-permute-start.4
  55.6 3.7 %collective-permute-done.4.b_ref = f32[64,384]{1,0:T(8,128)S(1)} collective-permute-done((f32[64,384]{1,0:T(8,128)S(1)}, f32[64,384]{1,0:T(8,128)S(1)}, u32[]{:S(2)}, u32[]{:S(2)}) %collective-permute-start.4) | collective-permute-done | bytes 98336 | tf_op jit(solution)/shard_map/ppermute | solution.py:402
  59.5 9.4 %all_to_all.65 = f32[16,1,128]{2,1,0:T(1,128)S(1)} all-to-all(f32[16,1,128]{2,1,0:T(1,128)S(1)} %bitcast.17), channel_id=1, replica_groups=mesh['sens'=2,'chip'=8,'core'=2] {'chip','core'}, dimensions={0} | all-to-all | bytes 16384 | tf_op jit(solution)/shard_map/all_to_all | solution.py:410
  68.9 5.6 %forward_next.2 = (f32[64,384]{1,0:T(8,128)S(1)}, f32[2,1536,128]{2,1,0:T(8,128)S(1)}, f32[8,16,384]{2,1,0:T(8,128)S(1)}) custom-call(bf16[2,192,256,128]{3,2,1,0:T(8,128)(2,1)S(1)} %relayout.1.k_ref, bf16[2,48,256,128]{3,2,1,0:T(8,128)(2,1)S(1)} %get-tuple-element.21.kept_ref, f32[64,384]{1,0:T(8,128)S(1)} %get-tuple-element.22.p_ref, ...), custom_call_target="tpu_custom_call" | custom-call | tf_op jit(solution)/shard_map/forward_next/pallas_call | solution.py:270
  75.2 0.9 collective-permute-done.5
  76.1 10.9 %all_to_all.66.parts_ref = f32[8,16,384]{2,1,0:T(8,128)S(1)} all-to-all(f32[8,16,384]{2,1,0:T(8,128)S(1)} %add.10), channel_id=1, replica_groups=mesh['sens'=2,'chip'=8,'core'=2] {'chip'}, dimensions={0} | all-to-all | bytes 393216 | tf_op jit(solution)/shard_map/all_to_all | solution.py:406
  87.0 10.7 %all_to_all.67.m_ref = f32[8,16,384]{2,1,0:T(8,128)S(1)} all-to-all(f32[8,16,384]{2,1,0:T(8,128)S(1)} %misfit.4), channel_id=1, replica_groups=mesh['sens'=2,'chip'=8,'core'=2] {'chip'}, dimensions={0} | all-to-all | bytes 393216 | tf_op jit(solution)/shard_map/all_to_all | solution.py:406
  97.8 2.6 %adjoint_mine.4.part_ref = f32[1536,128]{1,0:T(8,128)S(1)} custom-call(bf16[2,192,256,128]{3,2,1,0:T(8,128)(2,1)S(1)} %relayout.1.k_ref, f32[8,16,384]{2,1,0:T(8,128)S(1)} %all_to_all.67.m_ref, bf16[2,768,384]{2,1,0:T(8,128)(2,1)S(1)} %copy-done), custom_call_target="tpu_custom_call" | custom-call | flops 100663296 | bytes 12582912 | tf_op jit(solution)/shard_map/adjoint_mine/pallas_call | solution.py:368
  100.4 3.2 %adjoint_other.4.a_ref = f32[64,384]{1,0:T(8,128)S(1)} custom-call(bf16[2,192,256,128]{3,2,1,0:T(8,128)(2,1)S(1)} %relayout.1.k_ref, f32[8,16,384]{2,1,0:T(8,128)S(1)} %collective-permute-done.6.m_ref, f32[1536,128]{1,0:T(8,128)S(1)} %adjoint_mine.4.part_ref, bf16[2,768,384]{2,1,0:T(8,128)(2,1)S(1)} %copy-done), custom_call_target="tpu_custom_call" | custom-call | tf_op jit(solution)/shard_map/adjoint_other/pallas_call | solution.py:378
  103.6 1.6 collective-permute-start.7
  105.2 3.7 %collective-permute-done.7.b_ref = f32[64,384]{1,0:T(8,128)S(1)} collective-permute-done((f32[64,384]{1,0:T(8,128)S(1)}, f32[64,384]{1,0:T(8,128)S(1)}, u32[]{:S(2)}, u32[]{:S(2)}) %collective-permute-start.7) | collective-permute-done | bytes 98336 | tf_op jit(solution)/shard_map/ppermute | solution.py:402
  109.0 9.4 %all_to_all.68 = f32[16,1,128]{2,1,0:T(1,128)S(1)} all-to-all(f32[16,1,128]{2,1,0:T(1,128)S(1)} %bitcast.18), channel_id=1, replica_groups=mesh['sens'=2,'chip'=8,'core'=2] {'chip','core'}, dimensions={0} | all-to-all | bytes 16384 | tf_op jit(solution)/shard_map/all_to_all | solution.py:410
  118.4 5.6 %forward_next.3 = (f32[64,384]{1,0:T(8,128)S(1)}, f32[2,1536,128]{2,1,0:T(8,128)S(1)}, f32[8,16,384]{2,1,0:T(8,128)S(1)}) custom-call(bf16[2,192,256,128]{3,2,1,0:T(8,128)(2,1)S(1)} %relayout.1.k_ref, bf16[2,48,256,128]{3,2,1,0:T(8,128)(2,1)S(1)} %get-tuple-element.21.kept_ref, f32[64,384]{1,0:T(8,128)S(1)} %get-tuple-element.28.p_ref, ...), custom_call_target="tpu_custom_call" | custom-call | tf_op jit(solution)/shard_map/forward_next/pallas_call | solution.py:270
  124.7 0.8 collective-permute-done.8
  125.6 10.9 %all_to_all.69.parts_ref = f32[8,16,384]{2,1,0:T(8,128)S(1)} all-to-all(f32[8,16,384]{2,1,0:T(8,128)S(1)} %add.11), channel_id=1, replica_groups=mesh['sens'=2,'chip'=8,'core'=2] {'chip'}, dimensions={0} | all-to-all | bytes 393216 | tf_op jit(solution)/shard_map/all_to_all | solution.py:406
  136.5 0.6 misfit.5
  137.2 10.7 %all_to_all.70.m_ref = f32[8,16,384]{2,1,0:T(8,128)S(1)} all-to-all(f32[8,16,384]{2,1,0:T(8,128)S(1)} %get-tuple-element.36), channel_id=1, replica_groups=mesh['sens'=2,'chip'=8,'core'=2] {'chip'}, dimensions={0} | all-to-all | bytes 393216 | tf_op jit(solution)/shard_map/all_to_all | solution.py:406
  147.9 2.6 %adjoint_mine.5.part_ref = f32[1536,128]{1,0:T(8,128)S(1)} custom-call(bf16[2,192,256,128]{3,2,1,0:T(8,128)(2,1)S(1)} %relayout.1.k_ref, f32[8,16,384]{2,1,0:T(8,128)S(1)} %all_to_all.70.m_ref, bf16[2,768,384]{2,1,0:T(8,128)(2,1)S(1)} %copy-done), custom_call_target="tpu_custom_call" | custom-call | flops 100663296 | bytes 12582912 | tf_op jit(solution)/shard_map/adjoint_mine/pallas_call | solution.py:368
  150.5 3.2 %adjoint_other.5.a_ref = f32[64,384]{1,0:T(8,128)S(1)} custom-call(bf16[2,192,256,128]{3,2,1,0:T(8,128)(2,1)S(1)} %relayout.1.k_ref, f32[8,16,384]{2,1,0:T(8,128)S(1)} %collective-permute-done.9.m_ref, f32[1536,128]{1,0:T(8,128)S(1)} %adjoint_mine.5.part_ref, bf16[2,768,384]{2,1,0:T(8,128)(2,1)S(1)} %copy-done), custom_call_target="tpu_custom_call" | custom-call | tf_op jit(solution)/shard_map/adjoint_other/pallas_call | solution.py:378
  153.7 1.6 collective-permute-start.10
  155.3 3.7 %collective-permute-done.10.b_ref = f32[64,384]{1,0:T(8,128)S(1)} collective-permute-done((f32[64,384]{1,0:T(8,128)S(1)}, f32[64,384]{1,0:T(8,128)S(1)}, u32[]{:S(2)}, u32[]{:S(2)}) %collective-permute-start.10) | collective-permute-done | bytes 98336 | tf_op jit(solution)/shard_map/ppermute | solution.py:402
  159.2 9.4 %all_to_all.71 = f32[16,1,128]{2,1,0:T(1,128)S(1)} all-to-all(f32[16,1,128]{2,1,0:T(1,128)S(1)} %bitcast.16), channel_id=1, replica_groups=mesh['sens'=2,'chip'=8,'core'=2] {'chip','core'}, dimensions={0} | all-to-all | bytes 16384 | tf_op jit(solution)/shard_map/all_to_all | solution.py:410
  168.6 0.7 finish.1
  (30 shorter events, 2.1 us)
Async XLA Ops:
  0.6 14.7 %collective-permute-start = (f32[32,384]{1,0:T(8,128)}, f32[32,384]{1,0:T(8,128)S(1)}, u32[]{:S(2)}, u32[]{:S(2)}) collective-permute-start(f32[32,384]{1,0:T(8,128)} %mine_ref.1), channel_id=1, source_target_pairs={{0,16},{16,0},{1,17},{17,1},{2,18},{18,2},{3,19},{19,3},{4,20},{20... | collective-permute-start | bytes 147464 | tf_op jit(solution)/shard_map/ppermute | solution.py:402
  3.7 11.7 %copy-start = (bf16[2,768,384]{2,1,0:T(8,128)(2,1)S(1)}, bf16[2,768,384]{2,1,0:T(8,128)(2,1)}, u32[]{:S(2)}) copy-start(bf16[2,768,384]{2,1,0:T(8,128)(2,1)} %constant.2.clone.t_ref) | copy-start | bytes 3538948
  3.7 11.7 %copy-start.2 = (f32[32,384]{1,0:T(8,128)S(1)}, f32[32,384]{1,0:T(8,128)}, u32[]{:S(2)}) copy-start(f32[32,384]{1,0:T(8,128)} %mine_ref.1) | copy-start | bytes 147460
  3.7 11.7 %copy-start.3 = (f32[32]{0:T(128)S(1)}, f32[32]{0:T(128)}, u32[]{:S(2)}) copy-start(f32[32]{0:T(128)} %param.6) | copy-start | bytes 388
  3.7 11.7 %collective-permute-start.1 = (f32[1,32]{1,0:T(1,128)}, f32[1,32]{1,0:T(1,128)S(1)}, u32[]{:S(2)}, u32[]{:S(2)}) collective-permute-start(f32[1,32]{1,0:T(1,128)} %bitcast.19), channel_id=1, source_target_pairs={{0,16},{16,0},{1,17},{17,1},{2,18},{18,2},{3,19},{19,3},{4,20},{20... | collective-permute-start | bytes 392 | tf_op jit(solution)/shard_map/ppermute | solution.py:402
  21.7 1.5 collective-permute-start.2
  21.8 15.7 %copy-start.1 = (f32[256,384]{1,0:T(8,128)S(1)}, f32[256,384]{1,0:T(8,128)}, u32[]{:S(2)}) copy-start(f32[256,384]{1,0:T(8,128)} %obs_ref.5) | copy-start | bytes 1179652
  48.2 2.6 %collective-permute-start.3 = (f32[8,16,384]{2,1,0:T(8,128)S(1)}, f32[8,16,384]{2,1,0:T(8,128)S(1)}, u32[]{:S(2)}, u32[]{:S(2)}) collective-permute-start(f32[8,16,384]{2,1,0:T(8,128)S(1)} %all_to_all.64.m_ref), channel_id=1, source_target_pairs={{0,1},{1,0},{2,3},{3,2},{4,5},{5,4},{6,7},{7,6},{8,9},{9,8},{10,11... | collective-permute-start | bytes 589832 | tf_op jit(solution)/shard_map/ppermute | solution.py:402
  54.1 5.3 %collective-permute-start.4 = (f32[64,384]{1,0:T(8,128)S(1)}, f32[64,384]{1,0:T(8,128)S(1)}, u32[]{:S(2)}, u32[]{:S(2)}) collective-permute-start(f32[64,384]{1,0:T(8,128)S(1)} %adjoint_other.3.a_ref), channel_id=1, source_target_pairs={{0,16},{16,0},{1,17},{17,1},{2,18},{18,2},{3,19},{19,3},{4,20},{20... | collective-permute-start | bytes 294920 | tf_op jit(solution)/shard_map/ppermute | solution.py:402
  74.5 1.5 collective-permute-start.5
  97.8 2.6 %collective-permute-start.6 = (f32[8,16,384]{2,1,0:T(8,128)S(1)}, f32[8,16,384]{2,1,0:T(8,128)S(1)}, u32[]{:S(2)}, u32[]{:S(2)}) collective-permute-start(f32[8,16,384]{2,1,0:T(8,128)S(1)} %all_to_all.67.m_ref), channel_id=1, source_target_pairs={{0,1},{1,0},{2,3},{3,2},{4,5},{5,4},{6,7},{7,6},{8,9},{9,8},{10,11... | collective-permute-start | bytes 589832 | tf_op jit(solution)/shard_map/ppermute | solution.py:402
  103.6 5.3 %collective-permute-start.7 = (f32[64,384]{1,0:T(8,128)S(1)}, f32[64,384]{1,0:T(8,128)S(1)}, u32[]{:S(2)}, u32[]{:S(2)}) collective-permute-start(f32[64,384]{1,0:T(8,128)S(1)} %adjoint_other.4.a_ref), channel_id=1, source_target_pairs={{0,16},{16,0},{1,17},{17,1},{2,18},{18,2},{3,19},{19,3},{4,20},{20... | collective-permute-start | bytes 294920 | tf_op jit(solution)/shard_map/ppermute | solution.py:402
  124.1 1.5 collective-permute-start.8
  147.9 2.6 %collective-permute-start.9 = (f32[8,16,384]{2,1,0:T(8,128)S(1)}, f32[8,16,384]{2,1,0:T(8,128)S(1)}, u32[]{:S(2)}, u32[]{:S(2)}) collective-permute-start(f32[8,16,384]{2,1,0:T(8,128)S(1)} %all_to_all.70.m_ref), channel_id=1, source_target_pairs={{0,1},{1,0},{2,3},{3,2},{4,5},{5,4},{6,7},{7,6},{8,9},{9,8},{10,11... | collective-permute-start | bytes 589832 | tf_op jit(solution)/shard_map/ppermute | solution.py:402
  153.7 5.3 %collective-permute-start.10 = (f32[64,384]{1,0:T(8,128)S(1)}, f32[64,384]{1,0:T(8,128)S(1)}, u32[]{:S(2)}, u32[]{:S(2)}) collective-permute-start(f32[64,384]{1,0:T(8,128)S(1)} %adjoint_other.5.a_ref), channel_id=1, source_target_pairs={{0,16},{16,0},{1,17},{17,1},{2,18},{18,2},{3,19},{19,3},{4,20},{20... | collective-permute-start | bytes 294920 | tf_op jit(solution)/shard_map/ppermute | solution.py:402

commit v10 on v9

--- a/solution.py
+++ b/solution.py
@@ -23,7 +23,7 @@
 PITCH = 196
 BUFFERS = 6
 UNROLL = 96
-ADJOINT_UNROLL = 64
+ADJOINT_UNROLL = 96
 
 
 def table_parts(length):

time: 170 us -> 169 us (level)
  no operation moved by 1% of the time
where the time goes in v10:
time: 169 us
  blocking collectives  96.5 us (57%)
  Pallas kernels  49.5 us (29%)
  waiting for transfers between devices  13.7 us (8%)
  starting transfers between devices  8.03 us (5%)
    all_to_all x6, blocking collectives, to_chips(): return lax.all_to_all(x, 'chip', 0, 0)  68.3 us
    all_to_all x3, blocking collectives, exchange_scalars(): return lax.all_to_all(sums, ('chip', 'core'), 0, 0, tiled=True)  28.2 us
    ppermute x11, waiting for transfers between devices, swap(): return lax.ppermute(x, axis, [(0, 1), (1, 0)])  13.7 us
    pallas_call x1, Pallas kernels, relayout(): pl.pallas_call(functools.partial(relayout_body, cores), in_specs=[pl.Bloc...  11.5 us
    pallas_call x2, Pallas kernels, forward_next(): pl.pallas_call(functools.partial(forward_next_body, entries), in_specs=[V...  11.2 us
    pallas_call x3, Pallas kernels, adjoint_other(): pl.pallas_call(adjoint_other_body, in_specs=[VM] * 4, out_specs=VM, out_s...  9.27 us
    ppermute x11, starting transfers between devices, swap(): return lax.ppermute(x, axis, [(0, 1), (1, 0)])  8.03 us
    pallas_call x3, Pallas kernels, adjoint_mine(): pl.pallas_call(adjoint_mine_body, in_specs=[VM] * 3, out_specs=VM, out_sh...  7.54 us
  transfers between devices with their start and end apart: 11, of which 6 were waited for; matrix products, arithmetic and copies ran while one was open for 0% of the time, Pallas kernels for 12%

profile of v10, /device:TPU:0, one launch (start us, length us, event | category | flops | bytes accessed | tf_op | source)
XLA Modules:
  0.0 168.6 jit_solution(12444547000109880962)
XLA Ops:
  0.6 3.0 %collective-permute-start = (f32[32,384]{1,0:T(8,128)}, f32[32,384]{1,0:T(8,128)S(1)}, u32[]{:S(2)}, u32[]{:S(2)}) collective-permute-start(f32[32,384]{1,0:T(8,128)} %mine_ref.1), channel_id=1, source_target_pairs={{0,16},{16,0},{1,17},{17,1},{2,18},{18,2},{3,19},{19,3},{4,20},{20... | collective-permute-start | bytes 147464 | tf_op jit(solution)/shard_map/ppermute | solution.py:402
  3.8 11.5 %relayout.1.k_ref = bf16[2,192,256,128]{3,2,1,0:T(8,128)(2,1)S(1)} custom-call(bf16[2,256,64,384]{3,2,1,0:T(8,128)(2,1)} %k_hbm.1), custom_call_target="tpu_custom_call" | custom-call | tf_op jit(solution)/shard_map/relayout/pallas_call | solution.py:108
  15.4 6.3 %forward_first.1 = (bf16[2,48,256,128]{3,2,1,0:T(8,128)(2,1)S(1)}, f32[64,384]{1,0:T(8,128)S(1)}, f32[64,128]{1,0:T(8,128)S(1)}, f32[2,1536,128]{2,1,0:T(8,128)S(1)}, f32[8,16,384]{2,1,0:T(8,128)S(1)}) custom-call(bf16[2,192,256,128]{3,2,1,0:T(8,128)(2,1)S(1)} %relayout.1.k_ref, f32[32,384]{1,0:T(8,128)S(1)} %copy-done.2, ...), custom_call_target="tpu_custom_call" | custom-call | tf_op jit(solution)/shard_map/forward_first/pallas_call | solution.py:260
  21.8 0.6 keep.3
  22.4 0.8 collective-permute-done.2
  23.2 14.3 %all_to_all.63.parts_ref = f32[8,16,384]{2,1,0:T(8,128)S(1)} all-to-all(f32[8,16,384]{2,1,0:T(8,128)S(1)} %add.9), channel_id=1, replica_groups=mesh['sens'=2,'chip'=8,'core'=2] {'chip'}, dimensions={0} | all-to-all | bytes 393216 | tf_op jit(solution)/shard_map/all_to_all | solution.py:406
  37.5 10.7 %all_to_all.64.m_ref = f32[8,16,384]{2,1,0:T(8,128)S(1)} all-to-all(f32[8,16,384]{2,1,0:T(8,128)S(1)} %misfit.3), channel_id=1, replica_groups=mesh['sens'=2,'chip'=8,'core'=2] {'chip'}, dimensions={0} | all-to-all | bytes 393216 | tf_op jit(solution)/shard_map/all_to_all | solution.py:406
  48.2 2.5 %adjoint_mine.3.part_ref = f32[1536,128]{1,0:T(8,128)S(1)} custom-call(bf16[2,192,256,128]{3,2,1,0:T(8,128)(2,1)S(1)} %relayout.1.k_ref, f32[8,16,384]{2,1,0:T(8,128)S(1)} %all_to_all.64.m_ref, bf16[2,768,384]{2,1,0:T(8,128)(2,1)S(1)} %copy-done), custom_call_target="tpu_custom_call" | custom-call | flops 100663296 | bytes 12582912 | tf_op jit(solution)/shard_map/adjoint_mine/pallas_call | solution.py:368
  50.7 3.1 %adjoint_other.3.a_ref = f32[64,384]{1,0:T(8,128)S(1)} custom-call(bf16[2,192,256,128]{3,2,1,0:T(8,128)(2,1)S(1)} %relayout.1.k_ref, f32[8,16,384]{2,1,0:T(8,128)S(1)} %collective-permute-done.3.m_ref, f32[1536,128]{1,0:T(8,128)S(1)} %adjoint_mine.3.part_ref, bf16[2,768,384]{2,1,0:T(8,128)(2,1)S(1)} %copy-done), custom_call_target="tpu_custom_call" | custom-call | tf_op jit(solution)/shard_map/adjoint_other/pallas_call | solution.py:378
  53.8 1.6 collective-permute-start.4
  55.4 3.7 %collective-permute-done.4.b_ref = f32[64,384]{1,0:T(8,128)S(1)} collective-permute-done((f32[64,384]{1,0:T(8,128)S(1)}, f32[64,384]{1,0:T(8,128)S(1)}, u32[]{:S(2)}, u32[]{:S(2)}) %collective-permute-start.4) | collective-permute-done | bytes 98336 | tf_op jit(solution)/shard_map/ppermute | solution.py:402
  59.3 9.4 %all_to_all.65 = f32[16,1,128]{2,1,0:T(1,128)S(1)} all-to-all(f32[16,1,128]{2,1,0:T(1,128)S(1)} %bitcast.17), channel_id=1, replica_groups=mesh['sens'=2,'chip'=8,'core'=2] {'chip','core'}, dimensions={0} | all-to-all | bytes 16384 | tf_op jit(solution)/shard_map/all_to_all | solution.py:410
  68.7 5.6 %forward_next.2 = (f32[64,384]{1,0:T(8,128)S(1)}, f32[2,1536,128]{2,1,0:T(8,128)S(1)}, f32[8,16,384]{2,1,0:T(8,128)S(1)}) custom-call(bf16[2,192,256,128]{3,2,1,0:T(8,128)(2,1)S(1)} %relayout.1.k_ref, bf16[2,48,256,128]{3,2,1,0:T(8,128)(2,1)S(1)} %get-tuple-element.21.kept_ref, f32[64,384]{1,0:T(8,128)S(1)} %get-tuple-element.22.p_ref, ...), custom_call_target="tpu_custom_call" | custom-call | tf_op jit(solution)/shard_map/forward_next/pallas_call | solution.py:270
  75.0 0.9 collective-permute-done.5
  75.8 10.9 %all_to_all.66.parts_ref = f32[8,16,384]{2,1,0:T(8,128)S(1)} all-to-all(f32[8,16,384]{2,1,0:T(8,128)S(1)} %add.10), channel_id=1, replica_groups=mesh['sens'=2,'chip'=8,'core'=2] {'chip'}, dimensions={0} | all-to-all | bytes 393216 | tf_op jit(solution)/shard_map/all_to_all | solution.py:406
  86.8 10.7 %all_to_all.67.m_ref = f32[8,16,384]{2,1,0:T(8,128)S(1)} all-to-all(f32[8,16,384]{2,1,0:T(8,128)S(1)} %misfit.4), channel_id=1, replica_groups=mesh['sens'=2,'chip'=8,'core'=2] {'chip'}, dimensions={0} | all-to-all | bytes 393216 | tf_op jit(solution)/shard_map/all_to_all | solution.py:406
  97.5 2.5 %adjoint_mine.4.part_ref = f32[1536,128]{1,0:T(8,128)S(1)} custom-call(bf16[2,192,256,128]{3,2,1,0:T(8,128)(2,1)S(1)} %relayout.1.k_ref, f32[8,16,384]{2,1,0:T(8,128)S(1)} %all_to_all.67.m_ref, bf16[2,768,384]{2,1,0:T(8,128)(2,1)S(1)} %copy-done), custom_call_target="tpu_custom_call" | custom-call | flops 100663296 | bytes 12582912 | tf_op jit(solution)/shard_map/adjoint_mine/pallas_call | solution.py:368
  100.0 3.1 %adjoint_other.4.a_ref = f32[64,384]{1,0:T(8,128)S(1)} custom-call(bf16[2,192,256,128]{3,2,1,0:T(8,128)(2,1)S(1)} %relayout.1.k_ref, f32[8,16,384]{2,1,0:T(8,128)S(1)} %collective-permute-done.6.m_ref, f32[1536,128]{1,0:T(8,128)S(1)} %adjoint_mine.4.part_ref, bf16[2,768,384]{2,1,0:T(8,128)(2,1)S(1)} %copy-done), custom_call_target="tpu_custom_call" | custom-call | tf_op jit(solution)/shard_map/adjoint_other/pallas_call | solution.py:378
  103.1 1.6 collective-permute-start.7
  104.7 3.7 %collective-permute-done.7.b_ref = f32[64,384]{1,0:T(8,128)S(1)} collective-permute-done((f32[64,384]{1,0:T(8,128)S(1)}, f32[64,384]{1,0:T(8,128)S(1)}, u32[]{:S(2)}, u32[]{:S(2)}) %collective-permute-start.7) | collective-permute-done | bytes 98336 | tf_op jit(solution)/shard_map/ppermute | solution.py:402
  108.6 9.4 %all_to_all.68 = f32[16,1,128]{2,1,0:T(1,128)S(1)} all-to-all(f32[16,1,128]{2,1,0:T(1,128)S(1)} %bitcast.18), channel_id=1, replica_groups=mesh['sens'=2,'chip'=8,'core'=2] {'chip','core'}, dimensions={0} | all-to-all | bytes 16384 | tf_op jit(solution)/shard_map/all_to_all | solution.py:410
  118.0 5.6 %forward_next.3 = (f32[64,384]{1,0:T(8,128)S(1)}, f32[2,1536,128]{2,1,0:T(8,128)S(1)}, f32[8,16,384]{2,1,0:T(8,128)S(1)}) custom-call(bf16[2,192,256,128]{3,2,1,0:T(8,128)(2,1)S(1)} %relayout.1.k_ref, bf16[2,48,256,128]{3,2,1,0:T(8,128)(2,1)S(1)} %get-tuple-element.21.kept_ref, f32[64,384]{1,0:T(8,128)S(1)} %get-tuple-element.28.p_ref, ...), custom_call_target="tpu_custom_call" | custom-call | tf_op jit(solution)/shard_map/forward_next/pallas_call | solution.py:270
  124.3 0.8 collective-permute-done.8
  125.1 10.9 %all_to_all.69.parts_ref = f32[8,16,384]{2,1,0:T(8,128)S(1)} all-to-all(f32[8,16,384]{2,1,0:T(8,128)S(1)} %add.11), channel_id=1, replica_groups=mesh['sens'=2,'chip'=8,'core'=2] {'chip'}, dimensions={0} | all-to-all | bytes 393216 | tf_op jit(solution)/shard_map/all_to_all | solution.py:406
  136.1 0.6 misfit.5
  136.7 10.7 %all_to_all.70.m_ref = f32[8,16,384]{2,1,0:T(8,128)S(1)} all-to-all(f32[8,16,384]{2,1,0:T(8,128)S(1)} %get-tuple-element.36), channel_id=1, replica_groups=mesh['sens'=2,'chip'=8,'core'=2] {'chip'}, dimensions={0} | all-to-all | bytes 393216 | tf_op jit(solution)/shard_map/all_to_all | solution.py:406
  147.4 2.5 %adjoint_mine.5.part_ref = f32[1536,128]{1,0:T(8,128)S(1)} custom-call(bf16[2,192,256,128]{3,2,1,0:T(8,128)(2,1)S(1)} %relayout.1.k_ref, f32[8,16,384]{2,1,0:T(8,128)S(1)} %all_to_all.70.m_ref, bf16[2,768,384]{2,1,0:T(8,128)(2,1)S(1)} %copy-done), custom_call_target="tpu_custom_call" | custom-call | flops 100663296 | bytes 12582912 | tf_op jit(solution)/shard_map/adjoint_mine/pallas_call | solution.py:368
  149.9 3.1 %adjoint_other.5.a_ref = f32[64,384]{1,0:T(8,128)S(1)} custom-call(bf16[2,192,256,128]{3,2,1,0:T(8,128)(2,1)S(1)} %relayout.1.k_ref, f32[8,16,384]{2,1,0:T(8,128)S(1)} %collective-permute-done.9.m_ref, f32[1536,128]{1,0:T(8,128)S(1)} %adjoint_mine.5.part_ref, bf16[2,768,384]{2,1,0:T(8,128)(2,1)S(1)} %copy-done), custom_call_target="tpu_custom_call" | custom-call | tf_op jit(solution)/shard_map/adjoint_other/pallas_call | solution.py:378
  153.0 1.6 collective-permute-start.10
  154.6 3.7 %collective-permute-done.10.b_ref = f32[64,384]{1,0:T(8,128)S(1)} collective-permute-done((f32[64,384]{1,0:T(8,128)S(1)}, f32[64,384]{1,0:T(8,128)S(1)}, u32[]{:S(2)}, u32[]{:S(2)}) %collective-permute-start.10) | collective-permute-done | bytes 98336 | tf_op jit(solution)/shard_map/ppermute | solution.py:402
  158.5 9.4 %all_to_all.71 = f32[16,1,128]{2,1,0:T(1,128)S(1)} all-to-all(f32[16,1,128]{2,1,0:T(1,128)S(1)} %bitcast.16), channel_id=1, replica_groups=mesh['sens'=2,'chip'=8,'core'=2] {'chip','core'}, dimensions={0} | all-to-all | bytes 16384 | tf_op jit(solution)/shard_map/all_to_all | solution.py:410
  167.9 0.7 finish.1
  (30 shorter events, 2.1 us)
Async XLA Ops:
  0.6 14.7 %collective-permute-start = (f32[32,384]{1,0:T(8,128)}, f32[32,384]{1,0:T(8,128)S(1)}, u32[]{:S(2)}, u32[]{:S(2)}) collective-permute-start(f32[32,384]{1,0:T(8,128)} %mine_ref.1), channel_id=1, source_target_pairs={{0,16},{16,0},{1,17},{17,1},{2,18},{18,2},{3,19},{19,3},{4,20},{20... | collective-permute-start | bytes 147464 | tf_op jit(solution)/shard_map/ppermute | solution.py:402
  3.7 11.7 %copy-start = (bf16[2,768,384]{2,1,0:T(8,128)(2,1)S(1)}, bf16[2,768,384]{2,1,0:T(8,128)(2,1)}, u32[]{:S(2)}) copy-start(bf16[2,768,384]{2,1,0:T(8,128)(2,1)} %constant.2.clone.t_ref) | copy-start | bytes 3538948
  3.7 11.7 %copy-start.2 = (f32[32,384]{1,0:T(8,128)S(1)}, f32[32,384]{1,0:T(8,128)}, u32[]{:S(2)}) copy-start(f32[32,384]{1,0:T(8,128)} %mine_ref.1) | copy-start | bytes 147460
  3.7 11.7 %copy-start.3 = (f32[32]{0:T(128)S(1)}, f32[32]{0:T(128)}, u32[]{:S(2)}) copy-start(f32[32]{0:T(128)} %param.6) | copy-start | bytes 388
  3.7 11.7 %collective-permute-start.1 = (f32[1,32]{1,0:T(1,128)}, f32[1,32]{1,0:T(1,128)S(1)}, u32[]{:S(2)}, u32[]{:S(2)}) collective-permute-start(f32[1,32]{1,0:T(1,128)} %bitcast.19), channel_id=1, source_target_pairs={{0,16},{16,0},{1,17},{17,1},{2,18},{18,2},{3,19},{19,3},{4,20},{20... | collective-permute-start | bytes 392 | tf_op jit(solution)/shard_map/ppermute | solution.py:402
  21.7 1.5 collective-permute-start.2
  21.8 15.7 %copy-start.1 = (f32[256,384]{1,0:T(8,128)S(1)}, f32[256,384]{1,0:T(8,128)}, u32[]{:S(2)}) copy-start(f32[256,384]{1,0:T(8,128)} %obs_ref.5) | copy-start | bytes 1179652
  48.2 2.5 %collective-permute-start.3 = (f32[8,16,384]{2,1,0:T(8,128)S(1)}, f32[8,16,384]{2,1,0:T(8,128)S(1)}, u32[]{:S(2)}, u32[]{:S(2)}) collective-permute-start(f32[8,16,384]{2,1,0:T(8,128)S(1)} %all_to_all.64.m_ref), channel_id=1, source_target_pairs={{0,1},{1,0},{2,3},{3,2},{4,5},{5,4},{6,7},{7,6},{8,9},{9,8},{10,11... | collective-permute-start | bytes 589832 | tf_op jit(solution)/shard_map/ppermute | solution.py:402
  53.8 5.3 %collective-permute-start.4 = (f32[64,384]{1,0:T(8,128)S(1)}, f32[64,384]{1,0:T(8,128)S(1)}, u32[]{:S(2)}, u32[]{:S(2)}) collective-permute-start(f32[64,384]{1,0:T(8,128)S(1)} %adjoint_other.3.a_ref), channel_id=1, source_target_pairs={{0,16},{16,0},{1,17},{17,1},{2,18},{18,2},{3,19},{19,3},{4,20},{20... | collective-permute-start | bytes 294920 | tf_op jit(solution)/shard_map/ppermute | solution.py:402
  74.3 1.5 collective-permute-start.5
  97.5 2.5 %collective-permute-start.6 = (f32[8,16,384]{2,1,0:T(8,128)S(1)}, f32[8,16,384]{2,1,0:T(8,128)S(1)}, u32[]{:S(2)}, u32[]{:S(2)}) collective-permute-start(f32[8,16,384]{2,1,0:T(8,128)S(1)} %all_to_all.67.m_ref), channel_id=1, source_target_pairs={{0,1},{1,0},{2,3},{3,2},{4,5},{5,4},{6,7},{7,6},{8,9},{9,8},{10,11... | collective-permute-start | bytes 589832 | tf_op jit(solution)/shard_map/ppermute | solution.py:402
  103.1 5.3 %collective-permute-start.7 = (f32[64,384]{1,0:T(8,128)S(1)}, f32[64,384]{1,0:T(8,128)S(1)}, u32[]{:S(2)}, u32[]{:S(2)}) collective-permute-start(f32[64,384]{1,0:T(8,128)S(1)} %adjoint_other.4.a_ref), channel_id=1, source_target_pairs={{0,16},{16,0},{1,17},{17,1},{2,18},{18,2},{3,19},{19,3},{4,20},{20... | collective-permute-start | bytes 294920 | tf_op jit(solution)/shard_map/ppermute | solution.py:402
  123.6 1.5 collective-permute-start.8
  147.4 2.5 %collective-permute-start.9 = (f32[8,16,384]{2,1,0:T(8,128)S(1)}, f32[8,16,384]{2,1,0:T(8,128)S(1)}, u32[]{:S(2)}, u32[]{:S(2)}) collective-permute-start(f32[8,16,384]{2,1,0:T(8,128)S(1)} %all_to_all.70.m_ref), channel_id=1, source_target_pairs={{0,1},{1,0},{2,3},{3,2},{4,5},{5,4},{6,7},{7,6},{8,9},{9,8},{10,11... | collective-permute-start | bytes 589832 | tf_op jit(solution)/shard_map/ppermute | solution.py:402
  153.0 5.3 %collective-permute-start.10 = (f32[64,384]{1,0:T(8,128)S(1)}, f32[64,384]{1,0:T(8,128)S(1)}, u32[]{:S(2)}, u32[]{:S(2)}) collective-permute-start(f32[64,384]{1,0:T(8,128)S(1)} %adjoint_other.5.a_ref), channel_id=1, source_target_pairs={{0,16},{16,0},{1,17},{17,1},{2,18},{18,2},{3,19},{19,3},{4,20},{20... | collective-permute-start | bytes 294920 | tf_op jit(solution)/shard_map/ppermute | solution.py:402
